TPU v7x, 512 devices: a whole 4x8x8 slice. The times are simulated.
512 devices in a mesh: blk: 128 (over y, z, x_hi), col: 4 (over x_lo, core).
Axes of the slice: x: 4 (x_hi: 2, x_lo: 2; x = x_hi * 2 + x_lo), y: 8, z: 8, core: 2. Of those that a mesh axis runs over, the one named last changes fastest.
Arguments:
- start_panel: float32 [128, 262144], P('col', 'blk'), may hold values from -6 to 6
- tile_values: float32 [3072, 128, 128], P('blk'), may hold values from -0.3125 to 0.3125
- tile_rows: int32 [3072], P('blk'), may hold values from 0 to 2047, as said below
- tile_cols: int32 [3072], P('blk'), may hold values from 0 to 2047, as said below
- tile_counts: int32 [128], P('blk'), may hold values from 5 to 24, as said below
Outputs:
- ortho_panel: float32 [128, 262144], P('col', 'blk')
- gram_factor: float32 [128, 128], replicated
Inputs may be any that keep to these rules, and one draw needn't show every extreme that they name: `tile_rows`: slot s has a row block among those of blk index s // 24, that is s // 24 * 16 up to s // 24 * 16 + 15. `tile_cols`: slot s has a column block among those of blk indices s // 24 + o for o from -2 to 2, taken modulo the number of blk indices; slot j of each blk index with j < 5 takes o = j - 2. `tile_counts`: some blk index has all 24 slots live; every blk index has 5 or more.
All inputs are finite; a program needn't handle non-finite values.
Results may differ from a plain program's by a relative error of at most 0.0003.
Values sent between devices are 32-bit elements; how exact they have to be, the bound alone decides.
No kernel may reach another device: no remote copies, remote signals or barrier semaphores. Data moves between devices by JAX's collectives and lax.ppermute only.
A program may use at most 64 MiB of HBM per device.

v0:
```python
import jax
import jax.numpy as jnp
from jax import lax
from jax.sharding import PartitionSpec as P

BS = 128
K = 128
RB_DEV = 16
TILE_CAP = 24
REACH = 2
DEGREE = 4


def shifted(value, axis, steps):
    count = lax.axis_size(axis)
    pairs = [(source, (source + steps) % count) for source in range(count)]
    return lax.ppermute(value, axis, pairs)


def band_window(panel):
    lower = []
    current = panel
    for offset in range(REACH):
        current = shifted(current, "blk", 1)
        lower.append(current)
    higher = []
    current = panel
    for offset in range(REACH):
        current = shifted(current, "blk", -1)
        higher.append(current)
    pieces = lower[::-1] + [panel] + higher
    return jnp.concatenate(pieces, axis=1)


def apply_graph(panel, tile_values, local_cols, row_table, live):
    window = band_window(panel)
    width = panel.shape[0]
    blocks = window.reshape(width, (2 * REACH + 1) * RB_DEV, BS)
    piece = blocks[:, local_cols, :]
    contrib = jnp.einsum("ktb,tab->kta", piece, tile_values, precision=lax.Precision.HIGHEST)
    contrib = jnp.where(live[None, :, None], contrib, jnp.zeros_like(contrib))
    summed = jnp.einsum("kta,tr->kra", contrib, row_table, precision=lax.Precision.HIGHEST)
    return summed.reshape(width, RB_DEV * BS)


def per_device(start_panel, tile_values, tile_rows, tile_cols, tile_counts):
    position = lax.axis_index("blk")
    cycle_count = lax.axis_size("blk")
    local_cols = (
        tile_cols // RB_DEV - position + REACH + cycle_count
    ) % cycle_count * RB_DEV + tile_cols % RB_DEV
    local_rows = tile_rows - position * RB_DEV
    row_table = (local_rows[:, None] == jnp.arange(RB_DEV, dtype=jnp.int32)[None, :]).astype(
        jnp.float32
    )
    live = jnp.arange(TILE_CAP, dtype=jnp.int32) < tile_counts[0]
    previous = start_panel
    current = apply_graph(start_panel, tile_values, local_cols, row_table, live)
    for step in range(DEGREE - 1):
        upcoming = 2.0 * apply_graph(current, tile_values, local_cols, row_table, live) - previous
        previous, current = (current, upcoming)
    all_columns = lax.all_gather(current, "col", axis=0, tiled=True)
    partial_gram = jnp.dot(all_columns, all_columns.T, precision=lax.Precision.HIGHEST)
    gram = lax.psum(partial_gram, "blk")
    factor = jnp.linalg.cholesky(gram)
    total_rows = current.shape[1] * cycle_count
    scale = jnp.sqrt(jnp.asarray(total_rows, jnp.float32))
    inverse = lax.linalg.triangular_solve(
        factor, jnp.eye(K, dtype=jnp.float32), left_side=True, lower=True
    )
    width = current.shape[0]
    inverse_rows = lax.dynamic_slice_in_dim(inverse, lax.axis_index("col") * width, width, 0)
    ortho_panel = jnp.dot(inverse_rows, all_columns, precision=lax.Precision.HIGHEST) * scale
    return (ortho_panel, factor / scale)


def solution(mesh):
    in_specs = (P("col", "blk"), P("blk", None, None), P("blk"), P("blk"), P("blk"))
    out_specs = (P("col", "blk"), P())
    return jax.shard_map(
        per_device, mesh=mesh, in_specs=in_specs, out_specs=out_specs, check_vma=False
    )
```

profile of v0, /device:TPU:2, one launch (start us, length us, event | category | flops | bytes accessed | tf_op | source)
XLA Modules:
  0.0 1473.7 jit_solution(17373536719154956770)
XLA Ops:
  7.2 4.2 collective-permute-start
  11.4 13.3 collective-permute-start.2
  26.1 3.2 collective-permute-done
  31.9 9.6 collective-permute-start.3
  41.5 2.9 collective-permute-done.1
  45.5 2.8 collective-permute-done.3
  49.2 2.5 fusion.3
  54.2 9.6 collective-permute-start.6
  63.9 2.8 collective-permute-done.4
  66.6 3.5 collective-permute-start.5
  70.3 8.1 collective-permute-start.7
  80.9 4.3 collective-permute-done.7
  86.3 2.5 fusion.2
  91.4 9.6 collective-permute-start.10
  101.0 4.0 collective-permute-done.8
  105.0 3.5 collective-permute-start.9
  108.5 8.1 collective-permute-start.11
  116.6 3.0 collective-permute-done.9
  119.7 4.8 collective-permute-done.11
  126.0 3.5 fusion.1
  132.1 9.6 collective-permute-start.14
  141.8 3.8 collective-permute-done.12
  145.6 3.5 collective-permute-start.13
  149.1 8.2 collective-permute-start.15
  157.3 2.6 collective-permute-done.13
  160.0 4.8 collective-permute-done.15
  166.4 3.5 fusion
  171.3 18.4 %all-gather.2.cloned.1.call-done = f32[128,2048]{1,0:T(8,128)} async-done(((f32[32,2048]{1,0:T(8,128)}), f32[128,2048]{1,0:T(8,128)}) %all-gather.2.cloned.1.call-update) | async-done | bytes 1048592 | tf_op jit(solution)/shard_map/all_gather | solution.py:62
  189.7 3.3 fusion.31
  193.1 1246.8 %all-reduce.2.cloned.1.call-done = f32[128,128]{0,1:T(8,128)} async-done(((f32[128,128]{0,1:T(8,128)}), f32[128,128]{0,1:T(8,128)}) %all-reduce.2.cloned.1.call-update) | async-done | bytes 65552 | tf_op jit(solution)/shard_map/psum | solution.py:64
  1441.7 11.7 cholesky.17
  1455.4 9.8 custom-call.6
  (70 shorter events, 26.4 us)
Async XLA Ops:
  7.2 42.0 %copy-start = (f32[24,128,128]{2,1,0:T(8,128)S(1)}, f32[24,128,128]{2,1,0:T(8,128)}, u32[]{:S(2)}) copy-start(f32[24,128,128]{2,1,0:T(8,128)} %param.6) | copy-start | bytes 4718596
  7.2 182.5 %all-gather.2.cloned.1.call-start = ((), (), s32[]{:S(2)}) async-start(), calls=%async_computation | async-start | bytes 1310720 | tf_op jit(solution)/shard_map/all_gather | solution.py:62
  7.2 22.1 %collective-permute-start = (f32[32,2048]{1,0:T(8,128)}, f32[32,2048]{1,0:T(8,128)S(1)}, u32[]{:S(2)}, u32[]{:S(2)}) collective-permute-start(f32[32,2048]{1,0:T(8,128)} %param.5), channel_id=1, source_target_pairs={{0,4},{4,8},{8,12},{12,16},{16,20},{20,24},{24,28},{28,32},{32,36}... | collective-permute-start | bytes 786440 | tf_op jit(solution)/shard_map/ppermute | solution.py:17
  11.4 20.5 %collective-permute-start.2 = (f32[32,2048]{1,0:T(8,128)}, f32[32,2048]{1,0:T(8,128)S(1)}, u32[]{:S(2)}, u32[]{:S(2)}) collective-permute-start(f32[32,2048]{1,0:T(8,128)} %param.5), channel_id=1, source_target_pairs={{0,508},{4,0},{8,4},{12,8},{16,12},{20,16},{24,20},{28,24},{32,28}... | collective-permute-start | bytes 786440 | tf_op jit(solution)/shard_map/ppermute | solution.py:17
  29.3 15.2 %collective-permute-start.1 = (f32[32,2048]{1,0:T(8,128)S(1)}, f32[32,2048]{1,0:T(8,128)S(1)}, u32[]{:S(2)}, u32[]{:S(2)}) collective-permute-start(f32[32,2048]{1,0:T(8,128)S(1)} %collective-permute-done), channel_id=1, source_target_pairs={{0,4},{4,8},{8,12},{12,16},{16,20},{20,24},{24,28},{28,32},{32,36}... | collective-permute-start | bytes 786440 | tf_op jit(solution)/shard_map/ppermute | solution.py:17
  31.9 16.5 %collective-permute-start.3 = (f32[32,2048]{1,0:T(8,128)S(1)}, f32[32,2048]{1,0:T(8,128)S(1)}, u32[]{:S(2)}, u32[]{:S(2)}) collective-permute-start(f32[32,2048]{1,0:T(8,128)S(1)} %collective-permute-done.2), channel_id=1, source_target_pairs={{0,508},{4,0},{8,4},{12,8},{16,12},{20,16},{24,20},{28,24},{32,28}... | collective-permute-start | bytes 786440 | tf_op jit(solution)/shard_map/ppermute | solution.py:17
  52.3 14.3 collective-permute-start.4
  54.2 16.0 %collective-permute-start.6 = (f32[32,2048]{1,0:T(8,128)S(1)}, f32[32,2048]{1,0:T(8,128)S(1)}, u32[]{:S(2)}, u32[]{:S(2)}) collective-permute-start(f32[32,2048]{1,0:T(8,128)S(1)} %bitcast.100), channel_id=1, source_target_pairs={{0,508},{4,0},{8,4},{12,8},{16,12},{20,16},{24,20},{28,24},{32,28}... | collective-permute-start | bytes 786440 | tf_op jit(solution)/shard_map/ppermute | solution.py:17
  66.6 14.1 collective-permute-start.5
  70.3 14.9 %collective-permute-start.7 = (f32[32,2048]{1,0:T(8,128)S(1)}, f32[32,2048]{1,0:T(8,128)S(1)}, u32[]{:S(2)}, u32[]{:S(2)}) collective-permute-start(f32[32,2048]{1,0:T(8,128)S(1)} %collective-permute-done.6), channel_id=1, source_target_pairs={{0,508},{4,0},{8,4},{12,8},{16,12},{20,16},{24,20},{28,24},{32,28}... | collective-permute-start | bytes 786440 | tf_op jit(solution)/shard_map/ppermute | solution.py:17
  86.3 3.1 copy-start.2
  89.5 15.5 %collective-permute-start.8 = (f32[32,2048]{1,0:T(8,128)S(1)}, f32[32,2048]{1,0:T(8,128)S(1)}, u32[]{:S(2)}, u32[]{:S(2)}) collective-permute-start(f32[32,2048]{1,0:T(8,128)S(1)} %bitcast_subtract_fusion.2), channel_id=1, source_target_pairs={{0,4},{4,8},{8,12},{12,16},{16,20},{20,24},{24,28},{28,32},{32,36}... | collective-permute-start | bytes 786440 | tf_op jit(solution)/shard_map/ppermute | solution.py:17
  91.4 17.1 %collective-permute-start.10 = (f32[32,2048]{1,0:T(8,128)S(1)}, f32[32,2048]{1,0:T(8,128)S(1)}, u32[]{:S(2)}, u32[]{:S(2)}) collective-permute-start(f32[32,2048]{1,0:T(8,128)S(1)} %bitcast_subtract_fusion.2), channel_id=1, source_target_pairs={{0,508},{4,0},{8,4},{12,8},{16,12},{20,16},{24,20},{28,24},{32,28}... | collective-permute-start | bytes 786440 | tf_op jit(solution)/shard_map/ppermute | solution.py:17
  105.0 14.6 collective-permute-start.9
  108.5 16.0 %collective-permute-start.11 = (f32[32,2048]{1,0:T(8,128)S(1)}, f32[32,2048]{1,0:T(8,128)S(1)}, u32[]{:S(2)}, u32[]{:S(2)}) collective-permute-start(f32[32,2048]{1,0:T(8,128)S(1)} %collective-permute-done.10), channel_id=1, source_target_pairs={{0,508},{4,0},{8,4},{12,8},{16,12},{20,16},{24,20},{28,24},{32,28}... | collective-permute-start | bytes 786440 | tf_op jit(solution)/shard_map/ppermute | solution.py:17
  130.2 15.3 %collective-permute-start.12 = (f32[32,2048]{1,0:T(8,128)S(1)}, f32[32,2048]{1,0:T(8,128)S(1)}, u32[]{:S(2)}, u32[]{:S(2)}) collective-permute-start(f32[32,2048]{1,0:T(8,128)S(1)} %bitcast_subtract_fusion.1), channel_id=1, source_target_pairs={{0,4},{4,8},{8,12},{12,16},{16,20},{20,24},{24,28},{28,32},{32,36}... | collective-permute-start | bytes 786440 | tf_op jit(solution)/shard_map/ppermute | solution.py:17
  132.1 16.9 %collective-permute-start.14 = (f32[32,2048]{1,0:T(8,128)S(1)}, f32[32,2048]{1,0:T(8,128)S(1)}, u32[]{:S(2)}, u32[]{:S(2)}) collective-permute-start(f32[32,2048]{1,0:T(8,128)S(1)} %bitcast_subtract_fusion.1), channel_id=1, source_target_pairs={{0,508},{4,0},{8,4},{12,8},{16,12},{20,16},{24,20},{28,24},{32,28}... | collective-permute-start | bytes 786440 | tf_op jit(solution)/shard_map/ppermute | solution.py:17
  145.6 14.4 collective-permute-start.13
  149.1 15.8 %collective-permute-start.15 = (f32[32,2048]{1,0:T(8,128)S(1)}, f32[32,2048]{1,0:T(8,128)S(1)}, u32[]{:S(2)}, u32[]{:S(2)}) collective-permute-start(f32[32,2048]{1,0:T(8,128)S(1)} %collective-permute-done.14), channel_id=1, source_target_pairs={{0,508},{4,0},{8,4},{12,8},{16,12},{20,16},{24,20},{28,24},{32,28}... | collective-permute-start | bytes 786440 | tf_op jit(solution)/shard_map/ppermute | solution.py:17
  171.3 1268.6 %all-reduce.2.cloned.1.call-start = ((), (), s32[]{:S(2)}) async-start(), calls=%async_computation.1 | async-start | bytes 131072 | tf_op jit(solution)/shard_map/psum | solution.py:64
  189.7 1275.7 %copy-start.1 = (f32[128,2048]{1,0:T(8,128)S(1)}, f32[128,2048]{1,0:T(8,128)}, u32[]{:S(2)}) copy-start(f32[128,2048]{1,0:T(8,128)} %all-gather.2.cloned.1.call-done) | copy-start | bytes 3145732
Sparse Core Ops, SparseCore 0:
  171.4 18.2 all-gather.1
  193.2 1246.6 all-reduce.1
where the time goes:
time: 1470 us
  waiting for transfers between devices  1310 us (89%)
  starting transfers between devices  98.6 us (7%)
  other arithmetic  26.8 us (2%)
  matrix products  19.1 us (1%)
  between operations  15.2 us (1%)
    psum x1, waiting for transfers between devices, per_device(): gram = lax.psum(partial_gram, 'blk')  1250 us
    ppermute x16, starting transfers between devices, shifted(): return lax.ppermute(value, axis, pairs)  98.6 us
    ppermute x16, waiting for transfers between devices, shifted(): return lax.ppermute(value, axis, pairs)  41.4 us
  transfers between devices with their start and end apart: 18, of which 14 were waited for; matrix products, arithmetic and copies ran while one was open for 0% of the time, Pallas kernels for 0%

commit v1 on v0

v1 whole, which is shorter than its diff:
```python
import functools

import jax
import jax.numpy as jnp
from jax import lax
from jax.experimental import pallas as pl
from jax.experimental.pallas import tpu as pltpu
from jax.sharding import Mesh
from jax.sharding import PartitionSpec as P

BS = 128
K = 128
RB_DEV = 16
TILE_CAP = 24
DEGREE = 4
COLS = 16
HALF = 2 * RB_DEV
UNROLL = 4
GROUP = ("xh", "xl", "core")
COL = ("xl", "core")
VMEM = pl.BlockSpec(memory_space=pltpu.VMEM)
SMEM = pl.BlockSpec(memory_space=pltpu.SMEM)
INTERPRET = False


def split_bf16(value):
    high = value.astype(jnp.bfloat16)
    low = (value - high.astype(jnp.float32)).astype(jnp.bfloat16)
    return high, low


def call(kernel, out_shape, operands, specs, scratch=(), flops=0, moved=0):
    outs = jax.tree.map(lambda s: VMEM, out_shape)
    return pl.pallas_call(
        kernel,
        out_shape=out_shape,
        in_specs=specs,
        out_specs=outs,
        scratch_shapes=list(scratch),
        compiler_params=pltpu.CompilerParams(vmem_limit_bytes=24 << 20),
        cost_estimate=pl.CostEstimate(flops=flops, bytes_accessed=moved, transcendentals=0),
        interpret=INTERPRET,
    )(*operands)


def split_kernel(*refs):
    *pieces, out_ref = refs
    base = 0
    for piece in pieces:
        def body(slot, carry, piece=piece, base=base):
            high, low = split_bf16(piece[slot])
            out_ref[base + slot, 0] = high
            out_ref[base + slot, 1] = low
            return carry

        lax.fori_loop(0, piece.shape[0], body, 0, unroll=2)
        base += piece.shape[0]


def split_tiles(pieces):
    count = sum(piece.shape[0] for piece in pieces)
    return call(
        split_kernel,
        jax.ShapeDtypeStruct((count, 2, BS, BS), jnp.bfloat16),
        pieces,
        [VMEM] * len(pieces),
        moved=count * BS * BS * 8,
    )


def dot_t(left, right, precision=None):
    return lax.dot_general(
        left,
        right,
        (((1,), (1,)), ((), ())),
        preferred_element_type=jnp.float32,
        precision=precision,
    )


def step_kernel(first, last, *refs):
    if first:
        table, low_ref, mid_ref, high_ref, own_ref, other_ref, out_ref, window, total = refs
        prev_ref = None
    else:
        table, low_ref, mid_ref, high_ref, prev_ref, own_ref, other_ref, out_ref, window, total = refs
    for piece, ref in enumerate((low_ref, mid_ref, high_ref)):
        def fill(block, carry, piece=piece, ref=ref):
            high, low = split_bf16(ref[block])
            window[piece * HALF + block, 0:COLS] = high
            window[piece * HALF + block, COLS : 2 * COLS] = low
            return carry

        lax.fori_loop(0, HALF, fill, 0, unroll=8)
    total[...] = jnp.zeros_like(total)
    for which, tiles in enumerate((own_ref, other_ref)):
        base = which * 3 * TILE_CAP
        live = table[6 * TILE_CAP + which]

        def body(group, carry, base=base, tiles=tiles, live=live):
            terms = []
            for inner in range(UNROLL):
                slot = group * UNROLL + inner
                column = table[base + TILE_CAP + slot]
                place = table[base + 2 * TILE_CAP + slot]
                both = window[column]
                wide = dot_t(both, tiles[place, 0])
                narrow = dot_t(both[:COLS], tiles[place, 1])
                term = wide[:COLS] + (wide[COLS:] + narrow)
                terms.append(jnp.where(slot < live, term, jnp.zeros_like(term)))
            for inner in range(UNROLL):
                row = table[base + group * UNROLL + inner]
                total[row] = total[row] + terms[inner]
            return carry

        lax.fori_loop(0, (live + UNROLL - 1) // UNROLL, body, 0)
    swap = table[6 * TILE_CAP + 2] if last else 0

    def finish(block, carry):
        source = block ^ swap if last else block
        value = total[source]
        if prev_ref is not None:
            value = 2.0 * value - prev_ref[source]
        out_ref[block] = value
        return carry

    lax.fori_loop(0, HALF, finish, 0, unroll=8)


def graph_step(table, parts, prev, own_tiles, other_tiles, last):
    first = prev is None
    operands = [table, *parts] + ([] if first else [prev]) + [own_tiles, other_tiles]
    return call(
        functools.partial(step_kernel, first, last),
        jax.ShapeDtypeStruct((HALF, COLS, BS), jnp.float32),
        operands,
        [SMEM] + [VMEM] * (len(operands) - 1),
        scratch=[
            pltpu.VMEM((3 * HALF, 2 * COLS, BS), jnp.bfloat16),
            pltpu.VMEM((HALF, COLS, BS), jnp.float32),
        ],
        flops=2 * TILE_CAP * 6 * COLS * BS * BS,
        moved=8 << 20,
    )


def gram_kernel(parts_ref, all_ref, gram_ref):
    for half in range(2):
        for c in range(4):
            for block in range(4):
                row = (2 * c + half) * COLS
                all_ref[row : row + COLS, block * BS : (block + 1) * BS] = parts_ref[
                    half * 4 + c, block
                ]
    value = all_ref[...]
    gram_ref[...] = dot_t(value, value, precision=lax.Precision.HIGHEST)


def apply_kernel(inverse_ref, all_ref, out_ref):
    out_ref[...] = lax.dot_general(
        inverse_ref[...],
        all_ref[...],
        (((1,), (0,)), ((), ())),
        preferred_element_type=jnp.float32,
        precision=lax.Precision.HIGHEST,
    )


def exchange(value, axis):
    return lax.ppermute(value, axis, [(0, 1), (1, 0)])


def to_all(value, axis):
    return lax.all_to_all(value, axis, 0, 0, tiled=True)


def filtered_basis(start_panel, tile_values, tile_rows, tile_cols, tile_counts):
    q = lax.axis_index("q")
    count_q = lax.axis_size("q")
    xh = lax.axis_index("xh")
    c = lax.axis_index("xl") * 2 + lax.axis_index("core")
    quarter = TILE_CAP // 4

    halves = start_panel.reshape(2, COLS, RB_DEV, BS)
    mine = lax.dynamic_index_in_dim(halves, xh, 0, keepdims=False).transpose(1, 0, 2)
    given = lax.dynamic_index_in_dim(halves, 1 - xh, 0, keepdims=False).transpose(1, 0, 2)
    notes = jnp.concatenate(
        [
            tile_rows.astype(jnp.float32)[None],
            tile_cols.astype(jnp.float32)[None],
            jnp.broadcast_to(tile_counts.astype(jnp.float32)[None], (1, TILE_CAP)),
        ],
        axis=0,
    )
    notes = jnp.pad(notes, ((0, COLS - 3), (0, BS - TILE_CAP)))
    got = exchange(jnp.concatenate([given, notes[None]], axis=0), "xh")
    panel = jnp.concatenate([mine, got[:RB_DEV]], axis=0)
    other = jnp.round(got[RB_DEV, :3, :TILE_CAP]).astype(jnp.int32)

    piece = lax.dynamic_slice_in_dim(tile_values, c * quarter, quarter, 0)
    first = lax.ppermute(piece, ("xh", "xl"), [(i, 3 - i) for i in range(4)])
    second = exchange(first, "xl")
    pair = jnp.concatenate([first, second], axis=0)
    far = exchange(pair, "core")
    own_tiles = split_tiles([tile_values])
    other_tiles = split_tiles([pair, far])

    slots = jnp.arange(TILE_CAP, dtype=jnp.int32)

    def window_place(cols):
        owner = cols // RB_DEV
        step = (owner // 2 - q + 1 + count_q) % count_q
        place = step * HALF + ((owner % 2) ^ xh) * RB_DEV + cols % RB_DEV
        return jnp.clip(place, 0, 3 * HALF - 1)

    def row_place(rows, base):
        return jnp.clip(rows % RB_DEV, 0, RB_DEV - 1) + base

    order = (slots // quarter) ^ c
    order = (order % 2) * 2 + 1 - order // 2
    table = jnp.concatenate(
        [
            row_place(tile_rows, 0),
            window_place(tile_cols),
            slots,
            row_place(other[0], RB_DEV),
            window_place(other[1]),
            order * quarter + slots % quarter,
            tile_counts,
            other[2, :1],
            (xh * RB_DEV)[None],
        ]
    )

    up = [(i, (i + 1) % count_q) for i in range(count_q)]
    down = [(i, (i - 1) % count_q) for i in range(count_q)]
    previous, current = None, panel
    for step in range(DEGREE):
        lower = lax.ppermute(current, "q", up)
        higher = lax.ppermute(current, "q", down)
        upcoming = graph_step(
            table, (lower, current, higher), previous, own_tiles, other_tiles, step == DEGREE - 1
        )
        previous, current = current, upcoming

    parts = to_all(current.reshape(8, 4, COLS, BS), GROUP)
    everything, gram = call(
        gram_kernel,
        (
            jax.ShapeDtypeStruct((K, 4 * BS), jnp.float32),
            jax.ShapeDtypeStruct((K, K), jnp.float32),
        ),
        [parts],
        [VMEM],
        flops=2 * K * K * 4 * BS * 6,
        moved=1 << 20,
    )
    rows = K // count_q if K >= count_q else 1
    spread = to_all(gram, "q").reshape(count_q, rows, K).sum(axis=0)
    spread = to_all(jnp.broadcast_to(spread[None], (8, rows, K)), GROUP).sum(axis=0)
    gram = to_all(jnp.broadcast_to(spread[None], (count_q, rows, K)), "q").reshape(K, K)

    factor = jnp.linalg.cholesky(gram)
    total_rows = start_panel.shape[1] * count_q * 2
    scale = jnp.sqrt(jnp.asarray(total_rows, jnp.float32))
    inverse = lax.linalg.triangular_solve(
        factor, jnp.eye(K, dtype=jnp.float32), left_side=True, lower=True
    )
    ortho = call(
        apply_kernel,
        jax.ShapeDtypeStruct((K, 4 * BS), jnp.float32),
        [inverse * scale, everything],
        [VMEM, VMEM],
        flops=2 * K * K * 4 * BS * 6,
        moved=1 << 20,
    )
    ortho = to_all(ortho.reshape(4, K // 4, 4 * BS), COL)
    ortho_panel = ortho.transpose(1, 0, 2).reshape(K // 4, 16 * BS)
    return (ortho_panel, factor / scale)


def solution(mesh):
    grid = Mesh(
        mesh.devices.reshape(mesh.devices.shape[0] // 2, 2, 2, 2), ("q", "xh", "xl", "core")
    )
    blk = ("q", "xh")
    in_specs = (P(COL, blk), P(blk, None, None), P(blk), P(blk), P(blk))
    out_specs = (P(COL, blk), P())
    return jax.shard_map(
        filtered_basis, mesh=grid, in_specs=in_specs, out_specs=out_specs, check_vma=False
    )
```

time: 1470 us -> 204 us (0.14)
  the two profiles are of different devices: /device:TPU:2 before, /device:TPU:1 now
where the time goes in v1:
time: 204 us; the launch traced here: 203 us
  blocking collectives  66.8 us (33%)
  starting transfers between devices  53.6 us (26%)
  waiting for transfers between devices  40.1 us (20%)
  other arithmetic  24.3 us (12%)
  Pallas kernels  9.59 us (5%)
  local copies, waits for them, and re-layouts  6.79 us (3%)
    all_to_all x5, blocking collectives, to_all(): return lax.all_to_all(value, axis, 0, 0, tiled=True)  66.8 us
    ppermute x4, waiting for transfers between devices, filtered_basis(): lower = lax.ppermute(current, 'q', up)  22.1 us
    ppermute x4, starting transfers between devices, filtered_basis(): higher = lax.ppermute(current, 'q', down)  19.3 us
    ppermute x3, starting transfers between devices, exchange(): return lax.ppermute(value, axis, [(0, 1), (1, 0)])  17.1 us
    another operation x3, other arithmetic, filtered_basis(): factor = jnp.linalg.cholesky(gram)  12.4 us
    ppermute x4, starting transfers between devices, filtered_basis(): lower = lax.ppermute(current, 'q', up)  11.9 us
    another operation x1, other arithmetic, filtered_basis(): lax.linalg.triangular_solve(factor, jnp.eye(K, dtype=jnp.float32), left_s...  9.81 us
    pallas_call x8, Pallas kernels, call(): pl.pallas_call(kernel, out_shape=out_shape, in_specs=specs, out_specs=out...  9.59 us
  transfers between devices with their start and end apart: 12, of which 10 were waited for; matrix products, arithmetic and copies ran while one was open for 2% of the time, Pallas kernels for 1%

profile of v1, /device:TPU:1, one launch (start us, length us, event | category | flops | bytes accessed | tf_op | source)
XLA Modules:
  0.0 203.0 jit_solution(13260057882107887152)
XLA Ops:
  1.7 5.2 %collective-permute-start.3 = (f32[6,128,128]{2,1,0:T(8,128)S(1)}, f32[6,128,128]{2,1,0:T(8,128)S(1)}, u32[]{:S(2)}, u32[]{:S(2)}) collective-permute-start(f32[6,128,128]{2,1,0:T(8,128)S(1)} %constant_dynamic-slice_fusion), channel_id=1, source_target_pairs={{0,6},{2,4},{4,2},{6,0},{1,7},{3,5},{5,3},{7,1},{8,14},{10,12},{12... | collective-permute-start | bytes 1179656 | tf_op jit(solution)/shard_map/ppermute | solution.py:201
  9.4 2.7 %collective-permute-done.3 = f32[6,128,128]{2,1,0:T(8,128)S(1)} collective-permute-done((f32[6,128,128]{2,1,0:T(8,128)S(1)}, f32[6,128,128]{2,1,0:T(8,128)S(1)}, u32[]{:S(2)}, u32[]{:S(2)}) %collective-permute-start.3) | collective-permute-done | bytes 393248 | tf_op jit(solution)/shard_map/ppermute | solution.py:201
  12.1 5.4 %collective-permute-start.4 = (f32[6,128,128]{2,1,0:T(8,128)S(1)}, f32[6,128,128]{2,1,0:T(8,128)S(1)}, u32[]{:S(2)}, u32[]{:S(2)}) collective-permute-start(f32[6,128,128]{2,1,0:T(8,128)S(1)} %collective-permute-done.3), channel_id=1, source_target_pairs={{0,2},{2,0},{1,3},{3,1},{4,6},{6,4},{5,7},{7,5},{8,10},{10,8},{9,1... | collective-permute-start | bytes 1179656 | tf_op jit(solution)/shard_map/ppermute | solution.py:170
  18.4 4.3 %collective-permute-done.4 = f32[6,128,128]{2,1,0:T(8,128)S(1)} collective-permute-done((f32[6,128,128]{2,1,0:T(8,128)S(1)}, f32[6,128,128]{2,1,0:T(8,128)S(1)}, u32[]{:S(2)}, u32[]{:S(2)}) %collective-permute-start.4) | collective-permute-done | bytes 393248 | tf_op jit(solution)/shard_map/ppermute | solution.py:170
  23.5 8.3 %collective-permute-start.5 = (f32[12,128,128]{2,1,0:T(8,128)}, f32[12,128,128]{2,1,0:T(8,128)}, u32[]{:S(2)}, u32[]{:S(2)}) collective-permute-start(f32[12,128,128]{2,1,0:T(8,128)} %constant_dynamic-update-slice_fusion.refs_0_), channel_id=1, source_target_pairs={{0,1},{1,0},{2,3},{3,2},{4,5},{5,4},{6,7},{7,6},{8,9},{9,8},{10,11... | collective-permute-start | bytes 2359304 | tf_op jit(solution)/shard_map/ppermute | solution.py:170
  31.8 3.4 %collective-permute-start = (f32[17,16,128]{2,1,0:T(8,128)S(1)}, f32[17,16,128]{2,1,0:T(8,128)S(1)}, u32[]{:S(2)}, u32[]{:S(2)}) collective-permute-start(f32[17,16,128]{2,1,0:T(8,128)S(1)} %pad_maximum_fusion.1), channel_id=1, source_target_pairs={{0,4},{4,0},{1,5},{5,1},{2,6},{6,2},{3,7},{7,3},{8,12},{12,8},{9,1... | collective-permute-start | bytes 417800 | tf_op jit(solution)/shard_map/ppermute | solution.py:170
  35.5 4.9 %collective-permute-done = f32[17,16,128]{2,1,0:T(8,128)S(1)} collective-permute-done((f32[17,16,128]{2,1,0:T(8,128)S(1)}, f32[17,16,128]{2,1,0:T(8,128)S(1)}, u32[]{:S(2)}, u32[]{:S(2)}) %collective-permute-start) | collective-permute-done | bytes 139296 | tf_op jit(solution)/shard_map/ppermute | solution.py:170
  40.4 13.5 %collective-permute-start.2 = (f32[32,16,128]{2,1,0:T(8,128)S(1)}, f32[32,16,128]{2,1,0:T(8,128)S(1)}, u32[]{:S(2)}, u32[]{:S(2)}) collective-permute-start(f32[32,16,128]{2,1,0:T(8,128)S(1)} %pad_maximum_fusion.refs_2_.refs_4_), channel_id=1, source_target_pairs={{0,504},{8,0},{16,8},{24,16},{32,24},{40,32},{48,40},{56,48},{64,5... | collective-permute-start | bytes 786440 | tf_op jit(solution)/shard_map/ppermute | solution.py:240
  54.0 1.9 collective-permute-start.1
  59.6 6.3 %collective-permute-done.1.refs_1_ = f32[32,16,128]{2,1,0:T(8,128)S(1)} collective-permute-done((f32[32,16,128]{2,1,0:T(8,128)S(1)}, f32[32,16,128]{2,1,0:T(8,128)S(1)}, u32[]{:S(2)}, u32[]{:S(2)}) %collective-permute-start.1) | collective-permute-done | bytes 262176 | tf_op jit(solution)/shard_map/ppermute | solution.py:239
  67.7 1.9 collective-permute-start.7
  69.6 3.4 %collective-permute-start.6 = (f32[32,16,128]{2,1,0:T(8,128)S(1)}, f32[32,16,128]{2,1,0:T(8,128)S(1)}, u32[]{:S(2)}, u32[]{:S(2)}) collective-permute-start(f32[32,16,128]{2,1,0:T(8,128)S(1)} %shard_map.70.refs_2_.refs_4_), channel_id=1, source_target_pairs={{0,8},{8,16},{16,24},{24,32},{32,40},{40,48},{48,56},{56,64},{64,7... | collective-permute-start | bytes 786440 | tf_op jit(solution)/shard_map/ppermute | solution.py:239
  72.9 2.5 %collective-permute-done.7.refs_3_ = f32[32,16,128]{2,1,0:T(8,128)S(1)} collective-permute-done((f32[32,16,128]{2,1,0:T(8,128)S(1)}, f32[32,16,128]{2,1,0:T(8,128)S(1)}, u32[]{:S(2)}, u32[]{:S(2)}) %collective-permute-start.7) | collective-permute-done | bytes 262176 | tf_op jit(solution)/shard_map/ppermute | solution.py:240
  75.4 5.2 %collective-permute-done.6.refs_1_ = f32[32,16,128]{2,1,0:T(8,128)S(1)} collective-permute-done((f32[32,16,128]{2,1,0:T(8,128)S(1)}, f32[32,16,128]{2,1,0:T(8,128)S(1)}, u32[]{:S(2)}, u32[]{:S(2)}) %collective-permute-start.6) | collective-permute-done | bytes 262176 | tf_op jit(solution)/shard_map/ppermute | solution.py:239
  80.6 1.8 shard_map.71.refs_2_.refs_4_
  82.4 1.9 collective-permute-start.9
  84.3 3.4 %collective-permute-start.8 = (f32[32,16,128]{2,1,0:T(8,128)S(1)}, f32[32,16,128]{2,1,0:T(8,128)S(1)}, u32[]{:S(2)}, u32[]{:S(2)}) collective-permute-start(f32[32,16,128]{2,1,0:T(8,128)S(1)} %shard_map.71.refs_2_.refs_4_), channel_id=1, source_target_pairs={{0,8},{8,16},{16,24},{24,32},{32,40},{40,48},{48,56},{56,64},{64,7... | collective-permute-start | bytes 786440 | tf_op jit(solution)/shard_map/ppermute | solution.py:239
  87.7 1.8 collective-permute-done.9.refs_3_
  89.5 5.2 %collective-permute-done.8.refs_1_ = f32[32,16,128]{2,1,0:T(8,128)S(1)} collective-permute-done((f32[32,16,128]{2,1,0:T(8,128)S(1)}, f32[32,16,128]{2,1,0:T(8,128)S(1)}, u32[]{:S(2)}, u32[]{:S(2)}) %collective-permute-start.8) | collective-permute-done | bytes 262176 | tf_op jit(solution)/shard_map/ppermute | solution.py:239
  94.7 1.8 shard_map.72.refs_2_
  96.5 2.0 collective-permute-start.11
  98.5 3.3 %collective-permute-start.10 = (f32[32,16,128]{2,1,0:T(8,128)S(1)}, f32[32,16,128]{2,1,0:T(8,128)S(1)}, u32[]{:S(2)}, u32[]{:S(2)}) collective-permute-start(f32[32,16,128]{2,1,0:T(8,128)S(1)} %shard_map.72.refs_2_), channel_id=1, source_target_pairs={{0,8},{8,16},{16,24},{24,32},{32,40},{40,48},{48,56},{56,64},{64,7... | collective-permute-start | bytes 786440 | tf_op jit(solution)/shard_map/ppermute | solution.py:239
  101.8 1.8 collective-permute-done.11.refs_3_
  103.6 5.3 %collective-permute-done.10.refs_1_ = f32[32,16,128]{2,1,0:T(8,128)S(1)} collective-permute-done((f32[32,16,128]{2,1,0:T(8,128)S(1)}, f32[32,16,128]{2,1,0:T(8,128)S(1)}, u32[]{:S(2)}, u32[]{:S(2)}) %collective-permute-start.10) | collective-permute-done | bytes 262176 | tf_op jit(solution)/shard_map/ppermute | solution.py:239
  108.9 1.8 shard_map.73
  110.7 15.5 %all_to_all.29.parts_ref = f32[8,4,16,128]{3,2,1,0:T(8,128)S(1)} all-to-all(f32[8,4,16,128]{3,2,1,0:T(8,128)S(1)} %bitcast.57), channel_id=1, replica_groups=mesh['q'=64,'xh'=2,'xl'=2,'core'=2] {'xh','xl','core'}, dimensions={0} | all-to-all | bytes 524288 | tf_op jit(solution)/shard_map/all_to_all | solution.py:174
  126.7 17.7 %all_to_all.30 = f32[64,2,128]{2,1,0:T(2,128)S(1)} all-to-all(f32[64,2,128]{2,1,0:T(2,128)S(1)} %bitcast.59), channel_id=1, replica_groups=mesh['q'=64,'xh'=2,'xl'=2,'core'=2] {'q'}, dimensions={0} | all-to-all | bytes 131072 | tf_op jit(solution)/shard_map/all_to_all | solution.py:174
  144.4 9.4 %all_to_all.31 = f32[8,2,128]{2,1,0:T(2,128)S(1)} all-to-all(f32[8,2,128]{2,1,0:T(2,128)S(1)} %broadcast_in_dim.40), channel_id=1, replica_groups=mesh['q'=64,'xh'=2,'xl'=2,'core'=2] {'xh','xl','core'}, dimensions={0} | all-to-all | bytes 16384 | tf_op jit(solution)/shard_map/all_to_all | solution.py:174
  153.9 15.0 %all_to_all.32 = f32[64,2,128]{2,1,0:T(2,128)S(1)} all-to-all(f32[64,2,128]{2,1,0:T(2,128)S(1)} %broadcast_in_dim.41), channel_id=1, replica_groups=mesh['q'=64,'xh'=2,'xl'=2,'core'=2] {'q'}, dimensions={0} | all-to-all | bytes 131072 | tf_op jit(solution)/shard_map/all_to_all | solution.py:174
  169.0 11.7 %cholesky.17 = f32[128,128]{1,0:T(8,128)S(1)} custom-call(f32[128,128]{1,0:T(8,128)S(1)} %fusion.1), custom_call_target="Cholesky" | custom-call | tf_op jit(solution)/shard_map/jit(cholesky)/cholesky | solution.py:263
  182.7 9.8 %custom-call.6 = f32[1,128,128]{1,2,0:T(8,128)S(1)} custom-call(f32[1,128,128]{2,1,0:T(8,128)S(1)} %get-tuple-element.11), custom_call_target="InvertDiagBlocksLowerTriangular" | custom-call | tf_op jit(solution)/shard_map/triangular_solve | solution.py:266
  193.1 9.2 %all_to_all.33 = f32[4,32,512]{2,1,0:T(8,128)S(1)} all-to-all(f32[4,32,512]{2,1,0:T(8,128)S(1)} %bitcast.58), channel_id=1, replica_groups=mesh['q'=64,'xh'=2,'xl'=2,'core'=2] {'xl','core'}, dimensions={0} | all-to-all | bytes 524288 | tf_op jit(solution)/shard_map/all_to_all | solution.py:174
  (44 shorter events, 14.1 us)
Async XLA Ops:
  0.6 8.2 %copy-start.1 = (s32[24]{0:T(128)S(1)}, s32[24]{0:T(128)}, u32[]{:S(2)}) copy-start(s32[24]{0:T(128)} %param.8) | copy-start | bytes 292
  0.6 8.2 %copy-start.2 = (s32[24]{0:T(128)S(1)}, s32[24]{0:T(128)}, u32[]{:S(2)}) copy-start(s32[24]{0:T(128)} %param.7) | copy-start | bytes 292
  1.7 10.4 %collective-permute-start.3 = (f32[6,128,128]{2,1,0:T(8,128)S(1)}, f32[6,128,128]{2,1,0:T(8,128)S(1)}, u32[]{:S(2)}, u32[]{:S(2)}) collective-permute-start(f32[6,128,128]{2,1,0:T(8,128)S(1)} %constant_dynamic-slice_fusion), channel_id=1, source_target_pairs={{0,6},{2,4},{4,2},{6,0},{1,7},{3,5},{5,3},{7,1},{8,14},{10,12},{12... | collective-permute-start | bytes 1179656 | tf_op jit(solution)/shard_map/ppermute | solution.py:201
  7.6 27.6 %copy-start = (f32[24,128,128]{2,1,0:T(8,128)S(1)}, f32[24,128,128]{2,1,0:T(8,128)}, u32[]{:S(2)}) copy-start(f32[24,128,128]{2,1,0:T(8,128)} %refs_0_.1) | copy-start | bytes 4718596
  12.1 10.6 %collective-permute-start.4 = (f32[6,128,128]{2,1,0:T(8,128)S(1)}, f32[6,128,128]{2,1,0:T(8,128)S(1)}, u32[]{:S(2)}, u32[]{:S(2)}) collective-permute-start(f32[6,128,128]{2,1,0:T(8,128)S(1)} %collective-permute-done.3), channel_id=1, source_target_pairs={{0,2},{2,0},{1,3},{3,1},{4,6},{6,4},{5,7},{7,5},{8,10},{10,8},{9,1... | collective-permute-start | bytes 1179656 | tf_op jit(solution)/shard_map/ppermute | solution.py:170
  23.5 34.5 %collective-permute-start.5 = (f32[12,128,128]{2,1,0:T(8,128)}, f32[12,128,128]{2,1,0:T(8,128)}, u32[]{:S(2)}, u32[]{:S(2)}) collective-permute-start(f32[12,128,128]{2,1,0:T(8,128)} %constant_dynamic-update-slice_fusion.refs_0_), channel_id=1, source_target_pairs={{0,1},{1,0},{2,3},{3,2},{4,5},{5,4},{6,7},{7,6},{8,9},{9,8},{10,11... | collective-permute-start | bytes 2359304 | tf_op jit(solution)/shard_map/ppermute | solution.py:170
  31.8 8.6 %collective-permute-start = (f32[17,16,128]{2,1,0:T(8,128)S(1)}, f32[17,16,128]{2,1,0:T(8,128)S(1)}, u32[]{:S(2)}, u32[]{:S(2)}) collective-permute-start(f32[17,16,128]{2,1,0:T(8,128)S(1)} %pad_maximum_fusion.1), channel_id=1, source_target_pairs={{0,4},{4,0},{1,5},{5,1},{2,6},{6,2},{3,7},{7,3},{8,12},{12,8},{9,1... | collective-permute-start | bytes 417800 | tf_op jit(solution)/shard_map/ppermute | solution.py:170
  40.4 19.1 %collective-permute-start.2 = (f32[32,16,128]{2,1,0:T(8,128)S(1)}, f32[32,16,128]{2,1,0:T(8,128)S(1)}, u32[]{:S(2)}, u32[]{:S(2)}) collective-permute-start(f32[32,16,128]{2,1,0:T(8,128)S(1)} %pad_maximum_fusion.refs_2_.refs_4_), channel_id=1, source_target_pairs={{0,504},{8,0},{16,8},{24,16},{32,24},{40,32},{48,40},{56,48},{64,5... | collective-permute-start | bytes 786440 | tf_op jit(solution)/shard_map/ppermute | solution.py:240
  54.0 11.9 %collective-permute-start.1 = (f32[32,16,128]{2,1,0:T(8,128)S(1)}, f32[32,16,128]{2,1,0:T(8,128)S(1)}, u32[]{:S(2)}, u32[]{:S(2)}) collective-permute-start(f32[32,16,128]{2,1,0:T(8,128)S(1)} %pad_maximum_fusion.refs_2_.refs_4_), channel_id=1, source_target_pairs={{0,8},{8,16},{16,24},{24,32},{32,40},{40,48},{48,56},{56,64},{64,7... | collective-permute-start | bytes 786440 | tf_op jit(solution)/shard_map/ppermute | solution.py:239
  67.7 7.8 %collective-permute-start.7 = (f32[32,16,128]{2,1,0:T(8,128)S(1)}, f32[32,16,128]{2,1,0:T(8,128)S(1)}, u32[]{:S(2)}, u32[]{:S(2)}) collective-permute-start(f32[32,16,128]{2,1,0:T(8,128)S(1)} %shard_map.70.refs_2_.refs_4_), channel_id=1, source_target_pairs={{0,504},{8,0},{16,8},{24,16},{32,24},{40,32},{48,40},{56,48},{64,5... | collective-permute-start | bytes 786440 | tf_op jit(solution)/shard_map/ppermute | solution.py:240
  69.6 11.0 %collective-permute-start.6 = (f32[32,16,128]{2,1,0:T(8,128)S(1)}, f32[32,16,128]{2,1,0:T(8,128)S(1)}, u32[]{:S(2)}, u32[]{:S(2)}) collective-permute-start(f32[32,16,128]{2,1,0:T(8,128)S(1)} %shard_map.70.refs_2_.refs_4_), channel_id=1, source_target_pairs={{0,8},{8,16},{16,24},{24,32},{32,40},{40,48},{48,56},{56,64},{64,7... | collective-permute-start | bytes 786440 | tf_op jit(solution)/shard_map/ppermute | solution.py:239
  82.4 7.1 %collective-permute-start.9 = (f32[32,16,128]{2,1,0:T(8,128)S(1)}, f32[32,16,128]{2,1,0:T(8,128)S(1)}, u32[]{:S(2)}, u32[]{:S(2)}) collective-permute-start(f32[32,16,128]{2,1,0:T(8,128)S(1)} %shard_map.71.refs_2_.refs_4_), channel_id=1, source_target_pairs={{0,504},{8,0},{16,8},{24,16},{32,24},{40,32},{48,40},{56,48},{64,5... | collective-permute-start | bytes 786440 | tf_op jit(solution)/shard_map/ppermute | solution.py:240
  84.3 10.4 %collective-permute-start.8 = (f32[32,16,128]{2,1,0:T(8,128)S(1)}, f32[32,16,128]{2,1,0:T(8,128)S(1)}, u32[]{:S(2)}, u32[]{:S(2)}) collective-permute-start(f32[32,16,128]{2,1,0:T(8,128)S(1)} %shard_map.71.refs_2_.refs_4_), channel_id=1, source_target_pairs={{0,8},{8,16},{16,24},{24,32},{32,40},{40,48},{48,56},{56,64},{64,7... | collective-permute-start | bytes 786440 | tf_op jit(solution)/shard_map/ppermute | solution.py:239
  96.5 7.1 %collective-permute-start.11 = (f32[32,16,128]{2,1,0:T(8,128)S(1)}, f32[32,16,128]{2,1,0:T(8,128)S(1)}, u32[]{:S(2)}, u32[]{:S(2)}) collective-permute-start(f32[32,16,128]{2,1,0:T(8,128)S(1)} %shard_map.72.refs_2_), channel_id=1, source_target_pairs={{0,504},{8,0},{16,8},{24,16},{32,24},{40,32},{48,40},{56,48},{64,5... | collective-permute-start | bytes 786440 | tf_op jit(solution)/shard_map/ppermute | solution.py:240
  98.5 10.4 %collective-permute-start.10 = (f32[32,16,128]{2,1,0:T(8,128)S(1)}, f32[32,16,128]{2,1,0:T(8,128)S(1)}, u32[]{:S(2)}, u32[]{:S(2)}) collective-permute-start(f32[32,16,128]{2,1,0:T(8,128)S(1)} %shard_map.72.refs_2_), channel_id=1, source_target_pairs={{0,8},{8,16},{16,24},{24,32},{32,40},{40,48},{48,56},{56,64},{64,7... | collective-permute-start | bytes 786440 | tf_op jit(solution)/shard_map/ppermute | solution.py:239

commit v2 on v1

--- a/solution.py
+++ b/solution.py
@@ -1,4 +1,5 @@
 import functools
+import math
 
 import jax
 import jax.numpy as jnp
@@ -16,6 +17,8 @@
 COLS = 16
 HALF = 2 * RB_DEV
 UNROLL = 4
+BLOCK = 32
+FEW = 4
 GROUP = ("xh", "xl", "core")
 COL = ("xl", "core")
 VMEM = pl.BlockSpec(memory_space=pltpu.VMEM)
@@ -156,14 +159,72 @@
     gram_ref[...] = dot_t(value, value, precision=lax.Precision.HIGHEST)
 
 
-def apply_kernel(inverse_ref, all_ref, out_ref):
-    out_ref[...] = lax.dot_general(
-        inverse_ref[...],
-        all_ref[...],
+def dot_n(left, right):
+    return lax.dot_general(
+        left,
+        right,
         (((1,), (0,)), ((), ())),
         preferred_element_type=jnp.float32,
         precision=lax.Precision.HIGHEST,
     )
+
+
+def eliminate(value, size):
+    shape = value.shape
+    row = lax.broadcasted_iota(jnp.int32, shape, 0)
+    for start in range(0, size, FEW):
+        raw = [jnp.broadcast_to(value[:, start + b : start + b + 1], shape) for b in range(FEW)]
+        lines = [jnp.broadcast_to(value[start + b : start + b + 1], shape) for b in range(FEW)]
+        small = [
+            [jnp.broadcast_to(raw[b][start + a : start + a + 1], shape) for b in range(a + 1)]
+            for a in range(FEW)
+        ]
+        columns, ups = [], []
+        for b in range(FEW):
+            root = lax.rsqrt(small[b][b])
+            for a in range(b + 1, FEW):
+                small[a][b] = small[a][b] * root
+            for a in range(b + 1, FEW):
+                for c in range(b + 1, a + 1):
+                    small[a][c] = small[a][c] - small[a][b] * small[c][b]
+            column, up = raw[b], lines[b]
+            for c in range(b):
+                column = column - columns[c] * small[b][c]
+                up = up - ups[c] * small[b][c]
+            columns.append(column * root)
+            ups.append(up * root)
+        change = columns[0] * ups[0]
+        for b in range(1, FEW):
+            change = change + columns[b] * ups[b]
+        value = jnp.where(row >= start + FEW, value - change, value)
+        for b in range(FEW):
+            value = jnp.where(row == start + b, ups[b], value)
+    return value
+
+
+def factor_kernel(scale, gram_ref, all_ref, factor_ref, ortho_ref, work):
+    row = lax.broadcasted_iota(jnp.int32, (K, K), 0)
+    lane = lax.broadcasted_iota(jnp.int32, (K, K), 1)
+    work[:, :K] = gram_ref[...]
+    work[:, K:] = (row == lane).astype(jnp.float32)
+    small_row = lax.broadcasted_iota(jnp.int32, (BLOCK, K), 0)
+    small_lane = lax.broadcasted_iota(jnp.int32, (BLOCK, K), 1)
+    unit = (small_row + BLOCK == small_lane).astype(jnp.float32)
+    for start in range(0, K, BLOCK):
+        rows = slice(start, start + BLOCK)
+        diagonal = work[rows, :K]
+        if start:
+            diagonal = pltpu.roll(diagonal, K - start, 1)
+        done = eliminate(jnp.where(small_lane < BLOCK, diagonal, unit), BLOCK)
+        inverse = pltpu.roll(done, K - BLOCK, 1)[:, :BLOCK]
+        ups = dot_n(inverse, work[rows, :])
+        work[rows, :] = ups
+        below = start + BLOCK
+        if below < K:
+            change = dot_n(ups[:, :K].T, ups)
+            work[below:, :] = work[below:, :] - change[below:]
+    factor_ref[...] = (jnp.where(lane >= row, work[:, :K], 0.0) / scale).T
+    ortho_ref[...] = dot_n(work[:, K:] * scale, all_ref[...])
 
 
 def exchange(value, axis):
@@ -178,7 +239,8 @@
     q = lax.axis_index("q")
     count_q = lax.axis_size("q")
     xh = lax.axis_index("xh")
-    c = lax.axis_index("xl") * 2 + lax.axis_index("core")
+    core = lax.axis_index("core")
+    c = lax.axis_index("xl") * 2 + core
     quarter = TILE_CAP // 4
 
     halves = start_panel.reshape(2, COLS, RB_DEV, BS)
@@ -210,6 +272,7 @@
     def window_place(cols):
         owner = cols // RB_DEV
         step = (owner // 2 - q + 1 + count_q) % count_q
+        step = jnp.where(core == 1, 2 - step, step)
         place = step * HALF + ((owner % 2) ^ xh) * RB_DEV + cols % RB_DEV
         return jnp.clip(place, 0, 3 * HALF - 1)
 
@@ -232,12 +295,17 @@
         ]
     )
 
-    up = [(i, (i + 1) % count_q) for i in range(count_q)]
-    down = [(i, (i - 1) % count_q) for i in range(count_q)]
+    def pairs(shift):
+        return [
+            (2 * i + k, 2 * ((i + (shift if k == 0 else -shift)) % count_q) + k)
+            for i in range(count_q)
+            for k in range(2)
+        ]
+
     previous, current = None, panel
     for step in range(DEGREE):
-        lower = lax.ppermute(current, "q", up)
-        higher = lax.ppermute(current, "q", down)
+        lower = lax.ppermute(current, ("q", "core"), pairs(1))
+        higher = lax.ppermute(current, ("q", "core"), pairs(-1))
         upcoming = graph_step(
             table, (lower, current, higher), previous, own_tiles, other_tiles, step == DEGREE - 1
         )
@@ -260,23 +328,22 @@
     spread = to_all(jnp.broadcast_to(spread[None], (8, rows, K)), GROUP).sum(axis=0)
     gram = to_all(jnp.broadcast_to(spread[None], (count_q, rows, K)), "q").reshape(K, K)
 
-    factor = jnp.linalg.cholesky(gram)
     total_rows = start_panel.shape[1] * count_q * 2
-    scale = jnp.sqrt(jnp.asarray(total_rows, jnp.float32))
-    inverse = lax.linalg.triangular_solve(
-        factor, jnp.eye(K, dtype=jnp.float32), left_side=True, lower=True
-    )
-    ortho = call(
-        apply_kernel,
-        jax.ShapeDtypeStruct((K, 4 * BS), jnp.float32),
-        [inverse * scale, everything],
+    factor, ortho = call(
+        functools.partial(factor_kernel, math.sqrt(total_rows)),
+        (
+            jax.ShapeDtypeStruct((K, K), jnp.float32),
+            jax.ShapeDtypeStruct((K, 4 * BS), jnp.float32),
+        ),
+        [gram, everything],
         [VMEM, VMEM],
+        scratch=[pltpu.VMEM((K, 2 * K), jnp.float32)],
         flops=2 * K * K * 4 * BS * 6,
         moved=1 << 20,
     )
     ortho = to_all(ortho.reshape(4, K // 4, 4 * BS), COL)
     ortho_panel = ortho.transpose(1, 0, 2).reshape(K // 4, 16 * BS)
-    return (ortho_panel, factor / scale)
+    return (ortho_panel, factor)
 
 
 def solution(mesh):

time: 204 us -> 186 us (0.912)
  other arithmetic: 24.3 us -> 0.81 us
  waiting for transfers between devices: 40.1 us -> 26.6 us
  starting transfers between devices: 53.6 us -> 66.5 us
  Pallas kernels: 9.59 us -> 17.3 us
    another operation x4 -> x0, other arithmetic: 22.2 us -> none  [the longest x3 12.4 us: filtered_basis(): factor = jnp.linalg.cholesky(gram)]
    ppermute x8, waiting for transfers between devices: 28.2 us -> 14.7 us  [the longest x4 9.23 us: filtered_basis(): lower = lax.ppermute(current, ('q', 'core'), pairs(1))]
    ppermute x8, starting transfers between devices: 31.3 us -> 44.1 us  [the longest x4 34.4 us: filtered_basis(): lower = lax.ppermute(current, ('q', 'core'), pairs(1))]
    pallas_call x8, Pallas kernels: 9.59 us -> 17.3 us  [call(): pl.pallas_call(kernel, out_shape=out_shape, in_specs=specs, out_specs=out...]
  transfers between devices with their start and end apart: 12 -> 12, of which waited for: 10 -> 10; matrix products, arithmetic and copies ran while one was open for 2% -> 3% of each run, Pallas kernels for 1% -> 1%
where the time goes in v2:
time: 186 us; the launch traced here: 185 us
  starting transfers between devices  66.5 us (36%)
  blocking collectives  66.1 us (36%)
  waiting for transfers between devices  26.6 us (14%)
  Pallas kernels  17.3 us (9%)
  local copies, waits for them, and re-layouts  6.53 us (4%)
    all_to_all x5, blocking collectives, to_all(): return lax.all_to_all(value, axis, 0, 0, tiled=True)  66.1 us
    ppermute x4, starting transfers between devices, filtered_basis(): lower = lax.ppermute(current, ('q', 'core'), pairs(1))  34.4 us
    pallas_call x8, Pallas kernels, call(): pl.pallas_call(kernel, out_shape=out_shape, in_specs=specs, out_specs=out...  17.3 us
    ppermute x3, starting transfers between devices, exchange(): return lax.ppermute(value, axis, [(0, 1), (1, 0)])  17.1 us
    ppermute x4, starting transfers between devices, filtered_basis(): higher = lax.ppermute(current, ('q', 'core'), pairs(-1))  9.72 us
    ppermute x4, waiting for transfers between devices, filtered_basis(): lower = lax.ppermute(current, ('q', 'core'), pairs(1))  9.23 us
    ppermute x3, waiting for transfers between devices, exchange(): return lax.ppermute(value, axis, [(0, 1), (1, 0)])  9.2 us
    ppermute x4, waiting for transfers between devices, filtered_basis(): higher = lax.ppermute(current, ('q', 'core'), pairs(-1))  5.46 us
  transfers between devices with their start and end apart: 12, of which 10 were waited for; matrix products, arithmetic and copies ran while one was open for 3% of the time, Pallas kernels for 1%

profile of v2, /device:TPU:1, one launch (start us, length us, event | category | flops | bytes accessed | tf_op | source)
XLA Modules:
  0.0 185.4 jit_solution(16289784614428426753)
XLA Ops:
  1.7 5.2 %collective-permute-start.3 = (f32[6,128,128]{2,1,0:T(8,128)S(1)}, f32[6,128,128]{2,1,0:T(8,128)S(1)}, u32[]{:S(2)}, u32[]{:S(2)}) collective-permute-start(f32[6,128,128]{2,1,0:T(8,128)S(1)} %constant_dynamic-slice_fusion), channel_id=1, source_target_pairs={{0,6},{2,4},{4,2},{6,0},{1,7},{3,5},{5,3},{7,1},{8,14},{10,12},{12... | collective-permute-start | bytes 1179656 | tf_op jit(solution)/shard_map/ppermute | solution.py:263
  9.4 2.7 %collective-permute-done.3 = f32[6,128,128]{2,1,0:T(8,128)S(1)} collective-permute-done((f32[6,128,128]{2,1,0:T(8,128)S(1)}, f32[6,128,128]{2,1,0:T(8,128)S(1)}, u32[]{:S(2)}, u32[]{:S(2)}) %collective-permute-start.3) | collective-permute-done | bytes 393248 | tf_op jit(solution)/shard_map/ppermute | solution.py:263
  12.1 5.4 %collective-permute-start.4 = (f32[6,128,128]{2,1,0:T(8,128)S(1)}, f32[6,128,128]{2,1,0:T(8,128)S(1)}, u32[]{:S(2)}, u32[]{:S(2)}) collective-permute-start(f32[6,128,128]{2,1,0:T(8,128)S(1)} %collective-permute-done.3), channel_id=1, source_target_pairs={{0,2},{2,0},{1,3},{3,1},{4,6},{6,4},{5,7},{7,5},{8,10},{10,8},{9,1... | collective-permute-start | bytes 1179656 | tf_op jit(solution)/shard_map/ppermute | solution.py:231
  18.4 4.3 %collective-permute-done.4 = f32[6,128,128]{2,1,0:T(8,128)S(1)} collective-permute-done((f32[6,128,128]{2,1,0:T(8,128)S(1)}, f32[6,128,128]{2,1,0:T(8,128)S(1)}, u32[]{:S(2)}, u32[]{:S(2)}) %collective-permute-start.4) | collective-permute-done | bytes 393248 | tf_op jit(solution)/shard_map/ppermute | solution.py:231
  23.5 8.3 %collective-permute-start.5 = (f32[12,128,128]{2,1,0:T(8,128)}, f32[12,128,128]{2,1,0:T(8,128)}, u32[]{:S(2)}, u32[]{:S(2)}) collective-permute-start(f32[12,128,128]{2,1,0:T(8,128)} %constant_dynamic-update-slice_fusion.refs_0_), channel_id=1, source_target_pairs={{0,1},{1,0},{2,3},{3,2},{4,5},{5,4},{6,7},{7,6},{8,9},{9,8},{10,11... | collective-permute-start | bytes 2359304 | tf_op jit(solution)/shard_map/ppermute | solution.py:231
  31.8 3.4 %collective-permute-start = (f32[17,16,128]{2,1,0:T(8,128)S(1)}, f32[17,16,128]{2,1,0:T(8,128)S(1)}, u32[]{:S(2)}, u32[]{:S(2)}) collective-permute-start(f32[17,16,128]{2,1,0:T(8,128)S(1)} %pad_maximum_fusion.1), channel_id=1, source_target_pairs={{0,4},{4,0},{1,5},{5,1},{2,6},{6,2},{3,7},{7,3},{8,12},{12,8},{9,1... | collective-permute-start | bytes 417800 | tf_op jit(solution)/shard_map/ppermute | solution.py:231
  35.5 4.9 %collective-permute-done = f32[17,16,128]{2,1,0:T(8,128)S(1)} collective-permute-done((f32[17,16,128]{2,1,0:T(8,128)S(1)}, f32[17,16,128]{2,1,0:T(8,128)S(1)}, u32[]{:S(2)}, u32[]{:S(2)}) %collective-permute-start) | collective-permute-done | bytes 139296 | tf_op jit(solution)/shard_map/ppermute | solution.py:231
  40.4 4.0 %collective-permute-start.2 = (f32[32,16,128]{2,1,0:T(8,128)S(1)}, f32[32,16,128]{2,1,0:T(8,128)S(1)}, u32[]{:S(2)}, u32[]{:S(2)}) collective-permute-start(f32[32,16,128]{2,1,0:T(8,128)S(1)} %pad_maximum_fusion.refs_2_.refs_4_), channel_id=1, source_target_pairs={{0,504},{1,9},{8,0},{9,17},{16,8},{17,25},{24,16},{25,33},{32,24},... | collective-permute-start | bytes 786440 | tf_op jit(solution)/shard_map/ppermute | solution.py:308
  44.4 11.5 %collective-permute-start.1 = (f32[32,16,128]{2,1,0:T(8,128)S(1)}, f32[32,16,128]{2,1,0:T(8,128)S(1)}, u32[]{:S(2)}, u32[]{:S(2)}) collective-permute-start(f32[32,16,128]{2,1,0:T(8,128)S(1)} %pad_maximum_fusion.refs_2_.refs_4_), channel_id=1, source_target_pairs={{0,8},{1,505},{8,16},{9,1},{16,24},{17,9},{24,32},{25,17},{32,40},... | collective-permute-start | bytes 786440 | tf_op jit(solution)/shard_map/ppermute | solution.py:307
  59.4 2.0 %collective-permute-done.1.refs_1_ = f32[32,16,128]{2,1,0:T(8,128)S(1)} collective-permute-done((f32[32,16,128]{2,1,0:T(8,128)S(1)}, f32[32,16,128]{2,1,0:T(8,128)S(1)}, u32[]{:S(2)}, u32[]{:S(2)}) %collective-permute-start.1) | collective-permute-done | bytes 262176 | tf_op jit(solution)/shard_map/ppermute | solution.py:307
  61.4 1.7 shard_map.70.refs_2_.refs_4_
  63.2 1.9 %collective-permute-start.7 = (f32[32,16,128]{2,1,0:T(8,128)S(1)}, f32[32,16,128]{2,1,0:T(8,128)S(1)}, u32[]{:S(2)}, u32[]{:S(2)}) collective-permute-start(f32[32,16,128]{2,1,0:T(8,128)S(1)} %shard_map.70.refs_2_.refs_4_), channel_id=1, source_target_pairs={{0,504},{1,9},{8,0},{9,17},{16,8},{17,25},{24,16},{25,33},{32,24},... | collective-permute-start | bytes 786440 | tf_op jit(solution)/shard_map/ppermute | solution.py:308
  65.1 7.6 %collective-permute-start.6 = (f32[32,16,128]{2,1,0:T(8,128)S(1)}, f32[32,16,128]{2,1,0:T(8,128)S(1)}, u32[]{:S(2)}, u32[]{:S(2)}) collective-permute-start(f32[32,16,128]{2,1,0:T(8,128)S(1)} %shard_map.70.refs_2_.refs_4_), channel_id=1, source_target_pairs={{0,8},{1,505},{8,16},{9,1},{16,24},{17,9},{24,32},{25,17},{32,40},... | collective-permute-start | bytes 786440 | tf_op jit(solution)/shard_map/ppermute | solution.py:307
  72.7 1.8 collective-permute-done.7.refs_3_
  74.6 2.9 %collective-permute-done.6.refs_1_ = f32[32,16,128]{2,1,0:T(8,128)S(1)} collective-permute-done((f32[32,16,128]{2,1,0:T(8,128)S(1)}, f32[32,16,128]{2,1,0:T(8,128)S(1)}, u32[]{:S(2)}, u32[]{:S(2)}) %collective-permute-start.6) | collective-permute-done | bytes 262176 | tf_op jit(solution)/shard_map/ppermute | solution.py:307
  77.5 1.8 shard_map.71.refs_2_.refs_4_
  79.2 1.9 %collective-permute-start.9 = (f32[32,16,128]{2,1,0:T(8,128)S(1)}, f32[32,16,128]{2,1,0:T(8,128)S(1)}, u32[]{:S(2)}, u32[]{:S(2)}) collective-permute-start(f32[32,16,128]{2,1,0:T(8,128)S(1)} %shard_map.71.refs_2_.refs_4_), channel_id=1, source_target_pairs={{0,504},{1,9},{8,0},{9,17},{16,8},{17,25},{24,16},{25,33},{32,24},... | collective-permute-start | bytes 786440 | tf_op jit(solution)/shard_map/ppermute | solution.py:308
  81.2 7.6 %collective-permute-start.8 = (f32[32,16,128]{2,1,0:T(8,128)S(1)}, f32[32,16,128]{2,1,0:T(8,128)S(1)}, u32[]{:S(2)}, u32[]{:S(2)}) collective-permute-start(f32[32,16,128]{2,1,0:T(8,128)S(1)} %shard_map.71.refs_2_.refs_4_), channel_id=1, source_target_pairs={{0,8},{1,505},{8,16},{9,1},{16,24},{17,9},{24,32},{25,17},{32,40},... | collective-permute-start | bytes 786440 | tf_op jit(solution)/shard_map/ppermute | solution.py:307
  88.8 1.8 collective-permute-done.9.refs_3_
  90.6 2.2 %collective-permute-done.8.refs_1_ = f32[32,16,128]{2,1,0:T(8,128)S(1)} collective-permute-done((f32[32,16,128]{2,1,0:T(8,128)S(1)}, f32[32,16,128]{2,1,0:T(8,128)S(1)}, u32[]{:S(2)}, u32[]{:S(2)}) %collective-permute-start.8) | collective-permute-done | bytes 262176 | tf_op jit(solution)/shard_map/ppermute | solution.py:307
  92.8 1.8 shard_map.72.refs_2_
  94.6 1.9 %collective-permute-start.11 = (f32[32,16,128]{2,1,0:T(8,128)S(1)}, f32[32,16,128]{2,1,0:T(8,128)S(1)}, u32[]{:S(2)}, u32[]{:S(2)}) collective-permute-start(f32[32,16,128]{2,1,0:T(8,128)S(1)} %shard_map.72.refs_2_), channel_id=1, source_target_pairs={{0,504},{1,9},{8,0},{9,17},{16,8},{17,25},{24,16},{25,33},{32,24},... | collective-permute-start | bytes 786440 | tf_op jit(solution)/shard_map/ppermute | solution.py:308
  96.5 7.6 %collective-permute-start.10 = (f32[32,16,128]{2,1,0:T(8,128)S(1)}, f32[32,16,128]{2,1,0:T(8,128)S(1)}, u32[]{:S(2)}, u32[]{:S(2)}) collective-permute-start(f32[32,16,128]{2,1,0:T(8,128)S(1)} %shard_map.72.refs_2_), channel_id=1, source_target_pairs={{0,8},{1,505},{8,16},{9,1},{16,24},{17,9},{24,32},{25,17},{32,40},... | collective-permute-start | bytes 786440 | tf_op jit(solution)/shard_map/ppermute | solution.py:307
  104.1 1.8 collective-permute-done.11.refs_3_
  106.0 2.2 %collective-permute-done.10.refs_1_ = f32[32,16,128]{2,1,0:T(8,128)S(1)} collective-permute-done((f32[32,16,128]{2,1,0:T(8,128)S(1)}, f32[32,16,128]{2,1,0:T(8,128)S(1)}, u32[]{:S(2)}, u32[]{:S(2)}) %collective-permute-start.10) | collective-permute-done | bytes 262176 | tf_op jit(solution)/shard_map/ppermute | solution.py:307
  108.1 1.8 shard_map.73
  109.9 15.6 %all_to_all.29.parts_ref = f32[8,4,16,128]{3,2,1,0:T(8,128)S(1)} all-to-all(f32[8,4,16,128]{3,2,1,0:T(8,128)S(1)} %bitcast.48), channel_id=1, replica_groups=mesh['q'=64,'xh'=2,'xl'=2,'core'=2] {'xh','xl','core'}, dimensions={0} | all-to-all | bytes 524288 | tf_op jit(solution)/shard_map/all_to_all | solution.py:235
  125.9 16.9 %all_to_all.30 = f32[64,2,128]{2,1,0:T(2,128)S(1)} all-to-all(f32[64,2,128]{2,1,0:T(2,128)S(1)} %bitcast.51), channel_id=1, replica_groups=mesh['q'=64,'xh'=2,'xl'=2,'core'=2] {'q'}, dimensions={0} | all-to-all | bytes 131072 | tf_op jit(solution)/shard_map/all_to_all | solution.py:235
  142.9 9.4 %all_to_all.31 = f32[8,2,128]{2,1,0:T(2,128)S(1)} all-to-all(f32[8,2,128]{2,1,0:T(2,128)S(1)} %broadcast_in_dim.38), channel_id=1, replica_groups=mesh['q'=64,'xh'=2,'xl'=2,'core'=2] {'xh','xl','core'}, dimensions={0} | all-to-all | bytes 16384 | tf_op jit(solution)/shard_map/all_to_all | solution.py:235
  152.4 15.0 %all_to_all.32 = f32[64,2,128]{2,1,0:T(2,128)S(1)} all-to-all(f32[64,2,128]{2,1,0:T(2,128)S(1)} %broadcast_in_dim.39), channel_id=1, replica_groups=mesh['q'=64,'xh'=2,'xl'=2,'core'=2] {'q'}, dimensions={0} | all-to-all | bytes 131072 | tf_op jit(solution)/shard_map/all_to_all | solution.py:235
  167.4 8.1 %shard_map.75 = (f32[128,128]{1,0:T(8,128)}, f32[128,512]{1,0:T(8,128)S(1)}) custom-call(f32[128,128]{1,0:T(8,128)S(1)} %bitcast.50, f32[128,512]{1,0:T(8,128)S(1)} %get-tuple-element.7.all_ref), custom_call_target="tpu_custom_call" | custom-call | flops 100663296 | bytes 1048576 | tf_op jit(solution)/shard_map/pallas_call | solution.py:37
  175.5 9.1 %all_to_all.33 = f32[4,32,512]{2,1,0:T(8,128)S(1)} all-to-all(f32[4,32,512]{2,1,0:T(8,128)S(1)} %bitcast.49), channel_id=1, replica_groups=mesh['q'=64,'xh'=2,'xl'=2,'core'=2] {'xl','core'}, dimensions={0} | all-to-all | bytes 524288 | tf_op jit(solution)/shard_map/all_to_all | solution.py:235
  (36 shorter events, 9.5 us)
Async XLA Ops:
  0.6 8.2 %copy-start.1 = (s32[24]{0:T(128)S(1)}, s32[24]{0:T(128)}, u32[]{:S(2)}) copy-start(s32[24]{0:T(128)} %param.8) | copy-start | bytes 292
  0.6 8.2 %copy-start.2 = (s32[24]{0:T(128)S(1)}, s32[24]{0:T(128)}, u32[]{:S(2)}) copy-start(s32[24]{0:T(128)} %param.7) | copy-start | bytes 292
  1.7 10.4 %collective-permute-start.3 = (f32[6,128,128]{2,1,0:T(8,128)S(1)}, f32[6,128,128]{2,1,0:T(8,128)S(1)}, u32[]{:S(2)}, u32[]{:S(2)}) collective-permute-start(f32[6,128,128]{2,1,0:T(8,128)S(1)} %constant_dynamic-slice_fusion), channel_id=1, source_target_pairs={{0,6},{2,4},{4,2},{6,0},{1,7},{3,5},{5,3},{7,1},{8,14},{10,12},{12... | collective-permute-start | bytes 1179656 | tf_op jit(solution)/shard_map/ppermute | solution.py:263
  7.6 27.6 %copy-start = (f32[24,128,128]{2,1,0:T(8,128)S(1)}, f32[24,128,128]{2,1,0:T(8,128)}, u32[]{:S(2)}) copy-start(f32[24,128,128]{2,1,0:T(8,128)} %refs_0_.1) | copy-start | bytes 4718596
  12.1 10.6 %collective-permute-start.4 = (f32[6,128,128]{2,1,0:T(8,128)S(1)}, f32[6,128,128]{2,1,0:T(8,128)S(1)}, u32[]{:S(2)}, u32[]{:S(2)}) collective-permute-start(f32[6,128,128]{2,1,0:T(8,128)S(1)} %collective-permute-done.3), channel_id=1, source_target_pairs={{0,2},{2,0},{1,3},{3,1},{4,6},{6,4},{5,7},{7,5},{8,10},{10,8},{9,1... | collective-permute-start | bytes 1179656 | tf_op jit(solution)/shard_map/ppermute | solution.py:231
  23.5 34.3 %collective-permute-start.5 = (f32[12,128,128]{2,1,0:T(8,128)}, f32[12,128,128]{2,1,0:T(8,128)}, u32[]{:S(2)}, u32[]{:S(2)}) collective-permute-start(f32[12,128,128]{2,1,0:T(8,128)} %constant_dynamic-update-slice_fusion.refs_0_), channel_id=1, source_target_pairs={{0,1},{1,0},{2,3},{3,2},{4,5},{5,4},{6,7},{7,6},{8,9},{9,8},{10,11... | collective-permute-start | bytes 2359304 | tf_op jit(solution)/shard_map/ppermute | solution.py:231
  31.8 8.6 %collective-permute-start = (f32[17,16,128]{2,1,0:T(8,128)S(1)}, f32[17,16,128]{2,1,0:T(8,128)S(1)}, u32[]{:S(2)}, u32[]{:S(2)}) collective-permute-start(f32[17,16,128]{2,1,0:T(8,128)S(1)} %pad_maximum_fusion.1), channel_id=1, source_target_pairs={{0,4},{4,0},{1,5},{5,1},{2,6},{6,2},{3,7},{7,3},{8,12},{12,8},{9,1... | collective-permute-start | bytes 417800 | tf_op jit(solution)/shard_map/ppermute | solution.py:231
  40.4 19.0 %collective-permute-start.2 = (f32[32,16,128]{2,1,0:T(8,128)S(1)}, f32[32,16,128]{2,1,0:T(8,128)S(1)}, u32[]{:S(2)}, u32[]{:S(2)}) collective-permute-start(f32[32,16,128]{2,1,0:T(8,128)S(1)} %pad_maximum_fusion.refs_2_.refs_4_), channel_id=1, source_target_pairs={{0,504},{1,9},{8,0},{9,17},{16,8},{17,25},{24,16},{25,33},{32,24},... | collective-permute-start | bytes 786440 | tf_op jit(solution)/shard_map/ppermute | solution.py:308
  44.4 17.0 %collective-permute-start.1 = (f32[32,16,128]{2,1,0:T(8,128)S(1)}, f32[32,16,128]{2,1,0:T(8,128)S(1)}, u32[]{:S(2)}, u32[]{:S(2)}) collective-permute-start(f32[32,16,128]{2,1,0:T(8,128)S(1)} %pad_maximum_fusion.refs_2_.refs_4_), channel_id=1, source_target_pairs={{0,8},{1,505},{8,16},{9,1},{16,24},{17,9},{24,32},{25,17},{32,40},... | collective-permute-start | bytes 786440 | tf_op jit(solution)/shard_map/ppermute | solution.py:307
  63.2 11.4 %collective-permute-start.7 = (f32[32,16,128]{2,1,0:T(8,128)S(1)}, f32[32,16,128]{2,1,0:T(8,128)S(1)}, u32[]{:S(2)}, u32[]{:S(2)}) collective-permute-start(f32[32,16,128]{2,1,0:T(8,128)S(1)} %shard_map.70.refs_2_.refs_4_), channel_id=1, source_target_pairs={{0,504},{1,9},{8,0},{9,17},{16,8},{17,25},{24,16},{25,33},{32,24},... | collective-permute-start | bytes 786440 | tf_op jit(solution)/shard_map/ppermute | solution.py:308
  65.1 12.4 %collective-permute-start.6 = (f32[32,16,128]{2,1,0:T(8,128)S(1)}, f32[32,16,128]{2,1,0:T(8,128)S(1)}, u32[]{:S(2)}, u32[]{:S(2)}) collective-permute-start(f32[32,16,128]{2,1,0:T(8,128)S(1)} %shard_map.70.refs_2_.refs_4_), channel_id=1, source_target_pairs={{0,8},{1,505},{8,16},{9,1},{16,24},{17,9},{24,32},{25,17},{32,40},... | collective-permute-start | bytes 786440 | tf_op jit(solution)/shard_map/ppermute | solution.py:307
  79.2 11.4 %collective-permute-start.9 = (f32[32,16,128]{2,1,0:T(8,128)S(1)}, f32[32,16,128]{2,1,0:T(8,128)S(1)}, u32[]{:S(2)}, u32[]{:S(2)}) collective-permute-start(f32[32,16,128]{2,1,0:T(8,128)S(1)} %shard_map.71.refs_2_.refs_4_), channel_id=1, source_target_pairs={{0,504},{1,9},{8,0},{9,17},{16,8},{17,25},{24,16},{25,33},{32,24},... | collective-permute-start | bytes 786440 | tf_op jit(solution)/shard_map/ppermute | solution.py:308
  81.2 11.6 %collective-permute-start.8 = (f32[32,16,128]{2,1,0:T(8,128)S(1)}, f32[32,16,128]{2,1,0:T(8,128)S(1)}, u32[]{:S(2)}, u32[]{:S(2)}) collective-permute-start(f32[32,16,128]{2,1,0:T(8,128)S(1)} %shard_map.71.refs_2_.refs_4_), channel_id=1, source_target_pairs={{0,8},{1,505},{8,16},{9,1},{16,24},{17,9},{24,32},{25,17},{32,40},... | collective-permute-start | bytes 786440 | tf_op jit(solution)/shard_map/ppermute | solution.py:307
  94.6 11.4 %collective-permute-start.11 = (f32[32,16,128]{2,1,0:T(8,128)S(1)}, f32[32,16,128]{2,1,0:T(8,128)S(1)}, u32[]{:S(2)}, u32[]{:S(2)}) collective-permute-start(f32[32,16,128]{2,1,0:T(8,128)S(1)} %shard_map.72.refs_2_), channel_id=1, source_target_pairs={{0,504},{1,9},{8,0},{9,17},{16,8},{17,25},{24,16},{25,33},{32,24},... | collective-permute-start | bytes 786440 | tf_op jit(solution)/shard_map/ppermute | solution.py:308
  96.5 11.6 %collective-permute-start.10 = (f32[32,16,128]{2,1,0:T(8,128)S(1)}, f32[32,16,128]{2,1,0:T(8,128)S(1)}, u32[]{:S(2)}, u32[]{:S(2)}) collective-permute-start(f32[32,16,128]{2,1,0:T(8,128)S(1)} %shard_map.72.refs_2_), channel_id=1, source_target_pairs={{0,8},{1,505},{8,16},{9,1},{16,24},{17,9},{24,32},{25,17},{32,40},... | collective-permute-start | bytes 786440 | tf_op jit(solution)/shard_map/ppermute | solution.py:307

commit v3 on v2

--- a/solution.py
+++ b/solution.py
@@ -13,6 +13,7 @@
 K = 128
 RB_DEV = 16
 TILE_CAP = 24
+REACH = 2
 DEGREE = 4
 COLS = 16
 HALF = 2 * RB_DEV
@@ -81,12 +82,8 @@
     )
 
 
-def step_kernel(first, last, *refs):
-    if first:
-        table, low_ref, mid_ref, high_ref, own_ref, other_ref, out_ref, window, total = refs
-        prev_ref = None
-    else:
-        table, low_ref, mid_ref, high_ref, prev_ref, own_ref, other_ref, out_ref, window, total = refs
+def step_kernel(last, *refs):
+    table, low_ref, mid_ref, high_ref, prev_ref, own_ref, other_ref, out_ref, window, total = refs
     for piece, ref in enumerate((low_ref, mid_ref, high_ref)):
         def fill(block, carry, piece=piece, ref=ref):
             high, low = split_bf16(ref[block])
@@ -121,20 +118,53 @@
 
     def finish(block, carry):
         source = block ^ swap if last else block
-        value = total[source]
-        if prev_ref is not None:
-            value = 2.0 * value - prev_ref[source]
-        out_ref[block] = value
+        out_ref[block] = 2.0 * total[source] - prev_ref[source]
         return carry
 
     lax.fori_loop(0, HALF, finish, 0, unroll=8)
 
 
+def first_kernel(*refs):
+    table, notes_ref, *pieces, tiles, mine_ref, given_ref, start_ref, window, total = refs
+    wide_cols = 2 * COLS
+    for piece, ref in enumerate(pieces):
+        for block in range(RB_DEV):
+            high, low = split_bf16(ref[:, block * BS : (block + 1) * BS])
+            window[piece * RB_DEV + block, 0:wide_cols] = high
+            window[piece * RB_DEV + block, wide_cols : 2 * wide_cols] = low
+    total[...] = jnp.zeros_like(total)
+    live = table[2 * TILE_CAP]
+    upper = table[2 * TILE_CAP + 1] == 1
+
+    def body(group, carry):
+        terms = []
+        for inner in range(UNROLL):
+            slot = group * UNROLL + inner
+            both = window[table[TILE_CAP + slot]]
+            wide = dot_t(both, tiles[slot, 0])
+            narrow = dot_t(both[:wide_cols], tiles[slot, 1])
+            term = wide[:wide_cols] + (wide[wide_cols:] + narrow)
+            terms.append(jnp.where(slot < live, term, jnp.zeros_like(term)))
+        for inner in range(UNROLL):
+            row = table[group * UNROLL + inner]
+            total[row] = total[row] + terms[inner]
+        return carry
+
+    lax.fori_loop(0, (live + UNROLL - 1) // UNROLL, body, 0)
+    for block in range(RB_DEV):
+        value = total[block]
+        mine_ref[block] = jnp.where(upper, value[COLS:], value[:COLS])
+        given_ref[block] = jnp.where(upper, value[:COLS], value[COLS:])
+        for half, ref in enumerate((pieces[0], pieces[3])):
+            value = ref[:, block * BS : (block + 1) * BS]
+            start_ref[half * RB_DEV + block] = jnp.where(upper, value[COLS:], value[:COLS])
+    given_ref[RB_DEV] = notes_ref[...]
+
+
 def graph_step(table, parts, prev, own_tiles, other_tiles, last):
-    first = prev is None
-    operands = [table, *parts] + ([] if first else [prev]) + [own_tiles, other_tiles]
+    operands = [table, *parts, prev, own_tiles, other_tiles]
     return call(
-        functools.partial(step_kernel, first, last),
+        functools.partial(step_kernel, last),
         jax.ShapeDtypeStruct((HALF, COLS, BS), jnp.float32),
         operands,
         [SMEM] + [VMEM] * (len(operands) - 1),
@@ -243,9 +273,37 @@
     c = lax.axis_index("xl") * 2 + core
     quarter = TILE_CAP // 4
 
-    halves = start_panel.reshape(2, COLS, RB_DEV, BS)
-    mine = lax.dynamic_index_in_dim(halves, xh, 0, keepdims=False).transpose(1, 0, 2)
-    given = lax.dynamic_index_in_dim(halves, 1 - xh, 0, keepdims=False).transpose(1, 0, 2)
+    def pairs(shift):
+        return [
+            (2 * i + k, 2 * ((i + (shift if k == 0 else -shift)) % count_q) + k)
+            for i in range(count_q)
+            for k in range(2)
+        ]
+
+    def halo(value):
+        one = lax.ppermute(value, ("q", "core"), pairs(1))
+        two = lax.ppermute(value, ("q", "core"), pairs(-1))
+        return one, two
+
+    count = 2 * count_q
+    near = [(b, (b + 1 if b % 2 else b - 1) % count) for b in range(count)]
+    diagonal = lax.ppermute(start_panel, ("q", "xh"), near)
+    across = exchange(start_panel, "xh")
+    one, two = halo(start_panel)
+    piece = lax.dynamic_slice_in_dim(tile_values, c * quarter, quarter, 0)
+    first = lax.ppermute(piece, ("xh", "xl"), [(i, 3 - i) for i in range(4)])
+    second = exchange(first, "xl")
+    pair = jnp.concatenate([first, second], axis=0)
+    far = exchange(pair, "core")
+    own_tiles = split_tiles([tile_values])
+    other_tiles = split_tiles([pair, far])
+
+    offset = (tile_cols // RB_DEV - 2 * q - xh + REACH + count) % count
+    side = jnp.where(core == 1, 2 * REACH - offset, offset)
+    place = jnp.where(offset % 2 == 1, jnp.where((offset == 3) == (xh == 0), 3, 4), 0)
+    place = jnp.where(side == 0, 1, jnp.where(side == 4, 2, place))
+    place = place * RB_DEV + tile_cols % RB_DEV
+    own_table = jnp.concatenate([tile_rows % RB_DEV, place, tile_counts, xh[None]])
     notes = jnp.concatenate(
         [
             tile_rows.astype(jnp.float32)[None],
@@ -255,17 +313,26 @@
         axis=0,
     )
     notes = jnp.pad(notes, ((0, COLS - 3), (0, BS - TILE_CAP)))
-    got = exchange(jnp.concatenate([given, notes[None]], axis=0), "xh")
-    panel = jnp.concatenate([mine, got[:RB_DEV]], axis=0)
+    half = jax.ShapeDtypeStruct((RB_DEV, COLS, BS), jnp.float32)
+    mine, given, previous = call(
+        first_kernel,
+        (
+            half,
+            jax.ShapeDtypeStruct((RB_DEV + 1, COLS, BS), jnp.float32),
+            jax.ShapeDtypeStruct((HALF, COLS, BS), jnp.float32),
+        ),
+        [own_table, notes, start_panel, one, two, across, diagonal, own_tiles],
+        [SMEM] + [VMEM] * 7,
+        scratch=[
+            pltpu.VMEM((5 * RB_DEV, 4 * COLS, BS), jnp.bfloat16),
+            pltpu.VMEM((RB_DEV, 2 * COLS, BS), jnp.float32),
+        ],
+        flops=2 * TILE_CAP * 6 * COLS * BS * BS,
+        moved=4 << 20,
+    )
+    got = exchange(given, "xh")
+    current = jnp.concatenate([mine, got[:RB_DEV]], axis=0)
     other = jnp.round(got[RB_DEV, :3, :TILE_CAP]).astype(jnp.int32)
-
-    piece = lax.dynamic_slice_in_dim(tile_values, c * quarter, quarter, 0)
-    first = lax.ppermute(piece, ("xh", "xl"), [(i, 3 - i) for i in range(4)])
-    second = exchange(first, "xl")
-    pair = jnp.concatenate([first, second], axis=0)
-    far = exchange(pair, "core")
-    own_tiles = split_tiles([tile_values])
-    other_tiles = split_tiles([pair, far])
 
     slots = jnp.arange(TILE_CAP, dtype=jnp.int32)
 
@@ -295,17 +362,8 @@
         ]
     )
 
-    def pairs(shift):
-        return [
-            (2 * i + k, 2 * ((i + (shift if k == 0 else -shift)) % count_q) + k)
-            for i in range(count_q)
-            for k in range(2)
-        ]
-
-    previous, current = None, panel
-    for step in range(DEGREE):
-        lower = lax.ppermute(current, ("q", "core"), pairs(1))
-        higher = lax.ppermute(current, ("q", "core"), pairs(-1))
+    for step in range(1, DEGREE):
+        lower, higher = halo(current)
         upcoming = graph_step(
             table, (lower, current, higher), previous, own_tiles, other_tiles, step == DEGREE - 1
         )

time: 186 us -> 176 us (0.946)
  waiting for transfers between devices: 26.6 us -> 16.9 us
    ppermute x3 -> x4, waiting for transfers between devices: 9.2 us -> 0.01 us  [exchange(): return lax.ppermute(value, axis, [(0, 1), (1, 0)])]
    ppermute x3 -> x4, starting transfers between devices: 17.1 us -> 12 us  [exchange(): return lax.ppermute(value, axis, [(0, 1), (1, 0)])]
    ppermute x8 -> x9, starting transfers between devices: 44.1 us -> 48.9 us  [the longest x4 33.6 us: halo(): one = lax.ppermute(value, ('q', 'core'), pairs(1))]
    ppermute x1, waiting for transfers between devices: 2.67 us -> 0.01 us  [filtered_basis(): first = lax.ppermute(piece, ('xh', 'xl'), [(i, 3 - i) for i in range(4)])]
    ppermute x8 -> x9, waiting for transfers between devices: 14.7 us -> 16.9 us  [the longest x4 7.14 us: halo(): one = lax.ppermute(value, ('q', 'core'), pairs(1))]
  transfers between devices with their start and end apart: 12 -> 14, of which waited for: 10 -> 6; matrix products, arithmetic and copies ran while one was open for 3% -> 1% of each run, Pallas kernels for 1% -> 1%
where the time goes in v3:
time: 176 us; the launch traced here: 175 us
  blocking collectives  66.7 us (38%)
  starting transfers between devices  66.1 us (38%)
  waiting for transfers between devices  16.9 us (10%)
  Pallas kernels  16.7 us (9%)
  local copies, waits for them, and re-layouts  5.92 us (3%)
    all_to_all x5, blocking collectives, to_all(): return lax.all_to_all(value, axis, 0, 0, tiled=True)  66.7 us
    ppermute x4, starting transfers between devices, halo(): one = lax.ppermute(value, ('q', 'core'), pairs(1))  33.6 us
    pallas_call x8, Pallas kernels, call(): pl.pallas_call(kernel, out_shape=out_shape, in_specs=specs, out_specs=out...  16.7 us
    ppermute x4, starting transfers between devices, exchange(): return lax.ppermute(value, axis, [(0, 1), (1, 0)])  12 us
    ppermute x4, starting transfers between devices, halo(): two = lax.ppermute(value, ('q', 'core'), pairs(-1))  9.77 us
    ppermute x4, waiting for transfers between devices, halo(): one = lax.ppermute(value, ('q', 'core'), pairs(1))  7.14 us
    ppermute x1, waiting for transfers between devices, filtered_basis(): diagonal = lax.ppermute(start_panel, ('q', 'xh'), near)  6.11 us
    ppermute x1, starting transfers between devices, filtered_basis(): diagonal = lax.ppermute(start_panel, ('q', 'xh'), near)  5.53 us
  transfers between devices with their start and end apart: 14, of which 6 were waited for; matrix products, arithmetic and copies ran while one was open for 1% of the time, Pallas kernels for 1%

profile of v3, /device:TPU:1, one launch (start us, length us, event | category | flops | bytes accessed | tf_op | source)
XLA Modules:
  0.0 175.0 jit_solution(3029466687710603282)
XLA Ops:
  0.7 1.8 %constant_dynamic-slice_fusion = f32[6,128,128]{2,1,0:T(8,128)} fusion(f32[24,128,128]{2,1,0:T(8,128)} %refs_0_.1, s32[]{:T(128)S(6)} %select_n.136), kind=kLoop, calls=%fused_computation.91 | loop fusion | bytes 786436 | tf_op jit(solution)/shard_map/dynamic_slice | solution.py:293
  2.5 5.2 %collective-permute-start.7 = (f32[6,128,128]{2,1,0:T(8,128)}, f32[6,128,128]{2,1,0:T(8,128)S(1)}, u32[]{:S(2)}, u32[]{:S(2)}) collective-permute-start(f32[6,128,128]{2,1,0:T(8,128)} %constant_dynamic-slice_fusion), channel_id=1, source_target_pairs={{0,6},{2,4},{4,2},{6,0},{1,7},{3,5},{5,3},{7,1},{8,14},{10,12},{12... | collective-permute-start | bytes 1179656 | tf_op jit(solution)/shard_map/ppermute | solution.py:294
  7.7 2.4 %collective-permute-start.2 = (f32[32,2048]{1,0:T(8,128)}, f32[32,2048]{1,0:T(8,128)S(1)}, u32[]{:S(2)}, u32[]{:S(2)}) collective-permute-start(f32[32,2048]{1,0:T(8,128)} %refs_2_.1), channel_id=1, source_target_pairs={{0,4},{4,0},{1,5},{5,1},{2,6},{6,2},{3,7},{7,3},{8,12},{12,8},{9,1... | collective-permute-start | bytes 786440 | tf_op jit(solution)/shard_map/ppermute | solution.py:261
  10.1 4.0 %collective-permute-start.1 = (f32[32,2048]{1,0:T(8,128)}, f32[32,2048]{1,0:T(8,128)S(1)}, u32[]{:S(2)}, u32[]{:S(2)}) collective-permute-start(f32[32,2048]{1,0:T(8,128)} %refs_2_.1), channel_id=1, source_target_pairs={{0,504},{1,9},{8,0},{9,17},{16,8},{17,25},{24,16},{25,33},{32,24},... | collective-permute-start | bytes 786440 | tf_op jit(solution)/shard_map/ppermute | solution.py:285
  14.1 11.5 %collective-permute-start = (f32[32,2048]{1,0:T(8,128)}, f32[32,2048]{1,0:T(8,128)S(1)}, u32[]{:S(2)}, u32[]{:S(2)}) collective-permute-start(f32[32,2048]{1,0:T(8,128)} %refs_2_.1), channel_id=1, source_target_pairs={{0,8},{1,505},{8,16},{9,1},{16,24},{17,9},{24,32},{25,17},{32,40},... | collective-permute-start | bytes 786440 | tf_op jit(solution)/shard_map/ppermute | solution.py:284
  25.6 5.5 %collective-permute-start.3 = (f32[32,2048]{1,0:T(8,128)}, f32[32,2048]{1,0:T(8,128)S(1)}, u32[]{:S(2)}, u32[]{:S(2)}) collective-permute-start(f32[32,2048]{1,0:T(8,128)} %refs_2_.1), channel_id=1, source_target_pairs={{0,508},{4,8},{8,4},{12,16},{16,12},{20,24},{24,20},{28,32},{32,28... | collective-permute-start | bytes 786440 | tf_op jit(solution)/shard_map/ppermute | solution.py:290
  31.2 1.4 copy-done
  33.6 1.9 %collective-permute-start.8 = (f32[6,128,128]{2,1,0:T(8,128)S(1)}, f32[6,128,128]{2,1,0:T(8,128)S(1)}, u32[]{:S(2)}, u32[]{:S(2)}) collective-permute-start(f32[6,128,128]{2,1,0:T(8,128)S(1)} %collective-permute-done.7), channel_id=1, source_target_pairs={{0,2},{2,0},{1,3},{3,1},{4,6},{6,4},{5,7},{7,5},{8,10},{10,8},{9,1... | collective-permute-start | bytes 1179656 | tf_op jit(solution)/shard_map/ppermute | solution.py:261
  35.7 6.1 %collective-permute-done.3.refs_6_ = f32[32,2048]{1,0:T(8,128)S(1)} collective-permute-done((f32[32,2048]{1,0:T(8,128)}, f32[32,2048]{1,0:T(8,128)S(1)}, u32[]{:S(2)}, u32[]{:S(2)}) %collective-permute-start.3) | collective-permute-done | bytes 262176 | tf_op jit(solution)/shard_map/ppermute | solution.py:290
  41.8 1.9 %shard_map.69 = (f32[16,16,128]{2,1,0:T(8,128)S(1)}, f32[17,16,128]{2,1,0:T(8,128)}, f32[32,16,128]{2,1,0:T(8,128)S(1)}) custom-call(s32[50]{0:T(128)S(1)} %pad_add_fusion.refs_0_, f32[16,128]{1,0:T(8,128)S(1)} %pad.4.refs_1_, f32[32,2048]{1,0:T(8,128)S(1)} %copy-done.1, f32[32,2048]{1,0:T(8,128)S(1)} %collective-permute-done.refs_3_, ...), custom_call_target="tpu_custom_call" | custom-call | flops 75497472 | bytes 4194304 | tf_op jit(solution)/shard_map/pallas_call | solution.py:38
  43.7 1.9 %collective-permute-start.4 = (f32[17,16,128]{2,1,0:T(8,128)}, f32[17,16,128]{2,1,0:T(8,128)S(1)}, u32[]{:S(2)}, u32[]{:S(2)}) collective-permute-start(f32[17,16,128]{2,1,0:T(8,128)} %get-tuple-element.9), channel_id=1, source_target_pairs={{0,4},{4,0},{1,5},{5,1},{2,6},{6,2},{3,7},{7,3},{8,12},{12,8},{9,1... | collective-permute-start | bytes 417800 | tf_op jit(solution)/shard_map/ppermute | solution.py:261
  45.7 5.8 %collective-permute-start.9 = (f32[12,128,128]{2,1,0:T(8,128)S(1)}, f32[12,128,128]{2,1,0:T(8,128)S(1)}, u32[]{:S(2)}, u32[]{:S(2)}) collective-permute-start(f32[12,128,128]{2,1,0:T(8,128)S(1)} %constant_dynamic-update-slice_fusion.refs_0_), channel_id=1, source_target_pairs={{0,1},{1,0},{2,3},{3,2},{4,5},{5,4},{6,7},{7,6},{8,9},{9,8},{10,11... | collective-permute-start | bytes 2359304 | tf_op jit(solution)/shard_map/ppermute | solution.py:261
  52.3 1.9 %collective-permute-start.6 = (f32[32,16,128]{2,1,0:T(8,128)S(1)}, f32[32,16,128]{2,1,0:T(8,128)}, u32[]{:S(2)}, u32[]{:S(2)}) collective-permute-start(f32[32,16,128]{2,1,0:T(8,128)S(1)} %pad_maximum_fusion.refs_2_.refs_4_), channel_id=1, source_target_pairs={{0,504},{1,9},{8,0},{9,17},{16,8},{17,25},{24,16},{25,33},{32,24},... | collective-permute-start | bytes 786440 | tf_op jit(solution)/shard_map/ppermute | solution.py:285
  54.2 6.7 %collective-permute-start.5 = (f32[32,16,128]{2,1,0:T(8,128)S(1)}, f32[32,16,128]{2,1,0:T(8,128)}, u32[]{:S(2)}, u32[]{:S(2)}) collective-permute-start(f32[32,16,128]{2,1,0:T(8,128)S(1)} %pad_maximum_fusion.refs_2_.refs_4_), channel_id=1, source_target_pairs={{0,8},{1,505},{8,16},{9,1},{16,24},{17,9},{24,32},{25,17},{32,40},... | collective-permute-start | bytes 786440 | tf_op jit(solution)/shard_map/ppermute | solution.py:284
  63.0 2.7 %collective-permute-done.5.refs_1_ = f32[32,16,128]{2,1,0:T(8,128)} collective-permute-done((f32[32,16,128]{2,1,0:T(8,128)S(1)}, f32[32,16,128]{2,1,0:T(8,128)}, u32[]{:S(2)}, u32[]{:S(2)}) %collective-permute-start.5) | collective-permute-done | bytes 262176 | tf_op jit(solution)/shard_map/ppermute | solution.py:284
  65.7 2.3 %shard_map.71.refs_2_.refs_4_ = f32[32,16,128]{2,1,0:T(8,128)S(1)} custom-call(s32[147]{0:T(256)S(1)} %concatenate.17.refs_0_, f32[32,16,128]{2,1,0:T(8,128)} %collective-permute-done.5.refs_1_, f32[32,16,128]{2,1,0:T(8,128)S(1)} %pad_maximum_fusion.refs_2_.refs_4_, f32[32,16,128]{2,1,0:T(8,128)} %collective-permute-done.6.refs_3_, ...), custom_call_target="tpu_custom_call" | custom-call | flops 75497472 | bytes 8388608 | tf_op jit(solution)/shard_map/pallas_call | solution.py:38
  68.0 1.9 %collective-permute-start.11 = (f32[32,16,128]{2,1,0:T(8,128)S(1)}, f32[32,16,128]{2,1,0:T(8,128)S(1)}, u32[]{:S(2)}, u32[]{:S(2)}) collective-permute-start(f32[32,16,128]{2,1,0:T(8,128)S(1)} %shard_map.71.refs_2_.refs_4_), channel_id=1, source_target_pairs={{0,504},{1,9},{8,0},{9,17},{16,8},{17,25},{24,16},{25,33},{32,24},... | collective-permute-start | bytes 786440 | tf_op jit(solution)/shard_map/ppermute | solution.py:285
  69.9 7.8 %collective-permute-start.10 = (f32[32,16,128]{2,1,0:T(8,128)S(1)}, f32[32,16,128]{2,1,0:T(8,128)S(1)}, u32[]{:S(2)}, u32[]{:S(2)}) collective-permute-start(f32[32,16,128]{2,1,0:T(8,128)S(1)} %shard_map.71.refs_2_.refs_4_), channel_id=1, source_target_pairs={{0,8},{1,505},{8,16},{9,1},{16,24},{17,9},{24,32},{25,17},{32,40},... | collective-permute-start | bytes 786440 | tf_op jit(solution)/shard_map/ppermute | solution.py:284
  77.7 1.8 %collective-permute-done.11.refs_3_ = f32[32,16,128]{2,1,0:T(8,128)S(1)} collective-permute-done((f32[32,16,128]{2,1,0:T(8,128)S(1)}, f32[32,16,128]{2,1,0:T(8,128)S(1)}, u32[]{:S(2)}, u32[]{:S(2)}) %collective-permute-start.11) | collective-permute-done | bytes 262176 | tf_op jit(solution)/shard_map/ppermute | solution.py:285
  79.5 2.3 %collective-permute-done.10.refs_1_ = f32[32,16,128]{2,1,0:T(8,128)S(1)} collective-permute-done((f32[32,16,128]{2,1,0:T(8,128)S(1)}, f32[32,16,128]{2,1,0:T(8,128)S(1)}, u32[]{:S(2)}, u32[]{:S(2)}) %collective-permute-start.10) | collective-permute-done | bytes 262176 | tf_op jit(solution)/shard_map/ppermute | solution.py:284
  81.8 1.8 %shard_map.72.refs_2_ = f32[32,16,128]{2,1,0:T(8,128)S(1)} custom-call(s32[147]{0:T(256)S(1)} %concatenate.17.refs_0_, f32[32,16,128]{2,1,0:T(8,128)S(1)} %collective-permute-done.10.refs_1_, f32[32,16,128]{2,1,0:T(8,128)S(1)} %shard_map.71.refs_2_.refs_4_, f32[32,16,128]{2,1,0:T(8,128)S(1)} %collective-permute-done.11.refs_3_, ...), custom_call_target="tpu_custom_call" | custom-call | flops 75497472 | bytes 8388608 | tf_op jit(solution)/shard_map/pallas_call | solution.py:38
  83.5 1.9 %collective-permute-start.13 = (f32[32,16,128]{2,1,0:T(8,128)S(1)}, f32[32,16,128]{2,1,0:T(8,128)S(1)}, u32[]{:S(2)}, u32[]{:S(2)}) collective-permute-start(f32[32,16,128]{2,1,0:T(8,128)S(1)} %shard_map.72.refs_2_), channel_id=1, source_target_pairs={{0,504},{1,9},{8,0},{9,17},{16,8},{17,25},{24,16},{25,33},{32,24},... | collective-permute-start | bytes 786440 | tf_op jit(solution)/shard_map/ppermute | solution.py:285
  85.5 7.6 %collective-permute-start.12 = (f32[32,16,128]{2,1,0:T(8,128)S(1)}, f32[32,16,128]{2,1,0:T(8,128)S(1)}, u32[]{:S(2)}, u32[]{:S(2)}) collective-permute-start(f32[32,16,128]{2,1,0:T(8,128)S(1)} %shard_map.72.refs_2_), channel_id=1, source_target_pairs={{0,8},{1,505},{8,16},{9,1},{16,24},{17,9},{24,32},{25,17},{32,40},... | collective-permute-start | bytes 786440 | tf_op jit(solution)/shard_map/ppermute | solution.py:284
  93.1 1.8 %collective-permute-done.13.refs_3_ = f32[32,16,128]{2,1,0:T(8,128)S(1)} collective-permute-done((f32[32,16,128]{2,1,0:T(8,128)S(1)}, f32[32,16,128]{2,1,0:T(8,128)S(1)}, u32[]{:S(2)}, u32[]{:S(2)}) %collective-permute-start.13) | collective-permute-done | bytes 262176 | tf_op jit(solution)/shard_map/ppermute | solution.py:285
  94.9 2.2 %collective-permute-done.12.refs_1_ = f32[32,16,128]{2,1,0:T(8,128)S(1)} collective-permute-done((f32[32,16,128]{2,1,0:T(8,128)S(1)}, f32[32,16,128]{2,1,0:T(8,128)S(1)}, u32[]{:S(2)}, u32[]{:S(2)}) %collective-permute-start.12) | collective-permute-done | bytes 262176 | tf_op jit(solution)/shard_map/ppermute | solution.py:284
  97.1 1.8 %shard_map.73 = f32[32,16,128]{2,1,0:T(8,128)S(1)} custom-call(s32[147]{0:T(256)S(1)} %concatenate.17.refs_0_, f32[32,16,128]{2,1,0:T(8,128)S(1)} %collective-permute-done.12.refs_1_, f32[32,16,128]{2,1,0:T(8,128)S(1)} %shard_map.72.refs_2_, f32[32,16,128]{2,1,0:T(8,128)S(1)} %collective-permute-done.13.refs_3_, ...), custom_call_target="tpu_custom_call" | custom-call | flops 75497472 | bytes 8388608 | tf_op jit(solution)/shard_map/pallas_call | solution.py:38
  98.9 17.2 %all_to_all.29.parts_ref = f32[8,4,16,128]{3,2,1,0:T(8,128)S(1)} all-to-all(f32[8,4,16,128]{3,2,1,0:T(8,128)S(1)} %bitcast.34), channel_id=1, replica_groups=mesh['q'=64,'xh'=2,'xl'=2,'core'=2] {'xh','xl','core'}, dimensions={0} | all-to-all | bytes 524288 | tf_op jit(solution)/shard_map/all_to_all | solution.py:265
  116.5 16.0 %all_to_all.30 = f32[64,2,128]{2,1,0:T(2,128)S(1)} all-to-all(f32[64,2,128]{2,1,0:T(2,128)S(1)} %bitcast.37), channel_id=1, replica_groups=mesh['q'=64,'xh'=2,'xl'=2,'core'=2] {'q'}, dimensions={0} | all-to-all | bytes 131072 | tf_op jit(solution)/shard_map/all_to_all | solution.py:265
  132.6 9.4 %all_to_all.31 = f32[8,2,128]{2,1,0:T(2,128)S(1)} all-to-all(f32[8,2,128]{2,1,0:T(2,128)S(1)} %broadcast_in_dim.47), channel_id=1, replica_groups=mesh['q'=64,'xh'=2,'xl'=2,'core'=2] {'xh','xl','core'}, dimensions={0} | all-to-all | bytes 16384 | tf_op jit(solution)/shard_map/all_to_all | solution.py:265
  142.0 15.0 %all_to_all.32 = f32[64,2,128]{2,1,0:T(2,128)S(1)} all-to-all(f32[64,2,128]{2,1,0:T(2,128)S(1)} %broadcast_in_dim.48), channel_id=1, replica_groups=mesh['q'=64,'xh'=2,'xl'=2,'core'=2] {'q'}, dimensions={0} | all-to-all | bytes 131072 | tf_op jit(solution)/shard_map/all_to_all | solution.py:265
  157.0 8.1 %shard_map.75 = (f32[128,128]{1,0:T(8,128)}, f32[128,512]{1,0:T(8,128)S(1)}) custom-call(f32[128,128]{1,0:T(8,128)S(1)} %bitcast.36, f32[128,512]{1,0:T(8,128)S(1)} %get-tuple-element.13.all_ref), custom_call_target="tpu_custom_call" | custom-call | flops 100663296 | bytes 1048576 | tf_op jit(solution)/shard_map/pallas_call | solution.py:38
  165.1 9.1 %all_to_all.33 = f32[4,32,512]{2,1,0:T(8,128)S(1)} all-to-all(f32[4,32,512]{2,1,0:T(8,128)S(1)} %bitcast.35), channel_id=1, replica_groups=mesh['q'=64,'xh'=2,'xl'=2,'core'=2] {'xl','core'}, dimensions={0} | all-to-all | bytes 524288 | tf_op jit(solution)/shard_map/all_to_all | solution.py:265
  (45 shorter events, 4.6 us)
Async XLA Ops:
  0.6 32.9 %copy-start.5 = (s32[24]{0:T(128)S(1)}, s32[24]{0:T(128)}, u32[]{:S(2)}) copy-start(s32[24]{0:T(128)} %param.8) | copy-start | bytes 292
  0.6 32.9 %copy-start.6 = (s32[24]{0:T(128)S(1)}, s32[24]{0:T(128)}, u32[]{:S(2)}) copy-start(s32[24]{0:T(128)} %param.7) | copy-start | bytes 292
  0.7 41.1 %copy-start.1 = (f32[32,2048]{1,0:T(8,128)S(1)}, f32[32,2048]{1,0:T(8,128)}, u32[]{:S(2)}) copy-start(f32[32,2048]{1,0:T(8,128)} %refs_2_.1) | copy-start | bytes 786436
  2.5 31.1 %collective-permute-start.7 = (f32[6,128,128]{2,1,0:T(8,128)}, f32[6,128,128]{2,1,0:T(8,128)S(1)}, u32[]{:S(2)}, u32[]{:S(2)}) collective-permute-start(f32[6,128,128]{2,1,0:T(8,128)} %constant_dynamic-slice_fusion), channel_id=1, source_target_pairs={{0,6},{2,4},{4,2},{6,0},{1,7},{3,5},{5,3},{7,1},{8,14},{10,12},{12... | collective-permute-start | bytes 1179656 | tf_op jit(solution)/shard_map/ppermute | solution.py:294
  7.7 28.0 %collective-permute-start.2 = (f32[32,2048]{1,0:T(8,128)}, f32[32,2048]{1,0:T(8,128)S(1)}, u32[]{:S(2)}, u32[]{:S(2)}) collective-permute-start(f32[32,2048]{1,0:T(8,128)} %refs_2_.1), channel_id=1, source_target_pairs={{0,4},{4,0},{1,5},{5,1},{2,6},{6,2},{3,7},{7,3},{8,12},{12,8},{9,1... | collective-permute-start | bytes 786440 | tf_op jit(solution)/shard_map/ppermute | solution.py:261
  10.1 25.5 %collective-permute-start.1 = (f32[32,2048]{1,0:T(8,128)}, f32[32,2048]{1,0:T(8,128)S(1)}, u32[]{:S(2)}, u32[]{:S(2)}) collective-permute-start(f32[32,2048]{1,0:T(8,128)} %refs_2_.1), channel_id=1, source_target_pairs={{0,504},{1,9},{8,0},{9,17},{16,8},{17,25},{24,16},{25,33},{32,24},... | collective-permute-start | bytes 786440 | tf_op jit(solution)/shard_map/ppermute | solution.py:285
  14.1 21.5 %collective-permute-start = (f32[32,2048]{1,0:T(8,128)}, f32[32,2048]{1,0:T(8,128)S(1)}, u32[]{:S(2)}, u32[]{:S(2)}) collective-permute-start(f32[32,2048]{1,0:T(8,128)} %refs_2_.1), channel_id=1, source_target_pairs={{0,8},{1,505},{8,16},{9,1},{16,24},{17,9},{24,32},{25,17},{32,40},... | collective-permute-start | bytes 786440 | tf_op jit(solution)/shard_map/ppermute | solution.py:284
  25.6 16.2 %collective-permute-start.3 = (f32[32,2048]{1,0:T(8,128)}, f32[32,2048]{1,0:T(8,128)S(1)}, u32[]{:S(2)}, u32[]{:S(2)}) collective-permute-start(f32[32,2048]{1,0:T(8,128)} %refs_2_.1), channel_id=1, source_target_pairs={{0,508},{4,8},{8,4},{12,16},{16,12},{20,24},{24,20},{28,32},{32,28... | collective-permute-start | bytes 786440 | tf_op jit(solution)/shard_map/ppermute | solution.py:290
  31.2 1.4 copy-start
  33.6 12.1 %collective-permute-start.8 = (f32[6,128,128]{2,1,0:T(8,128)S(1)}, f32[6,128,128]{2,1,0:T(8,128)S(1)}, u32[]{:S(2)}, u32[]{:S(2)}) collective-permute-start(f32[6,128,128]{2,1,0:T(8,128)S(1)} %collective-permute-done.7), channel_id=1, source_target_pairs={{0,2},{2,0},{1,3},{3,1},{4,6},{6,4},{5,7},{7,5},{8,10},{10,8},{9,1... | collective-permute-start | bytes 1179656 | tf_op jit(solution)/shard_map/ppermute | solution.py:261
  43.7 2.0 %copy-start.2 = (f32[32,16,128]{2,1,0:T(8,128)}, f32[32,16,128]{2,1,0:T(8,128)S(1)}, u32[]{:S(2)}) copy-start(f32[32,16,128]{2,1,0:T(8,128)S(1)} %get-tuple-element.11.refs_4_) | copy-start | bytes 786436
  43.7 7.9 %collective-permute-start.4 = (f32[17,16,128]{2,1,0:T(8,128)}, f32[17,16,128]{2,1,0:T(8,128)S(1)}, u32[]{:S(2)}, u32[]{:S(2)}) collective-permute-start(f32[17,16,128]{2,1,0:T(8,128)} %get-tuple-element.9), channel_id=1, source_target_pairs={{0,4},{4,0},{1,5},{5,1},{2,6},{6,2},{3,7},{7,3},{8,12},{12,8},{9,1... | collective-permute-start | bytes 417800 | tf_op jit(solution)/shard_map/ppermute | solution.py:261
  45.7 17.0 %collective-permute-start.9 = (f32[12,128,128]{2,1,0:T(8,128)S(1)}, f32[12,128,128]{2,1,0:T(8,128)S(1)}, u32[]{:S(2)}, u32[]{:S(2)}) collective-permute-start(f32[12,128,128]{2,1,0:T(8,128)S(1)} %constant_dynamic-update-slice_fusion.refs_0_), channel_id=1, source_target_pairs={{0,1},{1,0},{2,3},{3,2},{4,5},{5,4},{6,7},{7,6},{8,9},{9,8},{10,11... | collective-permute-start | bytes 2359304 | tf_op jit(solution)/shard_map/ppermute | solution.py:261
  51.6 0.7 copy-start.4
  52.3 10.7 %collective-permute-start.6 = (f32[32,16,128]{2,1,0:T(8,128)S(1)}, f32[32,16,128]{2,1,0:T(8,128)}, u32[]{:S(2)}, u32[]{:S(2)}) collective-permute-start(f32[32,16,128]{2,1,0:T(8,128)S(1)} %pad_maximum_fusion.refs_2_.refs_4_), channel_id=1, source_target_pairs={{0,504},{1,9},{8,0},{9,17},{16,8},{17,25},{24,16},{25,33},{32,24},... | collective-permute-start | bytes 786440 | tf_op jit(solution)/shard_map/ppermute | solution.py:285
  54.2 11.5 %collective-permute-start.5 = (f32[32,16,128]{2,1,0:T(8,128)S(1)}, f32[32,16,128]{2,1,0:T(8,128)}, u32[]{:S(2)}, u32[]{:S(2)}) collective-permute-start(f32[32,16,128]{2,1,0:T(8,128)S(1)} %pad_maximum_fusion.refs_2_.refs_4_), channel_id=1, source_target_pairs={{0,8},{1,505},{8,16},{9,1},{16,24},{17,9},{24,32},{25,17},{32,40},... | collective-permute-start | bytes 786440 | tf_op jit(solution)/shard_map/ppermute | solution.py:284
  62.8 3.0 %copy-start.3 = (f32[32,16,128]{2,1,0:T(8,128)S(1)}, f32[32,16,128]{2,1,0:T(8,128)}, u32[]{:S(2)}) copy-start(f32[32,16,128]{2,1,0:T(8,128)} %copy-done.2) | copy-start | bytes 786436
  68.0 11.5 %collective-permute-start.11 = (f32[32,16,128]{2,1,0:T(8,128)S(1)}, f32[32,16,128]{2,1,0:T(8,128)S(1)}, u32[]{:S(2)}, u32[]{:S(2)}) collective-permute-start(f32[32,16,128]{2,1,0:T(8,128)S(1)} %shard_map.71.refs_2_.refs_4_), channel_id=1, source_target_pairs={{0,504},{1,9},{8,0},{9,17},{16,8},{17,25},{24,16},{25,33},{32,24},... | collective-permute-start | bytes 786440 | tf_op jit(solution)/shard_map/ppermute | solution.py:285
  69.9 11.8 %collective-permute-start.10 = (f32[32,16,128]{2,1,0:T(8,128)S(1)}, f32[32,16,128]{2,1,0:T(8,128)S(1)}, u32[]{:S(2)}, u32[]{:S(2)}) collective-permute-start(f32[32,16,128]{2,1,0:T(8,128)S(1)} %shard_map.71.refs_2_.refs_4_), channel_id=1, source_target_pairs={{0,8},{1,505},{8,16},{9,1},{16,24},{17,9},{24,32},{25,17},{32,40},... | collective-permute-start | bytes 786440 | tf_op jit(solution)/shard_map/ppermute | solution.py:284
  83.5 11.4 %collective-permute-start.13 = (f32[32,16,128]{2,1,0:T(8,128)S(1)}, f32[32,16,128]{2,1,0:T(8,128)S(1)}, u32[]{:S(2)}, u32[]{:S(2)}) collective-permute-start(f32[32,16,128]{2,1,0:T(8,128)S(1)} %shard_map.72.refs_2_), channel_id=1, source_target_pairs={{0,504},{1,9},{8,0},{9,17},{16,8},{17,25},{24,16},{25,33},{32,24},... | collective-permute-start | bytes 786440 | tf_op jit(solution)/shard_map/ppermute | solution.py:285
  85.5 11.6 %collective-permute-start.12 = (f32[32,16,128]{2,1,0:T(8,128)S(1)}, f32[32,16,128]{2,1,0:T(8,128)S(1)}, u32[]{:S(2)}, u32[]{:S(2)}) collective-permute-start(f32[32,16,128]{2,1,0:T(8,128)S(1)} %shard_map.72.refs_2_), channel_id=1, source_target_pairs={{0,8},{1,505},{8,16},{9,1},{16,24},{17,9},{24,32},{25,17},{32,40},... | collective-permute-start | bytes 786440 | tf_op jit(solution)/shard_map/ppermute | solution.py:284

commit v4 on v3

--- a/solution.py
+++ b/solution.py
@@ -52,7 +52,7 @@
     base = 0
     for piece in pieces:
         def body(slot, carry, piece=piece, base=base):
-            high, low = split_bf16(piece[slot])
+            high, low = split_bf16(piece[slot].T)
             out_ref[base + slot, 0] = high
             out_ref[base + slot, 1] = low
             return carry
@@ -82,50 +82,108 @@
     )
 
 
-def step_kernel(last, *refs):
-    table, low_ref, mid_ref, high_ref, prev_ref, own_ref, other_ref, out_ref, window, total = refs
-    for piece, ref in enumerate((low_ref, mid_ref, high_ref)):
-        def fill(block, carry, piece=piece, ref=ref):
-            high, low = split_bf16(ref[block])
-            window[piece * HALF + block, 0:COLS] = high
-            window[piece * HALF + block, COLS : 2 * COLS] = low
-            return carry
-
-        lax.fori_loop(0, HALF, fill, 0, unroll=8)
-    total[...] = jnp.zeros_like(total)
+def list_kernel(count_q, ids, own_rows, own_cols, own_count, notes, lists):
+    q, xh, c = ids[0], ids[1], ids[2]
+    quarter = TILE_CAP // 4
+    for which in range(6):
+        lists[6 * TILE_CAP + which] = 0
+    lists[6 * TILE_CAP + 6] = xh * RB_DEV
+
+    def add(which, row, column, place):
+        owner = column >> 4
+        step = lax.rem((owner >> 1) - q + 1 + count_q, count_q)
+        near = (step == 2) == ((q & 1) == 0)
+        piece = jnp.where(step == 1, 0, jnp.where(near, 1, 2))
+        local = ((owner & 1) ^ xh) * RB_DEV + (column & (RB_DEV - 1))
+        target = piece * 2 + which
+        fill = lists[6 * TILE_CAP + target]
+        lists[target * TILE_CAP + fill] = row + HALF * local + HALF * HALF * place
+        lists[6 * TILE_CAP + target] = fill + 1
+
+    def own(slot, carry):
+        add(0, own_rows[slot] & (RB_DEV - 1), own_cols[slot], slot)
+        return carry
+
+    def partner(slot, carry):
+        row = (notes[0, slot].astype(jnp.int32) & (RB_DEV - 1)) + RB_DEV
+        part = lax.div(slot, quarter)
+        order = part ^ c
+        order = (order & 1) * 2 + 1 - (order >> 1)
+        place = order * quarter + slot - part * quarter
+        add(1, row, notes[1, slot].astype(jnp.int32), place)
+        return carry
+
+    lax.fori_loop(0, own_count[0], own, 0)
+    lax.fori_loop(0, notes[2, 0].astype(jnp.int32), partner, 0)
+
+
+def part_kernel(piece, final, *refs):
+    lists, source_ref, *middle, own_ref, other_ref, out_ref, window, total = refs
+
+    def fill(block, carry):
+        high, low = split_bf16(source_ref[block])
+        window[block, 0:COLS] = high
+        window[block, COLS : 2 * COLS] = low
+        return carry
+
+    lax.fori_loop(0, HALF, fill, 0, unroll=8)
+    if piece == 0:
+        total[...] = jnp.zeros_like(total)
+    else:
+        total[...] = middle[0][...]
     for which, tiles in enumerate((own_ref, other_ref)):
-        base = which * 3 * TILE_CAP
-        live = table[6 * TILE_CAP + which]
+        base = (piece * 2 + which) * TILE_CAP
+        live = lists[6 * TILE_CAP + piece * 2 + which]
 
         def body(group, carry, base=base, tiles=tiles, live=live):
-            terms = []
+            terms, rows = [], []
             for inner in range(UNROLL):
                 slot = group * UNROLL + inner
-                column = table[base + TILE_CAP + slot]
-                place = table[base + 2 * TILE_CAP + slot]
-                both = window[column]
-                wide = dot_t(both, tiles[place, 0])
-                narrow = dot_t(both[:COLS], tiles[place, 1])
+                entry = jnp.where(slot < live, lists[base + slot], 0)
+                both = window[(entry // HALF) % HALF]
+                place = entry // (HALF * HALF)
+                wide = dot_b(both, tiles[place, 0])
+                narrow = dot_b(both[:COLS], tiles[place, 1])
                 term = wide[:COLS] + (wide[COLS:] + narrow)
                 terms.append(jnp.where(slot < live, term, jnp.zeros_like(term)))
+                rows.append(entry % HALF)
             for inner in range(UNROLL):
-                row = table[base + group * UNROLL + inner]
-                total[row] = total[row] + terms[inner]
+                total[rows[inner]] = total[rows[inner]] + terms[inner]
             return carry
 
         lax.fori_loop(0, (live + UNROLL - 1) // UNROLL, body, 0)
-    swap = table[6 * TILE_CAP + 2] if last else 0
+    if piece < 2:
+        out_ref[...] = total[...]
+        return
+    prev_ref = middle[1]
+    swap = lists[6 * TILE_CAP + 6] if final else 0
 
     def finish(block, carry):
-        source = block ^ swap if last else block
+        source = block ^ swap if final else block
         out_ref[block] = 2.0 * total[source] - prev_ref[source]
         return carry
 
     lax.fori_loop(0, HALF, finish, 0, unroll=8)
 
 
-def first_kernel(*refs):
-    table, notes_ref, *pieces, tiles, mine_ref, given_ref, start_ref, window, total = refs
+def dot_b(left, right):
+    return lax.dot_general(
+        left, right, (((1,), (0,)), ((), ())), preferred_element_type=jnp.float32
+    )
+
+
+def first_kernel(count_b, *refs):
+    ids, rows, cols, count, notes_ref, *refs = refs
+    *pieces, tiles, mine_ref, given_ref, start_ref, window, total = refs
+    q, xh = ids[0], ids[1]
+
+    def place_of(column):
+        offset = lax.rem((column >> 4) - 2 * q - xh + REACH + count_b, count_b)
+        side = jnp.where((q & 1) == 0, 2 * REACH - offset, offset)
+        place = jnp.where((offset & 1) == 1, jnp.where((offset == 3) == (xh == 0), 3, 4), 0)
+        place = jnp.where(side == 0, 1, jnp.where(side == 4, 2, place))
+        return place * RB_DEV + (column & (RB_DEV - 1))
+
     wide_cols = 2 * COLS
     for piece, ref in enumerate(pieces):
         for block in range(RB_DEV):
@@ -133,20 +191,21 @@
             window[piece * RB_DEV + block, 0:wide_cols] = high
             window[piece * RB_DEV + block, wide_cols : 2 * wide_cols] = low
     total[...] = jnp.zeros_like(total)
-    live = table[2 * TILE_CAP]
-    upper = table[2 * TILE_CAP + 1] == 1
+    live = count[0]
+    upper = xh == 1
 
     def body(group, carry):
         terms = []
         for inner in range(UNROLL):
             slot = group * UNROLL + inner
-            both = window[table[TILE_CAP + slot]]
-            wide = dot_t(both, tiles[slot, 0])
-            narrow = dot_t(both[:wide_cols], tiles[slot, 1])
+            both = window[place_of(cols[slot])]
+            high, low = split_bf16(tiles[slot])
+            wide = dot_t(both, high)
+            narrow = dot_t(both[:wide_cols], low)
             term = wide[:wide_cols] + (wide[wide_cols:] + narrow)
             terms.append(jnp.where(slot < live, term, jnp.zeros_like(term)))
         for inner in range(UNROLL):
-            row = table[group * UNROLL + inner]
+            row = rows[group * UNROLL + inner] & (RB_DEV - 1)
             total[row] = total[row] + terms[inner]
         return carry
 
@@ -161,19 +220,19 @@
     given_ref[RB_DEV] = notes_ref[...]
 
 
-def graph_step(table, parts, prev, own_tiles, other_tiles, last):
-    operands = [table, *parts, prev, own_tiles, other_tiles]
+def graph_part(lists, piece, source, middle, own_tiles, other_tiles, final):
+    operands = [lists, source, *middle, own_tiles, other_tiles]
     return call(
-        functools.partial(step_kernel, last),
+        functools.partial(part_kernel, piece, final),
         jax.ShapeDtypeStruct((HALF, COLS, BS), jnp.float32),
         operands,
         [SMEM] + [VMEM] * (len(operands) - 1),
         scratch=[
-            pltpu.VMEM((3 * HALF, 2 * COLS, BS), jnp.bfloat16),
+            pltpu.VMEM((HALF, 2 * COLS, BS), jnp.bfloat16),
             pltpu.VMEM((HALF, COLS, BS), jnp.float32),
         ],
-        flops=2 * TILE_CAP * 6 * COLS * BS * BS,
-        moved=8 << 20,
+        flops=2 * TILE_CAP * 2 * COLS * BS * BS,
+        moved=4 << 20,
     )
 
 
@@ -232,7 +291,8 @@
     return value
 
 
-def factor_kernel(scale, gram_ref, all_ref, factor_ref, ortho_ref, work):
+def factor_kernel(scale, place_ref, gram_ref, *refs):
+    *slices, factor_ref, ortho_ref, work = refs
     row = lax.broadcasted_iota(jnp.int32, (K, K), 0)
     lane = lax.broadcasted_iota(jnp.int32, (K, K), 1)
     work[:, :K] = gram_ref[...]
@@ -254,7 +314,19 @@
             change = dot_n(ups[:, :K].T, ups)
             work[below:, :] = work[below:, :] - change[below:]
     factor_ref[...] = (jnp.where(lane >= row, work[:, :K], 0.0) / scale).T
-    ortho_ref[...] = dot_n(work[:, K:] * scale, all_ref[...])
+    own = place_ref[0]
+    count = K // 4
+    inverse = work[pl.ds(pl.multiple_of(own * count, count), count), K:] * scale
+    width = 4 * BS
+    mine, second, pair = slices
+    for other, value in (
+        (0, mine[...]),
+        (2, second[...]),
+        (1, pair[:K]),
+        (3, pair[K:]),
+    ):
+        start = pl.multiple_of((own ^ other) * width, width)
+        ortho_ref[:, pl.ds(start, width)] = dot_n(inverse, value)
 
 
 def exchange(value, axis):
@@ -273,16 +345,12 @@
     c = lax.axis_index("xl") * 2 + core
     quarter = TILE_CAP // 4
 
-    def pairs(shift):
-        return [
-            (2 * i + k, 2 * ((i + (shift if k == 0 else -shift)) % count_q) + k)
-            for i in range(count_q)
-            for k in range(2)
-        ]
+    even = [(i, i ^ 1) for i in range(count_q)]
+    odd = [(i, (i + 1 if i % 2 else i - 1) % count_q) for i in range(count_q)]
 
     def halo(value):
-        one = lax.ppermute(value, ("q", "core"), pairs(1))
-        two = lax.ppermute(value, ("q", "core"), pairs(-1))
+        one = lax.ppermute(value, "q", even)
+        two = lax.ppermute(value, "q", odd)
         return one, two
 
     count = 2 * count_q
@@ -298,12 +366,7 @@
     own_tiles = split_tiles([tile_values])
     other_tiles = split_tiles([pair, far])
 
-    offset = (tile_cols // RB_DEV - 2 * q - xh + REACH + count) % count
-    side = jnp.where(core == 1, 2 * REACH - offset, offset)
-    place = jnp.where(offset % 2 == 1, jnp.where((offset == 3) == (xh == 0), 3, 4), 0)
-    place = jnp.where(side == 0, 1, jnp.where(side == 4, 2, place))
-    place = place * RB_DEV + tile_cols % RB_DEV
-    own_table = jnp.concatenate([tile_rows % RB_DEV, place, tile_counts, xh[None]])
+    ids = jnp.stack([q, xh, c])
     notes = jnp.concatenate(
         [
             tile_rows.astype(jnp.float32)[None],
@@ -315,14 +378,17 @@
     notes = jnp.pad(notes, ((0, COLS - 3), (0, BS - TILE_CAP)))
     half = jax.ShapeDtypeStruct((RB_DEV, COLS, BS), jnp.float32)
     mine, given, previous = call(
-        first_kernel,
+        functools.partial(first_kernel, count),
         (
             half,
             jax.ShapeDtypeStruct((RB_DEV + 1, COLS, BS), jnp.float32),
             jax.ShapeDtypeStruct((HALF, COLS, BS), jnp.float32),
         ),
-        [own_table, notes, start_panel, one, two, across, diagonal, own_tiles],
-        [SMEM] + [VMEM] * 7,
+        [
+            ids, tile_rows, tile_cols, tile_counts,
+            notes, start_panel, one, two, across, diagonal, tile_values,
+        ],
+        [SMEM] * 4 + [VMEM] * 7,
         scratch=[
             pltpu.VMEM((5 * RB_DEV, 4 * COLS, BS), jnp.bfloat16),
             pltpu.VMEM((RB_DEV, 2 * COLS, BS), jnp.float32),
@@ -332,41 +398,21 @@
     )
     got = exchange(given, "xh")
     current = jnp.concatenate([mine, got[:RB_DEV]], axis=0)
-    other = jnp.round(got[RB_DEV, :3, :TILE_CAP]).astype(jnp.int32)
-
-    slots = jnp.arange(TILE_CAP, dtype=jnp.int32)
-
-    def window_place(cols):
-        owner = cols // RB_DEV
-        step = (owner // 2 - q + 1 + count_q) % count_q
-        step = jnp.where(core == 1, 2 - step, step)
-        place = step * HALF + ((owner % 2) ^ xh) * RB_DEV + cols % RB_DEV
-        return jnp.clip(place, 0, 3 * HALF - 1)
-
-    def row_place(rows, base):
-        return jnp.clip(rows % RB_DEV, 0, RB_DEV - 1) + base
-
-    order = (slots // quarter) ^ c
-    order = (order % 2) * 2 + 1 - order // 2
-    table = jnp.concatenate(
-        [
-            row_place(tile_rows, 0),
-            window_place(tile_cols),
-            slots,
-            row_place(other[0], RB_DEV),
-            window_place(other[1]),
-            order * quarter + slots % quarter,
-            tile_counts,
-            other[2, :1],
-            (xh * RB_DEV)[None],
-        ]
-    )
-
+    lists = pl.pallas_call(
+        functools.partial(list_kernel, count_q),
+        out_shape=jax.ShapeDtypeStruct((6 * TILE_CAP + 7,), jnp.int32),
+        in_specs=[SMEM] * 5,
+        out_specs=SMEM,
+        interpret=INTERPRET,
+        name="lists",
+    )(ids, tile_rows, tile_cols, tile_counts, got[RB_DEV, :3, :TILE_CAP])
     for step in range(1, DEGREE):
-        lower, higher = halo(current)
-        upcoming = graph_step(
-            table, (lower, current, higher), previous, own_tiles, other_tiles, step == DEGREE - 1
-        )
+        one, two = halo(current)
+        final = step == DEGREE - 1
+        tiles = (own_tiles, other_tiles, final)
+        part = graph_part(lists, 0, current, (), *tiles)
+        part = graph_part(lists, 1, one, (part,), *tiles)
+        upcoming = graph_part(lists, 2, two, (part, previous), *tiles)
         previous, current = current, upcoming
 
     parts = to_all(current.reshape(8, 4, COLS, BS), GROUP)
@@ -381,26 +427,26 @@
         flops=2 * K * K * 4 * BS * 6,
         moved=1 << 20,
     )
+    second = exchange(everything, "xl")
+    far_slices = exchange(jnp.concatenate([everything, second], axis=0), "core")
     rows = K // count_q if K >= count_q else 1
     spread = to_all(gram, "q").reshape(count_q, rows, K).sum(axis=0)
     spread = to_all(jnp.broadcast_to(spread[None], (8, rows, K)), GROUP).sum(axis=0)
     gram = to_all(jnp.broadcast_to(spread[None], (count_q, rows, K)), "q").reshape(K, K)
 
     total_rows = start_panel.shape[1] * count_q * 2
-    factor, ortho = call(
+    factor, ortho_panel = call(
         functools.partial(factor_kernel, math.sqrt(total_rows)),
         (
             jax.ShapeDtypeStruct((K, K), jnp.float32),
-            jax.ShapeDtypeStruct((K, 4 * BS), jnp.float32),
+            jax.ShapeDtypeStruct((K // 4, 16 * BS), jnp.float32),
         ),
-        [gram, everything],
-        [VMEM, VMEM],
+        [c[None], gram, everything, second, far_slices],
+        [SMEM] + [VMEM] * 4,
         scratch=[pltpu.VMEM((K, 2 * K), jnp.float32)],
         flops=2 * K * K * 4 * BS * 6,
         moved=1 << 20,
     )
-    ortho = to_all(ortho.reshape(4, K // 4, 4 * BS), COL)
-    ortho_panel = ortho.transpose(1, 0, 2).reshape(K // 4, 16 * BS)
     return (ortho_panel, factor)
 
 

time: 176 us -> 184 us (1.045)
  blocking collectives: 66.7 us -> 54 us
  waiting for transfers between devices: 16.9 us -> 28.1 us
  Pallas kernels: 16.7 us -> 25.8 us
    all_to_all x5 -> x4, blocking collectives: 66.7 us -> 54 us  [to_all(): return lax.all_to_all(value, axis, 0, 0, tiled=True)]
    ppermute x4 -> x6, waiting for transfers between devices: 0.01 us -> 11.9 us  [exchange(): return lax.ppermute(value, axis, [(0, 1), (1, 0)])]
    ppermute x4 -> x6, starting transfers between devices: 12 us -> 23.5 us  [exchange(): return lax.ppermute(value, axis, [(0, 1), (1, 0)])]
    pallas_call x8 -> x14, Pallas kernels: 16.7 us -> 24.2 us  [call(): pl.pallas_call(kernel, out_shape=out_shape, in_specs=specs, out_specs=out...]
    ppermute x8, starting transfers between devices: 43.3 us -> 36.8 us  [the longest x4 25.7 us: halo(): two = lax.ppermute(value, 'q', odd)]
    ppermute x1, waiting for transfers between devices: 0.01 us -> 5.26 us  [filtered_basis(): first = lax.ppermute(piece, ('xh', 'xl'), [(i, 3 - i) for i in range(4)])]
    ppermute x1, waiting for transfers between devices: 6.11 us -> 1.43 us  [filtered_basis(): diagonal = lax.ppermute(start_panel, ('q', 'xh'), near)]
    ppermute x1, starting transfers between devices: 5.53 us -> 1.92 us  [filtered_basis(): diagonal = lax.ppermute(start_panel, ('q', 'xh'), near)]
  transfers between devices with their start and end apart: 14 -> 16, of which waited for: 6 -> 8; matrix products, arithmetic and copies ran while one was open for 1% -> 3% of each run, Pallas kernels for 1% -> 7%
where the time goes in v4:
time: 184 us; the launch traced here: 183 us
  starting transfers between devices  67.4 us (37%)
  blocking collectives  54 us (29%)
  waiting for transfers between devices  28.1 us (15%)
  Pallas kernels  25.8 us (14%)
  local copies, waits for them, and re-layouts  5.44 us (3%)
    all_to_all x4, blocking collectives, to_all(): return lax.all_to_all(value, axis, 0, 0, tiled=True)  54 us
    ppermute x4, starting transfers between devices, halo(): two = lax.ppermute(value, 'q', odd)  25.7 us
    pallas_call x14, Pallas kernels, call(): pl.pallas_call(kernel, out_shape=out_shape, in_specs=specs, out_specs=out...  24.2 us
    ppermute x6, starting transfers between devices, exchange(): return lax.ppermute(value, axis, [(0, 1), (1, 0)])  23.5 us
    ppermute x6, waiting for transfers between devices, exchange(): return lax.ppermute(value, axis, [(0, 1), (1, 0)])  11.9 us
    ppermute x4, starting transfers between devices, halo(): one = lax.ppermute(value, 'q', even)  11.1 us
    ppermute x4, waiting for transfers between devices, halo(): two = lax.ppermute(value, 'q', odd)  7.57 us
    ppermute x1, waiting for transfers between devices, filtered_basis(): first = lax.ppermute(piece, ('xh', 'xl'), [(i, 3 - i) for i in range(4)])  5.26 us
  transfers between devices with their start and end apart: 16, of which 8 were waited for; matrix products, arithmetic and copies ran while one was open for 3% of the time, Pallas kernels for 7%

profile of v4, /device:TPU:1, one launch (start us, length us, event | category | flops | bytes accessed | tf_op | source)
XLA Modules:
  0.0 183.4 jit_solution(7415786113839600675)
XLA Ops:
  1.8 5.2 %collective-permute-start.7 = (f32[6,128,128]{2,1,0:T(8,128)S(1)}, f32[6,128,128]{2,1,0:T(8,128)}, u32[]{:S(2)}, u32[]{:S(2)}) collective-permute-start(f32[6,128,128]{2,1,0:T(8,128)S(1)} %constant_dynamic-slice_fusion), channel_id=1, source_target_pairs={{0,6},{2,4},{4,2},{6,0},{1,7},{3,5},{5,3},{7,1},{8,14},{10,12},{12... | collective-permute-start | bytes 1179656 | tf_op jit(solution)/shard_map/ppermute | solution.py:362
  7.0 5.3 %collective-permute-done.7 = f32[6,128,128]{2,1,0:T(8,128)} collective-permute-done((f32[6,128,128]{2,1,0:T(8,128)S(1)}, f32[6,128,128]{2,1,0:T(8,128)}, u32[]{:S(2)}, u32[]{:S(2)}) %collective-permute-start.7) | collective-permute-done | bytes 393248 | tf_op jit(solution)/shard_map/ppermute | solution.py:362
  12.3 5.5 %collective-permute-start.8 = (f32[6,128,128]{2,1,0:T(8,128)}, f32[6,128,128]{2,1,0:T(8,128)}, u32[]{:S(2)}, u32[]{:S(2)}) collective-permute-start(f32[6,128,128]{2,1,0:T(8,128)} %collective-permute-done.7), channel_id=1, source_target_pairs={{0,2},{2,0},{1,3},{3,1},{4,6},{6,4},{5,7},{7,5},{8,10},{10,8},{9,1... | collective-permute-start | bytes 1179656 | tf_op jit(solution)/shard_map/ppermute | solution.py:333
  17.8 4.0 %collective-permute-start = (f32[32,2048]{1,0:T(8,128)}, f32[32,2048]{1,0:T(8,128)S(1)}, u32[]{:S(2)}, u32[]{:S(2)}) collective-permute-start(f32[32,2048]{1,0:T(8,128)} %refs_5_.1), channel_id=1, source_target_pairs={{0,8},{8,0},{16,24},{24,16},{32,40},{40,32},{48,56},{56,48},{64,72... | collective-permute-start | bytes 786440 | tf_op jit(solution)/shard_map/ppermute | solution.py:352
  21.8 11.8 %collective-permute-start.1 = (f32[32,2048]{1,0:T(8,128)}, f32[32,2048]{1,0:T(8,128)S(1)}, u32[]{:S(2)}, u32[]{:S(2)}) collective-permute-start(f32[32,2048]{1,0:T(8,128)} %refs_5_.1), channel_id=1, source_target_pairs={{0,504},{8,16},{16,8},{24,32},{32,24},{40,48},{48,40},{56,64},{64,... | collective-permute-start | bytes 786440 | tf_op jit(solution)/shard_map/ppermute | solution.py:353
  33.6 5.6 %collective-permute-start.2 = (f32[32,2048]{1,0:T(8,128)}, f32[32,2048]{1,0:T(8,128)S(1)}, u32[]{:S(2)}, u32[]{:S(2)}) collective-permute-start(f32[32,2048]{1,0:T(8,128)} %refs_5_.1), channel_id=1, source_target_pairs={{0,4},{4,0},{1,5},{5,1},{2,6},{6,2},{3,7},{7,3},{8,12},{12,8},{9,1... | collective-permute-start | bytes 786440 | tf_op jit(solution)/shard_map/ppermute | solution.py:333
  39.1 1.9 %collective-permute-start.3 = (f32[32,2048]{1,0:T(8,128)}, f32[32,2048]{1,0:T(8,128)S(1)}, u32[]{:S(2)}, u32[]{:S(2)}) collective-permute-start(f32[32,2048]{1,0:T(8,128)} %refs_5_.1), channel_id=1, source_target_pairs={{0,508},{4,8},{8,4},{12,16},{16,12},{20,24},{24,20},{28,32},{32,28... | collective-permute-start | bytes 786440 | tf_op jit(solution)/shard_map/ppermute | solution.py:358
  42.5 1.8 constant_dynamic-update-slice_fusion.1
  44.2 1.8 constant_dynamic-update-slice_fusion.refs_0_
  46.0 4.5 %collective-permute-start.9 = (f32[12,128,128]{2,1,0:T(8,128)}, f32[12,128,128]{2,1,0:T(8,128)}, u32[]{:S(2)}, u32[]{:S(2)}) collective-permute-start(f32[12,128,128]{2,1,0:T(8,128)} %constant_dynamic-update-slice_fusion.refs_0_), channel_id=1, source_target_pairs={{0,1},{1,0},{2,3},{3,2},{4,5},{5,4},{6,7},{7,6},{8,9},{9,8},{10,11... | collective-permute-start | bytes 2359304 | tf_op jit(solution)/shard_map/ppermute | solution.py:333
  53.5 1.9 %collective-permute-start.4 = (f32[17,16,128]{2,1,0:T(8,128)S(1)}, f32[17,16,128]{2,1,0:T(8,128)S(1)}, u32[]{:S(2)}, u32[]{:S(2)}) collective-permute-start(f32[17,16,128]{2,1,0:T(8,128)S(1)} %get-tuple-element.9), channel_id=1, source_target_pairs={{0,4},{4,0},{1,5},{5,1},{2,6},{6,2},{3,7},{7,3},{8,12},{12,8},{9,1... | collective-permute-start | bytes 417800 | tf_op jit(solution)/shard_map/ppermute | solution.py:333
  55.4 5.4 %collective-permute-done.4 = f32[17,16,128]{2,1,0:T(8,128)S(1)} collective-permute-done((f32[17,16,128]{2,1,0:T(8,128)S(1)}, f32[17,16,128]{2,1,0:T(8,128)S(1)}, u32[]{:S(2)}, u32[]{:S(2)}) %collective-permute-start.4) | collective-permute-done | bytes 139296 | tf_op jit(solution)/shard_map/ppermute | solution.py:333
  60.9 3.3 %collective-permute-start.6 = (f32[32,16,128]{2,1,0:T(8,128)S(1)}, f32[32,16,128]{2,1,0:T(8,128)}, u32[]{:S(2)}, u32[]{:S(2)}) collective-permute-start(f32[32,16,128]{2,1,0:T(8,128)S(1)} %pad_maximum_fusion.1.refs_1_.refs_3_), channel_id=1, source_target_pairs={{0,8},{8,0},{16,24},{24,16},{32,40},{40,32},{48,56},{56,48},{64,72... | collective-permute-start | bytes 786440 | tf_op jit(solution)/shard_map/ppermute | solution.py:352
  64.1 5.8 %collective-permute-start.5 = (f32[32,16,128]{2,1,0:T(8,128)S(1)}, f32[32,16,128]{2,1,0:T(8,128)}, u32[]{:S(2)}, u32[]{:S(2)}) collective-permute-start(f32[32,16,128]{2,1,0:T(8,128)S(1)} %pad_maximum_fusion.1.refs_1_.refs_3_), channel_id=1, source_target_pairs={{0,504},{8,16},{16,8},{24,32},{32,24},{40,48},{48,40},{56,64},{64,... | collective-permute-start | bytes 786440 | tf_op jit(solution)/shard_map/ppermute | solution.py:353
  71.8 1.6 lists.1.refs_0_
  73.4 2.6 %shard_map.70.refs_3_.refs_4_.refs_5_ = bf16[24,2,128,128]{3,2,1,0:T(8,128)(2,1)S(1)} custom-call(f32[12,128,128]{2,1,0:T(8,128)} %constant_dynamic-update-slice_fusion.refs_0_, f32[12,128,128]{2,1,0:T(8,128)} %collective-permute-done.9.refs_1_), custom_call_target="tpu_custom_call" | custom-call | bytes 3145728 | tf_op jit(solution)/shard_map/pallas_call | solution.py:38
  77.1 1.5 shard_map.72.refs_2_
  78.6 1.4 shard_map.73.refs_1_.refs_3_
  80.1 1.9 %collective-permute-start.11 = (f32[32,16,128]{2,1,0:T(8,128)S(1)}, f32[32,16,128]{2,1,0:T(8,128)S(1)}, u32[]{:S(2)}, u32[]{:S(2)}) collective-permute-start(f32[32,16,128]{2,1,0:T(8,128)S(1)} %shard_map.73.refs_1_.refs_3_), channel_id=1, source_target_pairs={{0,8},{8,0},{16,24},{24,16},{32,40},{40,32},{48,56},{56,48},{64,72... | collective-permute-start | bytes 786440 | tf_op jit(solution)/shard_map/ppermute | solution.py:352
  82.0 4.5 %collective-permute-start.10 = (f32[32,16,128]{2,1,0:T(8,128)S(1)}, f32[32,16,128]{2,1,0:T(8,128)S(1)}, u32[]{:S(2)}, u32[]{:S(2)}) collective-permute-start(f32[32,16,128]{2,1,0:T(8,128)S(1)} %shard_map.73.refs_1_.refs_3_), channel_id=1, source_target_pairs={{0,504},{8,16},{16,8},{24,32},{32,24},{40,48},{48,40},{56,64},{64,... | collective-permute-start | bytes 786440 | tf_op jit(solution)/shard_map/ppermute | solution.py:353
  90.0 3.3 %collective-permute-done.10.refs_1_ = f32[32,16,128]{2,1,0:T(8,128)S(1)} collective-permute-done((f32[32,16,128]{2,1,0:T(8,128)S(1)}, f32[32,16,128]{2,1,0:T(8,128)S(1)}, u32[]{:S(2)}, u32[]{:S(2)}) %collective-permute-start.10) | collective-permute-done | bytes 262176 | tf_op jit(solution)/shard_map/ppermute | solution.py:353
  94.4 1.9 %collective-permute-start.13 = (f32[32,16,128]{2,1,0:T(8,128)S(1)}, f32[32,16,128]{2,1,0:T(8,128)S(1)}, u32[]{:S(2)}, u32[]{:S(2)}) collective-permute-start(f32[32,16,128]{2,1,0:T(8,128)S(1)} %shard_map.76.refs_1_), channel_id=1, source_target_pairs={{0,8},{8,0},{16,24},{24,16},{32,40},{40,32},{48,56},{56,48},{64,72... | collective-permute-start | bytes 786440 | tf_op jit(solution)/shard_map/ppermute | solution.py:352
  96.3 3.6 %collective-permute-start.12 = (f32[32,16,128]{2,1,0:T(8,128)S(1)}, f32[32,16,128]{2,1,0:T(8,128)S(1)}, u32[]{:S(2)}, u32[]{:S(2)}) collective-permute-start(f32[32,16,128]{2,1,0:T(8,128)S(1)} %shard_map.76.refs_1_), channel_id=1, source_target_pairs={{0,504},{8,16},{16,8},{24,32},{32,24},{40,48},{48,40},{56,64},{64,... | collective-permute-start | bytes 786440 | tf_op jit(solution)/shard_map/ppermute | solution.py:353
  102.5 4.2 %collective-permute-done.12.refs_1_ = f32[32,16,128]{2,1,0:T(8,128)S(1)} collective-permute-done((f32[32,16,128]{2,1,0:T(8,128)S(1)}, f32[32,16,128]{2,1,0:T(8,128)S(1)}, u32[]{:S(2)}, u32[]{:S(2)}) %collective-permute-start.12) | collective-permute-done | bytes 262176 | tf_op jit(solution)/shard_map/ppermute | solution.py:353
  107.8 14.6 %all_to_all.24.parts_ref = f32[8,4,16,128]{3,2,1,0:T(8,128)S(1)} all-to-all(f32[8,4,16,128]{3,2,1,0:T(8,128)S(1)} %bitcast.13), channel_id=1, replica_groups=mesh['q'=64,'xh'=2,'xl'=2,'core'=2] {'xh','xl','core'}, dimensions={0} | all-to-all | bytes 524288 | tf_op jit(solution)/shard_map/all_to_all | solution.py:337
  122.8 2.2 %collective-permute-start.14 = (f32[128,512]{1,0:T(8,128)S(1)}, f32[128,512]{1,0:T(8,128)S(1)}, u32[]{:S(2)}, u32[]{:S(2)}) collective-permute-start(f32[128,512]{1,0:T(8,128)S(1)} %get-tuple-element.13.refs_0_), channel_id=1, source_target_pairs={{0,2},{2,0},{1,3},{3,1},{4,6},{6,4},{5,7},{7,5},{8,10},{10,8},{9,1... | collective-permute-start | bytes 786440 | tf_op jit(solution)/shard_map/ppermute | solution.py:333
  125.0 6.5 %collective-permute-done.14.refs_1_ = f32[128,512]{1,0:T(8,128)S(1)} collective-permute-done((f32[128,512]{1,0:T(8,128)S(1)}, f32[128,512]{1,0:T(8,128)S(1)}, u32[]{:S(2)}, u32[]{:S(2)}) %collective-permute-start.14) | collective-permute-done | bytes 262176 | tf_op jit(solution)/shard_map/ppermute | solution.py:333
  131.6 3.8 %collective-permute-start.15 = (f32[256,512]{1,0:T(8,128)S(1)}, f32[256,512]{1,0:T(8,128)S(1)}, u32[]{:S(2)}, u32[]{:S(2)}) collective-permute-start(f32[256,512]{1,0:T(8,128)S(1)} %pad_maximum_fusion), channel_id=1, source_target_pairs={{0,1},{1,0},{2,3},{3,2},{4,5},{5,4},{6,7},{7,6},{8,9},{9,8},{10,11... | collective-permute-start | bytes 1572872 | tf_op jit(solution)/shard_map/ppermute | solution.py:333
  135.4 16.0 %all_to_all.25 = f32[64,2,128]{2,1,0:T(2,128)S(1)} all-to-all(f32[64,2,128]{2,1,0:T(2,128)S(1)} %bitcast.15), channel_id=1, replica_groups=mesh['q'=64,'xh'=2,'xl'=2,'core'=2] {'q'}, dimensions={0} | all-to-all | bytes 131072 | tf_op jit(solution)/shard_map/all_to_all | solution.py:337
  151.4 8.4 %all_to_all.26 = f32[8,2,128]{2,1,0:T(2,128)S(1)} all-to-all(f32[8,2,128]{2,1,0:T(2,128)S(1)} %broadcast_in_dim.34), channel_id=1, replica_groups=mesh['q'=64,'xh'=2,'xl'=2,'core'=2] {'xh','xl','core'}, dimensions={0} | all-to-all | bytes 16384 | tf_op jit(solution)/shard_map/all_to_all | solution.py:337
  159.9 15.0 %all_to_all.27 = f32[64,2,128]{2,1,0:T(2,128)S(1)} all-to-all(f32[64,2,128]{2,1,0:T(2,128)S(1)} %broadcast_in_dim.35), channel_id=1, replica_groups=mesh['q'=64,'xh'=2,'xl'=2,'core'=2] {'q'}, dimensions={0} | all-to-all | bytes 131072 | tf_op jit(solution)/shard_map/all_to_all | solution.py:337
  174.9 8.5 %shard_map.81 = (f32[128,128]{1,0:T(8,128)}, f32[32,2048]{1,0:T(8,128)}) custom-call(s32[1]{0:T(128)} %bitcast.place_ref, f32[128,128]{1,0:T(8,128)S(1)} %bitcast.14, f32[128,512]{1,0:T(8,128)S(1)} %get-tuple-element.13.refs_0_, f32[128,512]{1,0:T(8,128)S(1)} %collective-permute-done.14.refs_1_, f32[256,512]{1,0:T(8,128)S(1)} %collective-permute-done.15.refs_2_), custom_call_target="tpu_custom_call" | custom-call | flops 100663296 | bytes 1048576 | tf_op jit(solution)/shard_map/pallas_call | solution.py:38
  (51 shorter events, 16.4 us)
Async XLA Ops:
  0.6 51.5 %copy-start = (f32[24,128,128]{2,1,0:T(8,128)S(1)}, f32[24,128,128]{2,1,0:T(8,128)}, u32[]{:S(2)}) copy-start(f32[24,128,128]{2,1,0:T(8,128)} %refs_0_.1) | copy-start | bytes 4718596
  0.6 51.5 %copy-start.1 = (f32[32,2048]{1,0:T(8,128)S(1)}, f32[32,2048]{1,0:T(8,128)}, u32[]{:S(2)}) copy-start(f32[32,2048]{1,0:T(8,128)} %refs_5_.1) | copy-start | bytes 786436
  0.7 51.5 %copy-start.5 = (s32[24]{0:T(128)S(1)}, s32[24]{0:T(128)}, u32[]{:S(2)}) copy-start(s32[24]{0:T(128)} %own_rows.1) | copy-start | bytes 292
  0.7 51.5 %copy-start.6 = (s32[24]{0:T(128)S(1)}, s32[24]{0:T(128)}, u32[]{:S(2)}) copy-start(s32[24]{0:T(128)} %own_cols.1) | copy-start | bytes 292
  1.8 10.5 %collective-permute-start.7 = (f32[6,128,128]{2,1,0:T(8,128)S(1)}, f32[6,128,128]{2,1,0:T(8,128)}, u32[]{:S(2)}, u32[]{:S(2)}) collective-permute-start(f32[6,128,128]{2,1,0:T(8,128)S(1)} %constant_dynamic-slice_fusion), channel_id=1, source_target_pairs={{0,6},{2,4},{4,2},{6,0},{1,7},{3,5},{5,3},{7,1},{8,14},{10,12},{12... | collective-permute-start | bytes 1179656 | tf_op jit(solution)/shard_map/ppermute | solution.py:362
  12.3 31.9 %collective-permute-start.8 = (f32[6,128,128]{2,1,0:T(8,128)}, f32[6,128,128]{2,1,0:T(8,128)}, u32[]{:S(2)}, u32[]{:S(2)}) collective-permute-start(f32[6,128,128]{2,1,0:T(8,128)} %collective-permute-done.7), channel_id=1, source_target_pairs={{0,2},{2,0},{1,3},{3,1},{4,6},{6,4},{5,7},{7,5},{8,10},{10,8},{9,1... | collective-permute-start | bytes 1179656 | tf_op jit(solution)/shard_map/ppermute | solution.py:333
  17.8 33.0 %collective-permute-start = (f32[32,2048]{1,0:T(8,128)}, f32[32,2048]{1,0:T(8,128)S(1)}, u32[]{:S(2)}, u32[]{:S(2)}) collective-permute-start(f32[32,2048]{1,0:T(8,128)} %refs_5_.1), channel_id=1, source_target_pairs={{0,8},{8,0},{16,24},{24,16},{32,40},{40,32},{48,56},{56,48},{64,72... | collective-permute-start | bytes 786440 | tf_op jit(solution)/shard_map/ppermute | solution.py:352
  21.8 28.9 %collective-permute-start.1 = (f32[32,2048]{1,0:T(8,128)}, f32[32,2048]{1,0:T(8,128)S(1)}, u32[]{:S(2)}, u32[]{:S(2)}) collective-permute-start(f32[32,2048]{1,0:T(8,128)} %refs_5_.1), channel_id=1, source_target_pairs={{0,504},{8,16},{16,8},{24,32},{32,24},{40,48},{48,40},{56,64},{64,... | collective-permute-start | bytes 786440 | tf_op jit(solution)/shard_map/ppermute | solution.py:353
  33.6 17.2 %collective-permute-start.2 = (f32[32,2048]{1,0:T(8,128)}, f32[32,2048]{1,0:T(8,128)S(1)}, u32[]{:S(2)}, u32[]{:S(2)}) collective-permute-start(f32[32,2048]{1,0:T(8,128)} %refs_5_.1), channel_id=1, source_target_pairs={{0,4},{4,0},{1,5},{5,1},{2,6},{6,2},{3,7},{7,3},{8,12},{12,8},{9,1... | collective-permute-start | bytes 786440 | tf_op jit(solution)/shard_map/ppermute | solution.py:333
  39.1 13.1 %collective-permute-start.3 = (f32[32,2048]{1,0:T(8,128)}, f32[32,2048]{1,0:T(8,128)S(1)}, u32[]{:S(2)}, u32[]{:S(2)}) collective-permute-start(f32[32,2048]{1,0:T(8,128)} %refs_5_.1), channel_id=1, source_target_pairs={{0,508},{4,8},{8,4},{12,16},{16,12},{20,24},{24,20},{28,32},{32,28... | collective-permute-start | bytes 786440 | tf_op jit(solution)/shard_map/ppermute | solution.py:358
  46.0 27.4 %collective-permute-start.9 = (f32[12,128,128]{2,1,0:T(8,128)}, f32[12,128,128]{2,1,0:T(8,128)}, u32[]{:S(2)}, u32[]{:S(2)}) collective-permute-start(f32[12,128,128]{2,1,0:T(8,128)} %constant_dynamic-update-slice_fusion.refs_0_), channel_id=1, source_target_pairs={{0,1},{1,0},{2,3},{3,2},{4,5},{5,4},{6,7},{7,6},{8,9},{9,8},{10,11... | collective-permute-start | bytes 2359304 | tf_op jit(solution)/shard_map/ppermute | solution.py:333
  50.7 10.1 %copy-start.7 = (s32[3]{0:T(128)}, s32[3]{0:T(128)S(1)}, u32[]{:S(2)}) copy-start(s32[3]{0:T(128)S(1)} %pad_add_fusion.refs_0_.ids) | copy-start | bytes 40
  53.5 10.7 %copy-start.2 = (f32[32,16,128]{2,1,0:T(8,128)}, f32[32,16,128]{2,1,0:T(8,128)S(1)}, u32[]{:S(2)}) copy-start(f32[32,16,128]{2,1,0:T(8,128)S(1)} %get-tuple-element.11.refs_3_) | copy-start | bytes 786436
  53.5 7.3 %collective-permute-start.4 = (f32[17,16,128]{2,1,0:T(8,128)S(1)}, f32[17,16,128]{2,1,0:T(8,128)S(1)}, u32[]{:S(2)}, u32[]{:S(2)}) collective-permute-start(f32[17,16,128]{2,1,0:T(8,128)S(1)} %get-tuple-element.9), channel_id=1, source_target_pairs={{0,4},{4,0},{1,5},{5,1},{2,6},{6,2},{3,7},{7,3},{8,12},{12,8},{9,1... | collective-permute-start | bytes 417800 | tf_op jit(solution)/shard_map/ppermute | solution.py:333
  60.9 16.3 %collective-permute-start.6 = (f32[32,16,128]{2,1,0:T(8,128)S(1)}, f32[32,16,128]{2,1,0:T(8,128)}, u32[]{:S(2)}, u32[]{:S(2)}) collective-permute-start(f32[32,16,128]{2,1,0:T(8,128)S(1)} %pad_maximum_fusion.1.refs_1_.refs_3_), channel_id=1, source_target_pairs={{0,8},{8,0},{16,24},{24,16},{32,40},{40,32},{48,56},{56,48},{64,72... | collective-permute-start | bytes 786440 | tf_op jit(solution)/shard_map/ppermute | solution.py:352
  64.1 14.5 %collective-permute-start.5 = (f32[32,16,128]{2,1,0:T(8,128)S(1)}, f32[32,16,128]{2,1,0:T(8,128)}, u32[]{:S(2)}, u32[]{:S(2)}) collective-permute-start(f32[32,16,128]{2,1,0:T(8,128)S(1)} %pad_maximum_fusion.1.refs_1_.refs_3_), channel_id=1, source_target_pairs={{0,504},{8,16},{16,8},{24,32},{32,24},{40,48},{48,40},{56,64},{64,... | collective-permute-start | bytes 786440 | tf_op jit(solution)/shard_map/ppermute | solution.py:353
  73.4 2.7 %copy-start.4 = (s32[151]{0:T(256)S(1)}, s32[151]{0:T(256)}, u32[]{:S(2)}) copy-start(s32[151]{0:T(256)} %lists.1.refs_0_) | copy-start | bytes 1816
  77.1 1.5 copy-start.3
  80.1 8.9 %collective-permute-start.11 = (f32[32,16,128]{2,1,0:T(8,128)S(1)}, f32[32,16,128]{2,1,0:T(8,128)S(1)}, u32[]{:S(2)}, u32[]{:S(2)}) collective-permute-start(f32[32,16,128]{2,1,0:T(8,128)S(1)} %shard_map.73.refs_1_.refs_3_), channel_id=1, source_target_pairs={{0,8},{8,0},{16,24},{24,16},{32,40},{40,32},{48,56},{56,48},{64,72... | collective-permute-start | bytes 786440 | tf_op jit(solution)/shard_map/ppermute | solution.py:352
  82.0 11.3 %collective-permute-start.10 = (f32[32,16,128]{2,1,0:T(8,128)S(1)}, f32[32,16,128]{2,1,0:T(8,128)S(1)}, u32[]{:S(2)}, u32[]{:S(2)}) collective-permute-start(f32[32,16,128]{2,1,0:T(8,128)S(1)} %shard_map.73.refs_1_.refs_3_), channel_id=1, source_target_pairs={{0,504},{8,16},{16,8},{24,32},{32,24},{40,48},{48,40},{56,64},{64,... | collective-permute-start | bytes 786440 | tf_op jit(solution)/shard_map/ppermute | solution.py:353
  94.4 7.1 %collective-permute-start.13 = (f32[32,16,128]{2,1,0:T(8,128)S(1)}, f32[32,16,128]{2,1,0:T(8,128)S(1)}, u32[]{:S(2)}, u32[]{:S(2)}) collective-permute-start(f32[32,16,128]{2,1,0:T(8,128)S(1)} %shard_map.76.refs_1_), channel_id=1, source_target_pairs={{0,8},{8,0},{16,24},{24,16},{32,40},{40,32},{48,56},{56,48},{64,72... | collective-permute-start | bytes 786440 | tf_op jit(solution)/shard_map/ppermute | solution.py:352
  96.3 10.4 %collective-permute-start.12 = (f32[32,16,128]{2,1,0:T(8,128)S(1)}, f32[32,16,128]{2,1,0:T(8,128)S(1)}, u32[]{:S(2)}, u32[]{:S(2)}) collective-permute-start(f32[32,16,128]{2,1,0:T(8,128)S(1)} %shard_map.76.refs_1_), channel_id=1, source_target_pairs={{0,504},{8,16},{16,8},{24,32},{32,24},{40,48},{48,40},{56,64},{64,... | collective-permute-start | bytes 786440 | tf_op jit(solution)/shard_map/ppermute | solution.py:353
  122.8 8.7 %collective-permute-start.14 = (f32[128,512]{1,0:T(8,128)S(1)}, f32[128,512]{1,0:T(8,128)S(1)}, u32[]{:S(2)}, u32[]{:S(2)}) collective-permute-start(f32[128,512]{1,0:T(8,128)S(1)} %get-tuple-element.13.refs_0_), channel_id=1, source_target_pairs={{0,2},{2,0},{1,3},{3,1},{4,6},{6,4},{5,7},{7,5},{8,10},{10,8},{9,1... | collective-permute-start | bytes 786440 | tf_op jit(solution)/shard_map/ppermute | solution.py:333
  131.6 43.3 %collective-permute-start.15 = (f32[256,512]{1,0:T(8,128)S(1)}, f32[256,512]{1,0:T(8,128)S(1)}, u32[]{:S(2)}, u32[]{:S(2)}) collective-permute-start(f32[256,512]{1,0:T(8,128)S(1)} %pad_maximum_fusion), channel_id=1, source_target_pairs={{0,1},{1,0},{2,3},{3,2},{4,5},{5,4},{6,7},{7,6},{8,9},{9,8},{10,11... | collective-permute-start | bytes 1572872 | tf_op jit(solution)/shard_map/ppermute | solution.py:333

commit v5 on v4

--- a/solution.py
+++ b/solution.py
@@ -18,6 +18,7 @@
 COLS = 16
 HALF = 2 * RB_DEV
 UNROLL = 4
+CHUNKS = 4
 BLOCK = 32
 FEW = 4
 GROUP = ("xh", "xl", "core")
@@ -25,6 +26,10 @@
 VMEM = pl.BlockSpec(memory_space=pltpu.VMEM)
 SMEM = pl.BlockSpec(memory_space=pltpu.SMEM)
 INTERPRET = False
+
+
+def in_hbm(value):
+    return value if INTERPRET else pltpu.with_memory_space_constraint(value, pltpu.MemorySpace.HBM)
 
 
 def split_bf16(value):
@@ -47,29 +52,75 @@
     )(*operands)
 
 
-def split_kernel(*refs):
-    *pieces, out_ref = refs
-    base = 0
-    for piece in pieces:
-        def body(slot, carry, piece=piece, base=base):
-            high, low = split_bf16(piece[slot].T)
-            out_ref[base + slot, 0] = high
-            out_ref[base + slot, 1] = low
+def sort_slots(ids, count_q, live, slot_of, lists):
+    q, xh = ids[0], ids[1]
+
+    def body(slot, fills):
+        row, column, place = slot_of(slot)
+        owner = column >> 4
+        step = lax.rem((owner >> 1) - q + 1 + count_q, count_q)
+        near = (step == 2) == ((q & 1) == 0)
+        piece = jnp.where(step == 1, 0, jnp.where(near, 1, 2))
+        local = ((owner & 1) ^ xh) * RB_DEV + (column & (RB_DEV - 1))
+        fill = jnp.where(piece == 0, fills[0], jnp.where(piece == 1, fills[1], fills[2]))
+        lists[piece * TILE_CAP + fill] = row + HALF * local + HALF * HALF * place
+        return tuple(fills[k] + (piece == k).astype(jnp.int32) for k in range(3))
+
+    zero = jnp.int32(0)
+    fills = lax.fori_loop(0, live, body, (zero, zero, zero))
+    for k in range(3):
+        lists[3 * TILE_CAP + k] = fills[k]
+    lists[3 * TILE_CAP + 3] = xh * RB_DEV
+
+
+def split_into(value, out_ref, slot):
+    high, low = split_bf16(value.T)
+    out_ref[slot, 0] = high
+    out_ref[slot, 1] = low
+
+
+def own_kernel(count_q, ids, rows, cols, count, tiles, split_ref, piece_ref, lists, held, sems):
+    chunk = TILE_CAP // CHUNKS
+    copies = []
+    for k in range(CHUNKS):
+        part = pl.ds(k * chunk, chunk)
+        copies.append(pltpu.make_async_copy(tiles.at[part], held.at[part], sems.at[k]))
+        copies[-1].start()
+
+    def slot_of(slot):
+        return rows[slot] & (RB_DEV - 1), cols[slot], slot
+
+    sort_slots(ids, count_q, count[0], slot_of, lists)
+    for k in range(CHUNKS):
+        copies[k].wait()
+
+        def body(slot, carry):
+            split_into(held[slot], split_ref, slot)
             return carry
 
-        lax.fori_loop(0, piece.shape[0], body, 0, unroll=2)
-        base += piece.shape[0]
-
-
-def split_tiles(pieces):
-    count = sum(piece.shape[0] for piece in pieces)
-    return call(
-        split_kernel,
-        jax.ShapeDtypeStruct((count, 2, BS, BS), jnp.bfloat16),
-        pieces,
-        [VMEM] * len(pieces),
-        moved=count * BS * BS * 8,
-    )
+        lax.fori_loop(k * chunk, (k + 1) * chunk, body, 0, unroll=2)
+    quarter = TILE_CAP // 4
+    for k in range(quarter):
+        piece_ref[k] = held[ids[2] * quarter + k]
+
+
+def other_kernel(count_q, ids, notes, pair, far, split_ref, lists):
+    quarter = TILE_CAP // 4
+
+    def slot_of(slot):
+        row = (notes[0, slot].astype(jnp.int32) & (RB_DEV - 1)) + RB_DEV
+        part = lax.div(slot, quarter)
+        order = part ^ ids[2]
+        order = (order & 1) * 2 + 1 - (order >> 1)
+        return row, notes[1, slot].astype(jnp.int32), order * quarter + slot - part * quarter
+
+    sort_slots(ids, count_q, notes[2, 0].astype(jnp.int32), slot_of, lists)
+    for base, piece in ((0, pair), (2 * quarter, far)):
+        def body(slot, carry, base=base, piece=piece):
+            split_into(piece[slot], split_ref, base + slot)
+            return carry
+
+        lax.fori_loop(0, 2 * quarter, body, 0, unroll=2)
 
 
 def dot_t(left, right, precision=None):
@@ -82,43 +133,8 @@
     )
 
 
-def list_kernel(count_q, ids, own_rows, own_cols, own_count, notes, lists):
-    q, xh, c = ids[0], ids[1], ids[2]
-    quarter = TILE_CAP // 4
-    for which in range(6):
-        lists[6 * TILE_CAP + which] = 0
-    lists[6 * TILE_CAP + 6] = xh * RB_DEV
-
-    def add(which, row, column, place):
-        owner = column >> 4
-        step = lax.rem((owner >> 1) - q + 1 + count_q, count_q)
-        near = (step == 2) == ((q & 1) == 0)
-        piece = jnp.where(step == 1, 0, jnp.where(near, 1, 2))
-        local = ((owner & 1) ^ xh) * RB_DEV + (column & (RB_DEV - 1))
-        target = piece * 2 + which
-        fill = lists[6 * TILE_CAP + target]
-        lists[target * TILE_CAP + fill] = row + HALF * local + HALF * HALF * place
-        lists[6 * TILE_CAP + target] = fill + 1
-
-    def own(slot, carry):
-        add(0, own_rows[slot] & (RB_DEV - 1), own_cols[slot], slot)
-        return carry
-
-    def partner(slot, carry):
-        row = (notes[0, slot].astype(jnp.int32) & (RB_DEV - 1)) + RB_DEV
-        part = lax.div(slot, quarter)
-        order = part ^ c
-        order = (order & 1) * 2 + 1 - (order >> 1)
-        place = order * quarter + slot - part * quarter
-        add(1, row, notes[1, slot].astype(jnp.int32), place)
-        return carry
-
-    lax.fori_loop(0, own_count[0], own, 0)
-    lax.fori_loop(0, notes[2, 0].astype(jnp.int32), partner, 0)
-
-
 def part_kernel(piece, final, *refs):
-    lists, source_ref, *middle, own_ref, other_ref, out_ref, window, total = refs
+    own_list, other_list, source_ref, *middle, own_ref, other_ref, out_ref, window, total = refs
 
     def fill(block, carry):
         high, low = split_bf16(source_ref[block])
@@ -131,11 +147,11 @@
         total[...] = jnp.zeros_like(total)
     else:
         total[...] = middle[0][...]
-    for which, tiles in enumerate((own_ref, other_ref)):
-        base = (piece * 2 + which) * TILE_CAP
-        live = lists[6 * TILE_CAP + piece * 2 + which]
-
-        def body(group, carry, base=base, tiles=tiles, live=live):
+    base = piece * TILE_CAP
+    for lists, tiles in ((own_list, own_ref), (other_list, other_ref)):
+        live = lists[3 * TILE_CAP + piece]
+
+        def body(group, carry, lists=lists, tiles=tiles, live=live):
             terms, rows = [], []
             for inner in range(UNROLL):
                 slot = group * UNROLL + inner
@@ -156,7 +172,7 @@
         out_ref[...] = total[...]
         return
     prev_ref = middle[1]
-    swap = lists[6 * TILE_CAP + 6] if final else 0
+    swap = own_list[3 * TILE_CAP + 3] if final else 0
 
     def finish(block, carry):
         source = block ^ swap if final else block
@@ -199,9 +215,8 @@
         for inner in range(UNROLL):
             slot = group * UNROLL + inner
             both = window[place_of(cols[slot])]
-            high, low = split_bf16(tiles[slot])
-            wide = dot_t(both, high)
-            narrow = dot_t(both[:wide_cols], low)
+            wide = dot_b(both, tiles[slot, 0])
+            narrow = dot_b(both[:wide_cols], tiles[slot, 1])
             term = wide[:wide_cols] + (wide[wide_cols:] + narrow)
             terms.append(jnp.where(slot < live, term, jnp.zeros_like(term)))
         for inner in range(UNROLL):
@@ -221,12 +236,12 @@
 
 
 def graph_part(lists, piece, source, middle, own_tiles, other_tiles, final):
-    operands = [lists, source, *middle, own_tiles, other_tiles]
+    operands = [*lists, source, *middle, own_tiles, other_tiles]
     return call(
         functools.partial(part_kernel, piece, final),
         jax.ShapeDtypeStruct((HALF, COLS, BS), jnp.float32),
         operands,
-        [SMEM] + [VMEM] * (len(operands) - 1),
+        [SMEM] * 2 + [VMEM] * (len(operands) - 2),
         scratch=[
             pltpu.VMEM((HALF, 2 * COLS, BS), jnp.bfloat16),
             pltpu.VMEM((HALF, COLS, BS), jnp.float32),
@@ -358,15 +373,27 @@
     diagonal = lax.ppermute(start_panel, ("q", "xh"), near)
     across = exchange(start_panel, "xh")
     one, two = halo(start_panel)
-    piece = lax.dynamic_slice_in_dim(tile_values, c * quarter, quarter, 0)
+    ids = jnp.stack([q, xh, c])
+    order = jax.ShapeDtypeStruct((3 * TILE_CAP + 4,), jnp.int32)
+    split = jax.ShapeDtypeStruct((TILE_CAP, 2, BS, BS), jnp.bfloat16)
+    own_tiles, piece, own_list = pl.pallas_call(
+        functools.partial(own_kernel, count_q),
+        out_shape=(split, jax.ShapeDtypeStruct((quarter, BS, BS), jnp.float32), order),
+        in_specs=[SMEM] * 4 + [pl.BlockSpec(memory_space=pltpu.MemorySpace.HBM)],
+        out_specs=(VMEM, VMEM, SMEM),
+        scratch_shapes=[
+            pltpu.VMEM((TILE_CAP, BS, BS), jnp.float32),
+            pltpu.SemaphoreType.DMA((CHUNKS,)),
+        ],
+        compiler_params=pltpu.CompilerParams(vmem_limit_bytes=24 << 20),
+        cost_estimate=pl.CostEstimate(flops=0, bytes_accessed=6 << 20, transcendentals=0),
+        interpret=INTERPRET,
+        name="own",
+    )(ids, in_hbm(tile_rows), in_hbm(tile_cols), tile_counts, in_hbm(tile_values))
     first = lax.ppermute(piece, ("xh", "xl"), [(i, 3 - i) for i in range(4)])
     second = exchange(first, "xl")
     pair = jnp.concatenate([first, second], axis=0)
     far = exchange(pair, "core")
-    own_tiles = split_tiles([tile_values])
-    other_tiles = split_tiles([pair, far])
-
-    ids = jnp.stack([q, xh, c])
     notes = jnp.concatenate(
         [
             tile_rows.astype(jnp.float32)[None],
@@ -386,7 +413,7 @@
         ),
         [
             ids, tile_rows, tile_cols, tile_counts,
-            notes, start_panel, one, two, across, diagonal, tile_values,
+            notes, start_panel, one, two, across, diagonal, own_tiles,
         ],
         [SMEM] * 4 + [VMEM] * 7,
         scratch=[
@@ -398,14 +425,17 @@
     )
     got = exchange(given, "xh")
     current = jnp.concatenate([mine, got[:RB_DEV]], axis=0)
-    lists = pl.pallas_call(
-        functools.partial(list_kernel, count_q),
-        out_shape=jax.ShapeDtypeStruct((6 * TILE_CAP + 7,), jnp.int32),
-        in_specs=[SMEM] * 5,
-        out_specs=SMEM,
+    other_tiles, other_list = pl.pallas_call(
+        functools.partial(other_kernel, count_q),
+        out_shape=(split, order),
+        in_specs=[SMEM] * 2 + [VMEM] * 2,
+        out_specs=(VMEM, SMEM),
+        compiler_params=pltpu.CompilerParams(vmem_limit_bytes=24 << 20),
+        cost_estimate=pl.CostEstimate(flops=0, bytes_accessed=6 << 20, transcendentals=0),
         interpret=INTERPRET,
-        name="lists",
-    )(ids, tile_rows, tile_cols, tile_counts, got[RB_DEV, :3, :TILE_CAP])
+        name="other",
+    )(ids, got[RB_DEV, :3, :TILE_CAP], pair, far)
+    lists = (own_list, other_list)
     for step in range(1, DEGREE):
         one, two = halo(current)
         final = step == DEGREE - 1

time: 184 us -> 183 us (level)
  waiting for transfers between devices: 28.1 us -> 37.5 us
  starting transfers between devices: 67.4 us -> 60.4 us
  local copies, waits for them, and re-layouts: 5.44 us -> 0.19 us
  blocking collectives: 54 us -> 56.6 us
    ppermute x4, starting transfers between devices: 25.7 us -> 20 us  [halo(): two = lax.ppermute(value, 'q', odd)]
    pallas_call x14 -> x12, Pallas kernels: 24.2 us -> 19.2 us  [call(): pl.pallas_call(kernel, out_shape=out_shape, in_specs=specs, out_specs=out...]
    ppermute x4, waiting for transfers between devices: 7.57 us -> 12.2 us  [halo(): two = lax.ppermute(value, 'q', odd)]
    ppermute x1, waiting for transfers between devices: 1.43 us -> 6.05 us  [filtered_basis(): diagonal = lax.ppermute(start_panel, ('q', 'xh'), near)]
    pallas_call x1 -> x2, Pallas kernels: 1.6 us -> 6.09 us  [the longest x1 3.6 us: filtered_basis(): pl.pallas_call(functools.partial(own_kernel, count_q), out_shape=(split,...]
    all_to_all x4, blocking collectives: 54 us -> 56.6 us  [to_all(): return lax.all_to_all(value, axis, 0, 0, tiled=True)]
  transfers between devices with their start and end apart: 16 -> 16, of which waited for: 8 -> 9; matrix products, arithmetic and copies ran while one was open for 3% -> 0% of each run, Pallas kernels for 7% -> 5%
where the time goes in v5:
time: 183 us; the launch traced here: 182 us
  starting transfers between devices  60.4 us (33%)
  blocking collectives  56.6 us (31%)
  waiting for transfers between devices  37.5 us (20%)
  Pallas kernels  25.3 us (14%)
    all_to_all x4, blocking collectives, to_all(): return lax.all_to_all(value, axis, 0, 0, tiled=True)  56.6 us
    ppermute x6, starting transfers between devices, exchange(): return lax.ppermute(value, axis, [(0, 1), (1, 0)])  23.5 us
    ppermute x4, starting transfers between devices, halo(): two = lax.ppermute(value, 'q', odd)  20 us
    pallas_call x12, Pallas kernels, call(): pl.pallas_call(kernel, out_shape=out_shape, in_specs=specs, out_specs=out...  19.2 us
    ppermute x4, waiting for transfers between devices, halo(): two = lax.ppermute(value, 'q', odd)  12.2 us
    ppermute x6, waiting for transfers between devices, exchange(): return lax.ppermute(value, axis, [(0, 1), (1, 0)])  11.9 us
    ppermute x4, starting transfers between devices, halo(): one = lax.ppermute(value, 'q', even)  9.77 us
    ppermute x1, waiting for transfers between devices, filtered_basis(): diagonal = lax.ppermute(start_panel, ('q', 'xh'), near)  6.05 us
  transfers between devices with their start and end apart: 16, of which 9 were waited for; matrix products, arithmetic and copies ran while one was open for 0% of the time, Pallas kernels for 5%

profile of v5, /device:TPU:1, one launch (start us, length us, event | category | flops | bytes accessed | tf_op | source)
XLA Modules:
  0.0 182.0 jit_solution(3305980155018112156)
XLA Ops:
  1.4 3.6 %own.1 = (bf16[24,2,128,128]{3,2,1,0:T(8,128)(2,1)S(1)}, f32[6,128,128]{2,1,0:T(8,128)S(1)}, s32[76]{0:T(128)S(1)}) custom-call(s32[3]{0:T(128)S(1)} %pad_add_fusion.ids.refs_0_, s32[24]{0:T(128)} %refs_1_.1, s32[24]{0:T(128)} %refs_2_.1, s32[1]{0:T(128)S(6)} %copy.10.count.refs_3_, f32[24,128,128]{2,1,0:T(8,128)} %tiles.1), custom_call_target="tpu_custom_call" | custom-call | bytes 6291456 | tf_op jit(solution)/shard_map/own/pallas_call | solution.py:379
  5.0 5.2 %collective-permute-start.5 = (f32[6,128,128]{2,1,0:T(8,128)S(1)}, f32[6,128,128]{2,1,0:T(8,128)S(1)}, u32[]{:S(2)}, u32[]{:S(2)}) collective-permute-start(f32[6,128,128]{2,1,0:T(8,128)S(1)} %get-tuple-element.17), channel_id=1, source_target_pairs={{0,6},{2,4},{4,2},{6,0},{1,7},{3,5},{5,3},{7,1},{8,14},{10,12},{12... | collective-permute-start | bytes 1179656 | tf_op jit(solution)/shard_map/ppermute | solution.py:393
  10.2 5.2 %collective-permute-done.5 = f32[6,128,128]{2,1,0:T(8,128)S(1)} collective-permute-done((f32[6,128,128]{2,1,0:T(8,128)S(1)}, f32[6,128,128]{2,1,0:T(8,128)S(1)}, u32[]{:S(2)}, u32[]{:S(2)}) %collective-permute-start.5) | collective-permute-done | bytes 393248 | tf_op jit(solution)/shard_map/ppermute | solution.py:393
  15.4 5.4 %collective-permute-start.6 = (f32[6,128,128]{2,1,0:T(8,128)S(1)}, f32[6,128,128]{2,1,0:T(8,128)S(1)}, u32[]{:S(2)}, u32[]{:S(2)}) collective-permute-start(f32[6,128,128]{2,1,0:T(8,128)S(1)} %collective-permute-done.5), channel_id=1, source_target_pairs={{0,2},{2,0},{1,3},{3,1},{4,6},{6,4},{5,7},{7,5},{8,10},{10,8},{9,1... | collective-permute-start | bytes 1179656 | tf_op jit(solution)/shard_map/ppermute | solution.py:348
  20.9 4.0 %collective-permute-start = (f32[32,2048]{1,0:T(8,128)S(1)}, f32[32,2048]{1,0:T(8,128)S(1)}, u32[]{:S(2)}, u32[]{:S(2)}) collective-permute-start(f32[32,2048]{1,0:T(8,128)S(1)} %copy-done), channel_id=1, source_target_pairs={{0,8},{8,0},{16,24},{24,16},{32,40},{40,32},{48,56},{56,48},{64,72... | collective-permute-start | bytes 786440 | tf_op jit(solution)/shard_map/ppermute | solution.py:367
  24.9 11.8 %collective-permute-start.1 = (f32[32,2048]{1,0:T(8,128)S(1)}, f32[32,2048]{1,0:T(8,128)S(1)}, u32[]{:S(2)}, u32[]{:S(2)}) collective-permute-start(f32[32,2048]{1,0:T(8,128)S(1)} %copy-done), channel_id=1, source_target_pairs={{0,504},{8,16},{16,8},{24,32},{32,24},{40,48},{48,40},{56,64},{64,... | collective-permute-start | bytes 786440 | tf_op jit(solution)/shard_map/ppermute | solution.py:368
  36.6 5.6 %collective-permute-start.2 = (f32[32,2048]{1,0:T(8,128)S(1)}, f32[32,2048]{1,0:T(8,128)S(1)}, u32[]{:S(2)}, u32[]{:S(2)}) collective-permute-start(f32[32,2048]{1,0:T(8,128)S(1)} %copy-done), channel_id=1, source_target_pairs={{0,4},{4,0},{1,5},{5,1},{2,6},{6,2},{3,7},{7,3},{8,12},{12,8},{9,1... | collective-permute-start | bytes 786440 | tf_op jit(solution)/shard_map/ppermute | solution.py:348
  42.2 1.9 %collective-permute-start.3 = (f32[32,2048]{1,0:T(8,128)S(1)}, f32[32,2048]{1,0:T(8,128)S(1)}, u32[]{:S(2)}, u32[]{:S(2)}) collective-permute-start(f32[32,2048]{1,0:T(8,128)S(1)} %copy-done), channel_id=1, source_target_pairs={{0,508},{4,8},{8,4},{12,16},{16,12},{20,24},{24,20},{28,32},{32,28... | collective-permute-start | bytes 786440 | tf_op jit(solution)/shard_map/ppermute | solution.py:373
  44.2 4.6 %collective-permute-start.7 = (f32[12,128,128]{2,1,0:T(8,128)S(1)}, f32[12,128,128]{2,1,0:T(8,128)S(1)}, u32[]{:S(2)}, u32[]{:S(2)}) collective-permute-start(f32[12,128,128]{2,1,0:T(8,128)S(1)} %constant_dynamic-update-slice_fusion.pair), channel_id=1, source_target_pairs={{0,1},{1,0},{2,3},{3,2},{4,5},{5,4},{6,7},{7,6},{8,9},{9,8},{10,11... | collective-permute-start | bytes 2359304 | tf_op jit(solution)/shard_map/ppermute | solution.py:348
  49.0 6.1 %collective-permute-done.3.refs_9_ = f32[32,2048]{1,0:T(8,128)S(1)} collective-permute-done((f32[32,2048]{1,0:T(8,128)S(1)}, f32[32,2048]{1,0:T(8,128)S(1)}, u32[]{:S(2)}, u32[]{:S(2)}) %collective-permute-start.3) | collective-permute-done | bytes 262176 | tf_op jit(solution)/shard_map/ppermute | solution.py:373
  55.0 1.1 shard_map.68
  56.2 1.9 %collective-permute-start.4 = (f32[17,16,128]{2,1,0:T(8,128)S(1)}, f32[17,16,128]{2,1,0:T(8,128)S(1)}, u32[]{:S(2)}, u32[]{:S(2)}) collective-permute-start(f32[17,16,128]{2,1,0:T(8,128)S(1)} %get-tuple-element.16), channel_id=1, source_target_pairs={{0,4},{4,0},{1,5},{5,1},{2,6},{6,2},{3,7},{7,3},{8,12},{12,8},{9,1... | collective-permute-start | bytes 417800 | tf_op jit(solution)/shard_map/ppermute | solution.py:348
  58.1 5.4 %collective-permute-done.4 = f32[17,16,128]{2,1,0:T(8,128)S(1)} collective-permute-done((f32[17,16,128]{2,1,0:T(8,128)S(1)}, f32[17,16,128]{2,1,0:T(8,128)S(1)}, u32[]{:S(2)}, u32[]{:S(2)}) %collective-permute-start.4) | collective-permute-done | bytes 139296 | tf_op jit(solution)/shard_map/ppermute | solution.py:348
  63.5 1.9 %collective-permute-start.9 = (f32[32,16,128]{2,1,0:T(8,128)S(1)}, f32[32,16,128]{2,1,0:T(8,128)S(1)}, u32[]{:S(2)}, u32[]{:S(2)}) collective-permute-start(f32[32,16,128]{2,1,0:T(8,128)S(1)} %pad_maximum_fusion.1.refs_2_.refs_4_), channel_id=1, source_target_pairs={{0,8},{8,0},{16,24},{24,16},{32,40},{40,32},{48,56},{56,48},{64,72... | collective-permute-start | bytes 786440 | tf_op jit(solution)/shard_map/ppermute | solution.py:367
  65.5 2.1 %collective-permute-start.8 = (f32[32,16,128]{2,1,0:T(8,128)S(1)}, f32[32,16,128]{2,1,0:T(8,128)S(1)}, u32[]{:S(2)}, u32[]{:S(2)}) collective-permute-start(f32[32,16,128]{2,1,0:T(8,128)S(1)} %pad_maximum_fusion.1.refs_2_.refs_4_), channel_id=1, source_target_pairs={{0,504},{8,16},{16,8},{24,32},{32,24},{40,48},{48,40},{56,64},{64,... | collective-permute-start | bytes 786440 | tf_op jit(solution)/shard_map/ppermute | solution.py:368
  67.6 2.5 %other.1 = (bf16[24,2,128,128]{3,2,1,0:T(8,128)(2,1)S(1)}, s32[76]{0:T(128)S(1)}) custom-call(s32[3]{0:T(128)S(1)} %pad_add_fusion.ids.refs_0_, f32[3,24]{1,0:T(4,128)S(1)} %slice_bitcast_fusion.notes, f32[12,128,128]{2,1,0:T(8,128)S(1)} %constant_dynamic-update-slice_fusion.pair, f32[12,128,128]{2,1,0:T(8,128)S(1)} %collective-permute-done.7.far), custom_call_target="tpu_custom_call" | custom-call | bytes 6291456 | tf_op jit(solution)/shard_map/other/pallas_call | solution.py:428
  72.2 3.7 %collective-permute-done.8.refs_2_ = f32[32,16,128]{2,1,0:T(8,128)S(1)} collective-permute-done((f32[32,16,128]{2,1,0:T(8,128)S(1)}, f32[32,16,128]{2,1,0:T(8,128)S(1)}, u32[]{:S(2)}, u32[]{:S(2)}) %collective-permute-start.8) | collective-permute-done | bytes 262176 | tf_op jit(solution)/shard_map/ppermute | solution.py:368
  76.9 1.9 %collective-permute-start.11 = (f32[32,16,128]{2,1,0:T(8,128)S(1)}, f32[32,16,128]{2,1,0:T(8,128)S(1)}, u32[]{:S(2)}, u32[]{:S(2)}) collective-permute-start(f32[32,16,128]{2,1,0:T(8,128)S(1)} %shard_map.71.refs_2_.refs_4_), channel_id=1, source_target_pairs={{0,8},{8,0},{16,24},{24,16},{32,40},{40,32},{48,56},{56,48},{64,72... | collective-permute-start | bytes 786440 | tf_op jit(solution)/shard_map/ppermute | solution.py:367
  78.9 3.1 %collective-permute-start.10 = (f32[32,16,128]{2,1,0:T(8,128)S(1)}, f32[32,16,128]{2,1,0:T(8,128)S(1)}, u32[]{:S(2)}, u32[]{:S(2)}) collective-permute-start(f32[32,16,128]{2,1,0:T(8,128)S(1)} %shard_map.71.refs_2_.refs_4_), channel_id=1, source_target_pairs={{0,504},{8,16},{16,8},{24,32},{32,24},{40,48},{48,40},{56,64},{64,... | collective-permute-start | bytes 786440 | tf_op jit(solution)/shard_map/ppermute | solution.py:368
  85.1 4.2 %collective-permute-done.10.refs_2_ = f32[32,16,128]{2,1,0:T(8,128)S(1)} collective-permute-done((f32[32,16,128]{2,1,0:T(8,128)S(1)}, f32[32,16,128]{2,1,0:T(8,128)S(1)}, u32[]{:S(2)}, u32[]{:S(2)}) %collective-permute-start.10) | collective-permute-done | bytes 262176 | tf_op jit(solution)/shard_map/ppermute | solution.py:368
  90.3 1.9 %collective-permute-start.13 = (f32[32,16,128]{2,1,0:T(8,128)S(1)}, f32[32,16,128]{2,1,0:T(8,128)S(1)}, u32[]{:S(2)}, u32[]{:S(2)}) collective-permute-start(f32[32,16,128]{2,1,0:T(8,128)S(1)} %shard_map.74.refs_2_), channel_id=1, source_target_pairs={{0,8},{8,0},{16,24},{24,16},{32,40},{40,32},{48,56},{56,48},{64,72... | collective-permute-start | bytes 786440 | tf_op jit(solution)/shard_map/ppermute | solution.py:367
  92.3 3.1 %collective-permute-start.12 = (f32[32,16,128]{2,1,0:T(8,128)S(1)}, f32[32,16,128]{2,1,0:T(8,128)S(1)}, u32[]{:S(2)}, u32[]{:S(2)}) collective-permute-start(f32[32,16,128]{2,1,0:T(8,128)S(1)} %shard_map.74.refs_2_), channel_id=1, source_target_pairs={{0,504},{8,16},{16,8},{24,32},{32,24},{40,48},{48,40},{56,64},{64,... | collective-permute-start | bytes 786440 | tf_op jit(solution)/shard_map/ppermute | solution.py:368
  96.4 1.1 collective-permute-done.13.refs_2_
  98.5 4.2 %collective-permute-done.12.refs_2_ = f32[32,16,128]{2,1,0:T(8,128)S(1)} collective-permute-done((f32[32,16,128]{2,1,0:T(8,128)S(1)}, f32[32,16,128]{2,1,0:T(8,128)S(1)}, u32[]{:S(2)}, u32[]{:S(2)}) %collective-permute-start.12) | collective-permute-done | bytes 262176 | tf_op jit(solution)/shard_map/ppermute | solution.py:368
  103.8 17.3 %all_to_all.24.parts_ref = f32[8,4,16,128]{3,2,1,0:T(8,128)S(1)} all-to-all(f32[8,4,16,128]{3,2,1,0:T(8,128)S(1)} %bitcast.13), channel_id=1, replica_groups=mesh['q'=64,'xh'=2,'xl'=2,'core'=2] {'xh','xl','core'}, dimensions={0} | all-to-all | bytes 524288 | tf_op jit(solution)/shard_map/all_to_all | solution.py:352
  121.4 2.2 %collective-permute-start.14 = (f32[128,512]{1,0:T(8,128)S(1)}, f32[128,512]{1,0:T(8,128)S(1)}, u32[]{:S(2)}, u32[]{:S(2)}) collective-permute-start(f32[128,512]{1,0:T(8,128)S(1)} %get-tuple-element.23.refs_0_), channel_id=1, source_target_pairs={{0,2},{2,0},{1,3},{3,1},{4,6},{6,4},{5,7},{7,5},{8,10},{10,8},{9,1... | collective-permute-start | bytes 786440 | tf_op jit(solution)/shard_map/ppermute | solution.py:348
  123.7 6.5 %collective-permute-done.14.refs_1_ = f32[128,512]{1,0:T(8,128)S(1)} collective-permute-done((f32[128,512]{1,0:T(8,128)S(1)}, f32[128,512]{1,0:T(8,128)S(1)}, u32[]{:S(2)}, u32[]{:S(2)}) %collective-permute-start.14) | collective-permute-done | bytes 262176 | tf_op jit(solution)/shard_map/ppermute | solution.py:348
  130.2 3.8 %collective-permute-start.15 = (f32[256,512]{1,0:T(8,128)S(1)}, f32[256,512]{1,0:T(8,128)S(1)}, u32[]{:S(2)}, u32[]{:S(2)}) collective-permute-start(f32[256,512]{1,0:T(8,128)S(1)} %pad_maximum_fusion), channel_id=1, source_target_pairs={{0,1},{1,0},{2,3},{3,2},{4,5},{5,4},{6,7},{7,6},{8,9},{9,8},{10,11... | collective-permute-start | bytes 1572872 | tf_op jit(solution)/shard_map/ppermute | solution.py:348
  134.0 15.9 %all_to_all.25 = f32[64,2,128]{2,1,0:T(2,128)S(1)} all-to-all(f32[64,2,128]{2,1,0:T(2,128)S(1)} %bitcast.15), channel_id=1, replica_groups=mesh['q'=64,'xh'=2,'xl'=2,'core'=2] {'q'}, dimensions={0} | all-to-all | bytes 131072 | tf_op jit(solution)/shard_map/all_to_all | solution.py:352
  150.0 8.4 %all_to_all.26 = f32[8,2,128]{2,1,0:T(2,128)S(1)} all-to-all(f32[8,2,128]{2,1,0:T(2,128)S(1)} %broadcast_in_dim.34), channel_id=1, replica_groups=mesh['q'=64,'xh'=2,'xl'=2,'core'=2] {'xh','xl','core'}, dimensions={0} | all-to-all | bytes 16384 | tf_op jit(solution)/shard_map/all_to_all | solution.py:352
  158.5 15.0 %all_to_all.27 = f32[64,2,128]{2,1,0:T(2,128)S(1)} all-to-all(f32[64,2,128]{2,1,0:T(2,128)S(1)} %broadcast_in_dim.35), channel_id=1, replica_groups=mesh['q'=64,'xh'=2,'xl'=2,'core'=2] {'q'}, dimensions={0} | all-to-all | bytes 131072 | tf_op jit(solution)/shard_map/all_to_all | solution.py:352
  173.5 8.5 %shard_map.79 = (f32[128,128]{1,0:T(8,128)}, f32[32,2048]{1,0:T(8,128)}) custom-call(s32[1]{0:T(128)} %bitcast.place_ref, f32[128,128]{1,0:T(8,128)S(1)} %bitcast.14, f32[128,512]{1,0:T(8,128)S(1)} %get-tuple-element.23.refs_0_, f32[128,512]{1,0:T(8,128)S(1)} %collective-permute-done.14.refs_1_, f32[256,512]{1,0:T(8,128)S(1)} %collective-permute-done.15.refs_2_), custom_call_target="tpu_custom_call" | custom-call | flops 100663296 | bytes 1048576 | tf_op jit(solution)/shard_map/pallas_call | solution.py:43
  (39 shorter events, 11.2 us)
Async XLA Ops:
  0.6 20.2 %copy-start = (f32[32,2048]{1,0:T(8,128)S(1)}, f32[32,2048]{1,0:T(8,128)}, u32[]{:S(2)}) copy-start(f32[32,2048]{1,0:T(8,128)} %refs_5_.1) | copy-start | bytes 786436
  1.4 47.4 %copy-start.1 = (s32[24]{0:T(128)S(1)}, s32[24]{0:T(128)}, u32[]{:S(2)}) copy-start(s32[24]{0:T(128)} %refs_1_.1) | copy-start | bytes 292
  1.4 47.4 %copy-start.2 = (s32[24]{0:T(128)S(1)}, s32[24]{0:T(128)}, u32[]{:S(2)}) copy-start(s32[24]{0:T(128)} %refs_2_.1) | copy-start | bytes 292
  5.0 10.4 %collective-permute-start.5 = (f32[6,128,128]{2,1,0:T(8,128)S(1)}, f32[6,128,128]{2,1,0:T(8,128)S(1)}, u32[]{:S(2)}, u32[]{:S(2)}) collective-permute-start(f32[6,128,128]{2,1,0:T(8,128)S(1)} %get-tuple-element.17), channel_id=1, source_target_pairs={{0,6},{2,4},{4,2},{6,0},{1,7},{3,5},{5,3},{7,1},{8,14},{10,12},{12... | collective-permute-start | bytes 1179656 | tf_op jit(solution)/shard_map/ppermute | solution.py:393
  15.4 28.8 %collective-permute-start.6 = (f32[6,128,128]{2,1,0:T(8,128)S(1)}, f32[6,128,128]{2,1,0:T(8,128)S(1)}, u32[]{:S(2)}, u32[]{:S(2)}) collective-permute-start(f32[6,128,128]{2,1,0:T(8,128)S(1)} %collective-permute-done.5), channel_id=1, source_target_pairs={{0,2},{2,0},{1,3},{3,1},{4,6},{6,4},{5,7},{7,5},{8,10},{10,8},{9,1... | collective-permute-start | bytes 1179656 | tf_op jit(solution)/shard_map/ppermute | solution.py:348
  20.9 28.1 %collective-permute-start = (f32[32,2048]{1,0:T(8,128)S(1)}, f32[32,2048]{1,0:T(8,128)S(1)}, u32[]{:S(2)}, u32[]{:S(2)}) collective-permute-start(f32[32,2048]{1,0:T(8,128)S(1)} %copy-done), channel_id=1, source_target_pairs={{0,8},{8,0},{16,24},{24,16},{32,40},{40,32},{48,56},{56,48},{64,72... | collective-permute-start | bytes 786440 | tf_op jit(solution)/shard_map/ppermute | solution.py:367
  24.9 24.1 %collective-permute-start.1 = (f32[32,2048]{1,0:T(8,128)S(1)}, f32[32,2048]{1,0:T(8,128)S(1)}, u32[]{:S(2)}, u32[]{:S(2)}) collective-permute-start(f32[32,2048]{1,0:T(8,128)S(1)} %copy-done), channel_id=1, source_target_pairs={{0,504},{8,16},{16,8},{24,32},{32,24},{40,48},{48,40},{56,64},{64,... | collective-permute-start | bytes 786440 | tf_op jit(solution)/shard_map/ppermute | solution.py:368
  36.6 12.3 %collective-permute-start.2 = (f32[32,2048]{1,0:T(8,128)S(1)}, f32[32,2048]{1,0:T(8,128)S(1)}, u32[]{:S(2)}, u32[]{:S(2)}) collective-permute-start(f32[32,2048]{1,0:T(8,128)S(1)} %copy-done), channel_id=1, source_target_pairs={{0,4},{4,0},{1,5},{5,1},{2,6},{6,2},{3,7},{7,3},{8,12},{12,8},{9,1... | collective-permute-start | bytes 786440 | tf_op jit(solution)/shard_map/ppermute | solution.py:348
  42.2 12.8 %collective-permute-start.3 = (f32[32,2048]{1,0:T(8,128)S(1)}, f32[32,2048]{1,0:T(8,128)S(1)}, u32[]{:S(2)}, u32[]{:S(2)}) collective-permute-start(f32[32,2048]{1,0:T(8,128)S(1)} %copy-done), channel_id=1, source_target_pairs={{0,508},{4,8},{8,4},{12,16},{16,12},{20,24},{24,20},{28,32},{32,28... | collective-permute-start | bytes 786440 | tf_op jit(solution)/shard_map/ppermute | solution.py:373
  44.2 23.4 %collective-permute-start.7 = (f32[12,128,128]{2,1,0:T(8,128)S(1)}, f32[12,128,128]{2,1,0:T(8,128)S(1)}, u32[]{:S(2)}, u32[]{:S(2)}) collective-permute-start(f32[12,128,128]{2,1,0:T(8,128)S(1)} %constant_dynamic-update-slice_fusion.pair), channel_id=1, source_target_pairs={{0,1},{1,0},{2,3},{3,2},{4,5},{5,4},{6,7},{7,6},{8,9},{9,8},{10,11... | collective-permute-start | bytes 2359304 | tf_op jit(solution)/shard_map/ppermute | solution.py:348
  56.2 7.3 %collective-permute-start.4 = (f32[17,16,128]{2,1,0:T(8,128)S(1)}, f32[17,16,128]{2,1,0:T(8,128)S(1)}, u32[]{:S(2)}, u32[]{:S(2)}) collective-permute-start(f32[17,16,128]{2,1,0:T(8,128)S(1)} %get-tuple-element.16), channel_id=1, source_target_pairs={{0,4},{4,0},{1,5},{5,1},{2,6},{6,2},{3,7},{7,3},{8,12},{12,8},{9,1... | collective-permute-start | bytes 417800 | tf_op jit(solution)/shard_map/ppermute | solution.py:348
  63.5 7.6 %collective-permute-start.9 = (f32[32,16,128]{2,1,0:T(8,128)S(1)}, f32[32,16,128]{2,1,0:T(8,128)S(1)}, u32[]{:S(2)}, u32[]{:S(2)}) collective-permute-start(f32[32,16,128]{2,1,0:T(8,128)S(1)} %pad_maximum_fusion.1.refs_2_.refs_4_), channel_id=1, source_target_pairs={{0,8},{8,0},{16,24},{24,16},{32,40},{40,32},{48,56},{56,48},{64,72... | collective-permute-start | bytes 786440 | tf_op jit(solution)/shard_map/ppermute | solution.py:367
  65.5 10.4 %collective-permute-start.8 = (f32[32,16,128]{2,1,0:T(8,128)S(1)}, f32[32,16,128]{2,1,0:T(8,128)S(1)}, u32[]{:S(2)}, u32[]{:S(2)}) collective-permute-start(f32[32,16,128]{2,1,0:T(8,128)S(1)} %pad_maximum_fusion.1.refs_2_.refs_4_), channel_id=1, source_target_pairs={{0,504},{8,16},{16,8},{24,32},{32,24},{40,48},{48,40},{56,64},{64,... | collective-permute-start | bytes 786440 | tf_op jit(solution)/shard_map/ppermute | solution.py:368
  76.9 7.1 %collective-permute-start.11 = (f32[32,16,128]{2,1,0:T(8,128)S(1)}, f32[32,16,128]{2,1,0:T(8,128)S(1)}, u32[]{:S(2)}, u32[]{:S(2)}) collective-permute-start(f32[32,16,128]{2,1,0:T(8,128)S(1)} %shard_map.71.refs_2_.refs_4_), channel_id=1, source_target_pairs={{0,8},{8,0},{16,24},{24,16},{32,40},{40,32},{48,56},{56,48},{64,72... | collective-permute-start | bytes 786440 | tf_op jit(solution)/shard_map/ppermute | solution.py:367
  78.9 10.4 %collective-permute-start.10 = (f32[32,16,128]{2,1,0:T(8,128)S(1)}, f32[32,16,128]{2,1,0:T(8,128)S(1)}, u32[]{:S(2)}, u32[]{:S(2)}) collective-permute-start(f32[32,16,128]{2,1,0:T(8,128)S(1)} %shard_map.71.refs_2_.refs_4_), channel_id=1, source_target_pairs={{0,504},{8,16},{16,8},{24,32},{32,24},{40,48},{48,40},{56,64},{64,... | collective-permute-start | bytes 786440 | tf_op jit(solution)/shard_map/ppermute | solution.py:368
  90.3 7.1 %collective-permute-start.13 = (f32[32,16,128]{2,1,0:T(8,128)S(1)}, f32[32,16,128]{2,1,0:T(8,128)S(1)}, u32[]{:S(2)}, u32[]{:S(2)}) collective-permute-start(f32[32,16,128]{2,1,0:T(8,128)S(1)} %shard_map.74.refs_2_), channel_id=1, source_target_pairs={{0,8},{8,0},{16,24},{24,16},{32,40},{40,32},{48,56},{56,48},{64,72... | collective-permute-start | bytes 786440 | tf_op jit(solution)/shard_map/ppermute | solution.py:367
  92.3 10.4 %collective-permute-start.12 = (f32[32,16,128]{2,1,0:T(8,128)S(1)}, f32[32,16,128]{2,1,0:T(8,128)S(1)}, u32[]{:S(2)}, u32[]{:S(2)}) collective-permute-start(f32[32,16,128]{2,1,0:T(8,128)S(1)} %shard_map.74.refs_2_), channel_id=1, source_target_pairs={{0,504},{8,16},{16,8},{24,32},{32,24},{40,48},{48,40},{56,64},{64,... | collective-permute-start | bytes 786440 | tf_op jit(solution)/shard_map/ppermute | solution.py:368
  121.4 8.7 %collective-permute-start.14 = (f32[128,512]{1,0:T(8,128)S(1)}, f32[128,512]{1,0:T(8,128)S(1)}, u32[]{:S(2)}, u32[]{:S(2)}) collective-permute-start(f32[128,512]{1,0:T(8,128)S(1)} %get-tuple-element.23.refs_0_), channel_id=1, source_target_pairs={{0,2},{2,0},{1,3},{3,1},{4,6},{6,4},{5,7},{7,5},{8,10},{10,8},{9,1... | collective-permute-start | bytes 786440 | tf_op jit(solution)/shard_map/ppermute | solution.py:348
  130.2 43.3 %collective-permute-start.15 = (f32[256,512]{1,0:T(8,128)S(1)}, f32[256,512]{1,0:T(8,128)S(1)}, u32[]{:S(2)}, u32[]{:S(2)}) collective-permute-start(f32[256,512]{1,0:T(8,128)S(1)} %pad_maximum_fusion), channel_id=1, source_target_pairs={{0,1},{1,0},{2,3},{3,2},{4,5},{5,4},{6,7},{7,6},{8,9},{9,8},{10,11... | collective-permute-start | bytes 1572872 | tf_op jit(solution)/shard_map/ppermute | solution.py:348

commit v6 on v5

--- a/solution.py
+++ b/solution.py
@@ -60,7 +60,7 @@
         owner = column >> 4
         step = lax.rem((owner >> 1) - q + 1 + count_q, count_q)
         near = (step == 2) == ((q & 1) == 0)
-        piece = jnp.where(step == 1, 0, jnp.where(near, 1, 2))
+        piece = jnp.where(step == 1, 0, jnp.where(near, 2, 1))
         local = ((owner & 1) ^ xh) * RB_DEV + (column & (RB_DEV - 1))
         fill = jnp.where(piece == 0, fills[0], jnp.where(piece == 1, fills[1], fills[2]))
         lists[piece * TILE_CAP + fill] = row + HALF * local + HALF * HALF * place
@@ -79,7 +79,7 @@
     out_ref[slot, 1] = low
 
 
-def own_kernel(count_q, ids, rows, cols, count, tiles, split_ref, piece_ref, lists, held, sems):
+def own_kernel(count_q, ids, rows, cols, count, tiles, split_ref, lists, held, sems):
     chunk = TILE_CAP // CHUNKS
     copies = []
     for k in range(CHUNKS):
@@ -99,9 +99,6 @@
             return carry
 
         lax.fori_loop(k * chunk, (k + 1) * chunk, body, 0, unroll=2)
-    quarter = TILE_CAP // 4
-    for k in range(quarter):
-        piece_ref[k] = held[ids[2] * quarter + k]
 
 
 def other_kernel(count_q, ids, notes, pair, far, split_ref, lists):
@@ -376,11 +373,11 @@
     ids = jnp.stack([q, xh, c])
     order = jax.ShapeDtypeStruct((3 * TILE_CAP + 4,), jnp.int32)
     split = jax.ShapeDtypeStruct((TILE_CAP, 2, BS, BS), jnp.bfloat16)
-    own_tiles, piece, own_list = pl.pallas_call(
+    own_tiles, own_list = pl.pallas_call(
         functools.partial(own_kernel, count_q),
-        out_shape=(split, jax.ShapeDtypeStruct((quarter, BS, BS), jnp.float32), order),
+        out_shape=(split, order),
         in_specs=[SMEM] * 4 + [pl.BlockSpec(memory_space=pltpu.MemorySpace.HBM)],
-        out_specs=(VMEM, VMEM, SMEM),
+        out_specs=(VMEM, SMEM),
         scratch_shapes=[
             pltpu.VMEM((TILE_CAP, BS, BS), jnp.float32),
             pltpu.SemaphoreType.DMA((CHUNKS,)),
@@ -390,6 +387,7 @@
         interpret=INTERPRET,
         name="own",
     )(ids, in_hbm(tile_rows), in_hbm(tile_cols), tile_counts, in_hbm(tile_values))
+    piece = lax.dynamic_slice_in_dim(tile_values, c * quarter, quarter, 0)
     first = lax.ppermute(piece, ("xh", "xl"), [(i, 3 - i) for i in range(4)])
     second = exchange(first, "xl")
     pair = jnp.concatenate([first, second], axis=0)
@@ -437,7 +435,7 @@
     )(ids, got[RB_DEV, :3, :TILE_CAP], pair, far)
     lists = (own_list, other_list)
     for step in range(1, DEGREE):
-        one, two = halo(current)
+        two, one = halo(current)
         final = step == DEGREE - 1
         tiles = (own_tiles, other_tiles, final)
         part = graph_part(lists, 0, current, (), *tiles)

time: 183 us -> 179 us (0.978)
  waiting for transfers between devices: 37.5 us -> 25.1 us
  starting transfers between devices: 60.4 us -> 71.4 us
  blocking collectives: 56.6 us -> 53.2 us
    ppermute x4, starting transfers between devices: 20 us -> 31.7 us  [halo(): two = lax.ppermute(value, 'q', odd)]
    ppermute x4, waiting for transfers between devices: 12.2 us -> 6.66 us  [halo(): two = lax.ppermute(value, 'q', odd)]
    ppermute x1, waiting for transfers between devices: 6.05 us -> 1.02 us  [filtered_basis(): diagonal = lax.ppermute(start_panel, ('q', 'xh'), near)]
    all_to_all x4, blocking collectives: 56.6 us -> 53.2 us  [to_all(): return lax.all_to_all(value, axis, 0, 0, tiled=True)]
    ppermute x6, waiting for transfers between devices: 11.9 us -> 8.96 us  [exchange(): return lax.ppermute(value, axis, [(0, 1), (1, 0)])]
    ppermute x4, starting transfers between devices: 9.77 us -> 7.68 us  [halo(): one = lax.ppermute(value, 'q', even)]
  transfers between devices with their start and end apart: 16 -> 16, of which waited for: 9 -> 9; matrix products, arithmetic and copies ran while one was open for 0% -> 1% of each run, Pallas kernels for 5% -> 7%
where the time goes in v6:
time: 179 us
  starting transfers between devices  71.4 us (40%)
  blocking collectives  53.2 us (30%)
  Pallas kernels  25.2 us (14%)
  waiting for transfers between devices  25.1 us (14%)
    all_to_all x4, blocking collectives, to_all(): return lax.all_to_all(value, axis, 0, 0, tiled=True)  53.2 us
    ppermute x4, starting transfers between devices, halo(): two = lax.ppermute(value, 'q', odd)  31.7 us
    ppermute x6, starting transfers between devices, exchange(): return lax.ppermute(value, axis, [(0, 1), (1, 0)])  24.6 us
    pallas_call x12, Pallas kernels, call(): pl.pallas_call(kernel, out_shape=out_shape, in_specs=specs, out_specs=out...  19.2 us
    ppermute x6, waiting for transfers between devices, exchange(): return lax.ppermute(value, axis, [(0, 1), (1, 0)])  8.96 us
    ppermute x4, starting transfers between devices, halo(): one = lax.ppermute(value, 'q', even)  7.68 us
    ppermute x4, waiting for transfers between devices, halo(): two = lax.ppermute(value, 'q', odd)  6.66 us
    ppermute x1, starting transfers between devices, filtered_basis(): first = lax.ppermute(piece, ('xh', 'xl'), [(i, 3 - i) for i in range(4)])  5.2 us
  transfers between devices with their start and end apart: 16, of which 9 were waited for; matrix products, arithmetic and copies ran while one was open for 1% of the time, Pallas kernels for 7%

profile of v6, /device:TPU:1, one launch (start us, length us, event | category | flops | bytes accessed | tf_op | source)
XLA Modules:
  0.0 178.6 jit_solution(372729769532728259)
XLA Ops:
  1.7 5.2 %collective-permute-start.5 = (f32[6,128,128]{2,1,0:T(8,128)S(1)}, f32[6,128,128]{2,1,0:T(8,128)S(1)}, u32[]{:S(2)}, u32[]{:S(2)}) collective-permute-start(f32[6,128,128]{2,1,0:T(8,128)S(1)} %constant_dynamic-slice_fusion), channel_id=1, source_target_pairs={{0,6},{2,4},{4,2},{6,0},{1,7},{3,5},{5,3},{7,1},{8,14},{10,12},{12... | collective-permute-start | bytes 1179656 | tf_op jit(solution)/shard_map/ppermute | solution.py:391
  6.9 5.2 %collective-permute-done.5 = f32[6,128,128]{2,1,0:T(8,128)S(1)} collective-permute-done((f32[6,128,128]{2,1,0:T(8,128)S(1)}, f32[6,128,128]{2,1,0:T(8,128)S(1)}, u32[]{:S(2)}, u32[]{:S(2)}) %collective-permute-start.5) | collective-permute-done | bytes 393248 | tf_op jit(solution)/shard_map/ppermute | solution.py:391
  12.1 5.4 %collective-permute-start.6 = (f32[6,128,128]{2,1,0:T(8,128)S(1)}, f32[6,128,128]{2,1,0:T(8,128)S(1)}, u32[]{:S(2)}, u32[]{:S(2)}) collective-permute-start(f32[6,128,128]{2,1,0:T(8,128)S(1)} %collective-permute-done.5), channel_id=1, source_target_pairs={{0,2},{2,0},{1,3},{3,1},{4,6},{6,4},{5,7},{7,5},{8,10},{10,8},{9,1... | collective-permute-start | bytes 1179656 | tf_op jit(solution)/shard_map/ppermute | solution.py:345
  17.5 3.5 %collective-permute-start.2 = (f32[32,2048]{1,0:T(8,128)}, f32[32,2048]{1,0:T(8,128)S(1)}, u32[]{:S(2)}, u32[]{:S(2)}) collective-permute-start(f32[32,2048]{1,0:T(8,128)} %refs_5_.1), channel_id=1, source_target_pairs={{0,4},{4,0},{1,5},{5,1},{2,6},{6,2},{3,7},{7,3},{8,12},{12,8},{9,1... | collective-permute-start | bytes 786440 | tf_op jit(solution)/shard_map/ppermute | solution.py:345
  21.0 15.7 %collective-permute-start.1 = (f32[32,2048]{1,0:T(8,128)}, f32[32,2048]{1,0:T(8,128)S(1)}, u32[]{:S(2)}, u32[]{:S(2)}) collective-permute-start(f32[32,2048]{1,0:T(8,128)} %refs_5_.1), channel_id=1, source_target_pairs={{0,504},{8,16},{16,8},{24,32},{32,24},{40,48},{48,40},{56,64},{64,... | collective-permute-start | bytes 786440 | tf_op jit(solution)/shard_map/ppermute | solution.py:365
  36.7 1.9 %collective-permute-start = (f32[32,2048]{1,0:T(8,128)}, f32[32,2048]{1,0:T(8,128)S(1)}, u32[]{:S(2)}, u32[]{:S(2)}) collective-permute-start(f32[32,2048]{1,0:T(8,128)} %refs_5_.1), channel_id=1, source_target_pairs={{0,8},{8,0},{16,24},{24,16},{32,40},{40,32},{48,56},{56,48},{64,72... | collective-permute-start | bytes 786440 | tf_op jit(solution)/shard_map/ppermute | solution.py:364
  38.6 2.2 %collective-permute-start.3 = (f32[32,2048]{1,0:T(8,128)}, f32[32,2048]{1,0:T(8,128)S(1)}, u32[]{:S(2)}, u32[]{:S(2)}) collective-permute-start(f32[32,2048]{1,0:T(8,128)} %refs_5_.1), channel_id=1, source_target_pairs={{0,508},{4,8},{8,4},{12,16},{16,12},{20,24},{24,20},{28,32},{32,28... | collective-permute-start | bytes 786440 | tf_op jit(solution)/shard_map/ppermute | solution.py:370
  41.5 4.7 %collective-permute-start.7 = (f32[12,128,128]{2,1,0:T(8,128)S(1)}, f32[12,128,128]{2,1,0:T(8,128)S(1)}, u32[]{:S(2)}, u32[]{:S(2)}) collective-permute-start(f32[12,128,128]{2,1,0:T(8,128)S(1)} %constant_dynamic-update-slice_fusion.pair), channel_id=1, source_target_pairs={{0,1},{1,0},{2,3},{3,2},{4,5},{5,4},{6,7},{7,6},{8,9},{9,8},{10,11... | collective-permute-start | bytes 2359304 | tf_op jit(solution)/shard_map/ppermute | solution.py:345
  47.0 3.5 %own.1 = (bf16[24,2,128,128]{3,2,1,0:T(8,128)(2,1)S(1)}, s32[76]{0:T(128)S(1)}) custom-call(s32[3]{0:T(128)S(1)} %pad_add_fusion.ids.refs_0_, s32[24]{0:T(128)} %refs_1_.1, s32[24]{0:T(128)} %refs_2_.1, s32[1]{0:T(128)S(6)} %copy.10.count.refs_3_, f32[24,128,128]{2,1,0:T(8,128)} %tiles.1), custom_call_target="tpu_custom_call" | custom-call | bytes 6291456 | tf_op jit(solution)/shard_map/own/pallas_call | solution.py:376
  51.6 1.1 shard_map.68
  52.8 5.1 %collective-permute-start.4 = (f32[17,16,128]{2,1,0:T(8,128)S(1)}, f32[17,16,128]{2,1,0:T(8,128)S(1)}, u32[]{:S(2)}, u32[]{:S(2)}) collective-permute-start(f32[17,16,128]{2,1,0:T(8,128)S(1)} %get-tuple-element.15), channel_id=1, source_target_pairs={{0,4},{4,0},{1,5},{5,1},{2,6},{6,2},{3,7},{7,3},{8,12},{12,8},{9,1... | collective-permute-start | bytes 417800 | tf_op jit(solution)/shard_map/ppermute | solution.py:345
  57.9 2.4 %collective-permute-done.4 = f32[17,16,128]{2,1,0:T(8,128)S(1)} collective-permute-done((f32[17,16,128]{2,1,0:T(8,128)S(1)}, f32[17,16,128]{2,1,0:T(8,128)S(1)}, u32[]{:S(2)}, u32[]{:S(2)}) %collective-permute-start.4) | collective-permute-done | bytes 139296 | tf_op jit(solution)/shard_map/ppermute | solution.py:345
  60.3 6.7 %collective-permute-start.9 = (f32[32,16,128]{2,1,0:T(8,128)S(1)}, f32[32,16,128]{2,1,0:T(8,128)S(1)}, u32[]{:S(2)}, u32[]{:S(2)}) collective-permute-start(f32[32,16,128]{2,1,0:T(8,128)S(1)} %pad_maximum_fusion.1.refs_2_.refs_4_), channel_id=1, source_target_pairs={{0,504},{8,16},{16,8},{24,32},{32,24},{40,48},{48,40},{56,64},{64,... | collective-permute-start | bytes 786440 | tf_op jit(solution)/shard_map/ppermute | solution.py:365
  67.1 1.9 %collective-permute-start.8 = (f32[32,16,128]{2,1,0:T(8,128)S(1)}, f32[32,16,128]{2,1,0:T(8,128)S(1)}, u32[]{:S(2)}, u32[]{:S(2)}) collective-permute-start(f32[32,16,128]{2,1,0:T(8,128)S(1)} %pad_maximum_fusion.1.refs_2_.refs_4_), channel_id=1, source_target_pairs={{0,8},{8,0},{16,24},{24,16},{32,40},{40,32},{48,56},{56,48},{64,72... | collective-permute-start | bytes 786440 | tf_op jit(solution)/shard_map/ppermute | solution.py:364
  69.1 2.5 %other.1 = (bf16[24,2,128,128]{3,2,1,0:T(8,128)(2,1)S(1)}, s32[76]{0:T(128)S(1)}) custom-call(s32[3]{0:T(128)S(1)} %pad_add_fusion.ids.refs_0_, f32[3,24]{1,0:T(4,128)S(1)} %slice_bitcast_fusion.notes, f32[12,128,128]{2,1,0:T(8,128)S(1)} %constant_dynamic-update-slice_fusion.pair, f32[12,128,128]{2,1,0:T(8,128)S(1)} %collective-permute-done.7.far), custom_call_target="tpu_custom_call" | custom-call | bytes 6291456 | tf_op jit(solution)/shard_map/other/pallas_call | solution.py:426
  73.6 2.4 %collective-permute-done.8.refs_2_ = f32[32,16,128]{2,1,0:T(8,128)S(1)} collective-permute-done((f32[32,16,128]{2,1,0:T(8,128)S(1)}, f32[32,16,128]{2,1,0:T(8,128)S(1)}, u32[]{:S(2)}, u32[]{:S(2)}) %collective-permute-start.8) | collective-permute-done | bytes 262176 | tf_op jit(solution)/shard_map/ppermute | solution.py:364
  77.0 4.6 %collective-permute-start.11 = (f32[32,16,128]{2,1,0:T(8,128)S(1)}, f32[32,16,128]{2,1,0:T(8,128)S(1)}, u32[]{:S(2)}, u32[]{:S(2)}) collective-permute-start(f32[32,16,128]{2,1,0:T(8,128)S(1)} %shard_map.71.refs_2_.refs_4_), channel_id=1, source_target_pairs={{0,504},{8,16},{16,8},{24,32},{32,24},{40,48},{48,40},{56,64},{64,... | collective-permute-start | bytes 786440 | tf_op jit(solution)/shard_map/ppermute | solution.py:365
  81.7 1.9 %collective-permute-start.10 = (f32[32,16,128]{2,1,0:T(8,128)S(1)}, f32[32,16,128]{2,1,0:T(8,128)S(1)}, u32[]{:S(2)}, u32[]{:S(2)}) collective-permute-start(f32[32,16,128]{2,1,0:T(8,128)S(1)} %shard_map.71.refs_2_.refs_4_), channel_id=1, source_target_pairs={{0,8},{8,0},{16,24},{24,16},{32,40},{40,32},{48,56},{56,48},{64,72... | collective-permute-start | bytes 786440 | tf_op jit(solution)/shard_map/ppermute | solution.py:364
  84.6 3.8 %collective-permute-done.11.refs_2_ = f32[32,16,128]{2,1,0:T(8,128)S(1)} collective-permute-done((f32[32,16,128]{2,1,0:T(8,128)S(1)}, f32[32,16,128]{2,1,0:T(8,128)S(1)}, u32[]{:S(2)}, u32[]{:S(2)}) %collective-permute-start.11) | collective-permute-done | bytes 262176 | tf_op jit(solution)/shard_map/ppermute | solution.py:365
  89.7 1.0 shard_map.74.refs_2_
  90.7 4.6 %collective-permute-start.13 = (f32[32,16,128]{2,1,0:T(8,128)S(1)}, f32[32,16,128]{2,1,0:T(8,128)S(1)}, u32[]{:S(2)}, u32[]{:S(2)}) collective-permute-start(f32[32,16,128]{2,1,0:T(8,128)S(1)} %shard_map.74.refs_2_), channel_id=1, source_target_pairs={{0,504},{8,16},{16,8},{24,32},{32,24},{40,48},{48,40},{56,64},{64,... | collective-permute-start | bytes 786440 | tf_op jit(solution)/shard_map/ppermute | solution.py:365
  95.3 1.9 %collective-permute-start.12 = (f32[32,16,128]{2,1,0:T(8,128)S(1)}, f32[32,16,128]{2,1,0:T(8,128)S(1)}, u32[]{:S(2)}, u32[]{:S(2)}) collective-permute-start(f32[32,16,128]{2,1,0:T(8,128)S(1)} %shard_map.74.refs_2_), channel_id=1, source_target_pairs={{0,8},{8,0},{16,24},{24,16},{32,40},{40,32},{48,56},{56,48},{64,72... | collective-permute-start | bytes 786440 | tf_op jit(solution)/shard_map/ppermute | solution.py:364
  98.3 2.9 %collective-permute-done.13.refs_2_ = f32[32,16,128]{2,1,0:T(8,128)S(1)} collective-permute-done((f32[32,16,128]{2,1,0:T(8,128)S(1)}, f32[32,16,128]{2,1,0:T(8,128)S(1)}, u32[]{:S(2)}, u32[]{:S(2)}) %collective-permute-start.13) | collective-permute-done | bytes 262176 | tf_op jit(solution)/shard_map/ppermute | solution.py:365
  102.8 1.0 shard_map.77
  103.8 13.7 %all_to_all.24.parts_ref = f32[8,4,16,128]{3,2,1,0:T(8,128)S(1)} all-to-all(f32[8,4,16,128]{3,2,1,0:T(8,128)S(1)} %bitcast.13), channel_id=1, replica_groups=mesh['q'=64,'xh'=2,'xl'=2,'core'=2] {'xh','xl','core'}, dimensions={0} | all-to-all | bytes 524288 | tf_op jit(solution)/shard_map/all_to_all | solution.py:349
  117.9 2.2 %collective-permute-start.14 = (f32[128,512]{1,0:T(8,128)S(1)}, f32[128,512]{1,0:T(8,128)S(1)}, u32[]{:S(2)}, u32[]{:S(2)}) collective-permute-start(f32[128,512]{1,0:T(8,128)S(1)} %get-tuple-element.21.refs_0_), channel_id=1, source_target_pairs={{0,2},{2,0},{1,3},{3,1},{4,6},{6,4},{5,7},{7,5},{8,10},{10,8},{9,1... | collective-permute-start | bytes 786440 | tf_op jit(solution)/shard_map/ppermute | solution.py:345
  120.1 6.5 %collective-permute-done.14.refs_1_ = f32[128,512]{1,0:T(8,128)S(1)} collective-permute-done((f32[128,512]{1,0:T(8,128)S(1)}, f32[128,512]{1,0:T(8,128)S(1)}, u32[]{:S(2)}, u32[]{:S(2)}) %collective-permute-start.14) | collective-permute-done | bytes 262176 | tf_op jit(solution)/shard_map/ppermute | solution.py:345
  126.6 3.8 %collective-permute-start.15 = (f32[256,512]{1,0:T(8,128)S(1)}, f32[256,512]{1,0:T(8,128)S(1)}, u32[]{:S(2)}, u32[]{:S(2)}) collective-permute-start(f32[256,512]{1,0:T(8,128)S(1)} %pad_maximum_fusion), channel_id=1, source_target_pairs={{0,1},{1,0},{2,3},{3,2},{4,5},{5,4},{6,7},{7,6},{8,9},{9,8},{10,11... | collective-permute-start | bytes 1572872 | tf_op jit(solution)/shard_map/ppermute | solution.py:345
  130.5 16.1 %all_to_all.25 = f32[64,2,128]{2,1,0:T(2,128)S(1)} all-to-all(f32[64,2,128]{2,1,0:T(2,128)S(1)} %bitcast.15), channel_id=1, replica_groups=mesh['q'=64,'xh'=2,'xl'=2,'core'=2] {'q'}, dimensions={0} | all-to-all | bytes 131072 | tf_op jit(solution)/shard_map/all_to_all | solution.py:349
  146.7 8.4 %all_to_all.26 = f32[8,2,128]{2,1,0:T(2,128)S(1)} all-to-all(f32[8,2,128]{2,1,0:T(2,128)S(1)} %broadcast_in_dim.34), channel_id=1, replica_groups=mesh['q'=64,'xh'=2,'xl'=2,'core'=2] {'xh','xl','core'}, dimensions={0} | all-to-all | bytes 16384 | tf_op jit(solution)/shard_map/all_to_all | solution.py:349
  155.1 15.0 %all_to_all.27 = f32[64,2,128]{2,1,0:T(2,128)S(1)} all-to-all(f32[64,2,128]{2,1,0:T(2,128)S(1)} %broadcast_in_dim.35), channel_id=1, replica_groups=mesh['q'=64,'xh'=2,'xl'=2,'core'=2] {'q'}, dimensions={0} | all-to-all | bytes 131072 | tf_op jit(solution)/shard_map/all_to_all | solution.py:349
  170.1 8.5 %shard_map.79 = (f32[128,128]{1,0:T(8,128)}, f32[32,2048]{1,0:T(8,128)}) custom-call(s32[1]{0:T(128)} %bitcast.place_ref, f32[128,128]{1,0:T(8,128)S(1)} %bitcast.14, f32[128,512]{1,0:T(8,128)S(1)} %get-tuple-element.21.refs_0_, f32[128,512]{1,0:T(8,128)S(1)} %collective-permute-done.14.refs_1_, f32[256,512]{1,0:T(8,128)S(1)} %collective-permute-done.15.refs_2_), custom_call_target="tpu_custom_call" | custom-call | flops 100663296 | bytes 1048576 | tf_op jit(solution)/shard_map/pallas_call | solution.py:43
  (40 shorter events, 11.6 us)
Async XLA Ops:
  1.7 10.4 %collective-permute-start.5 = (f32[6,128,128]{2,1,0:T(8,128)S(1)}, f32[6,128,128]{2,1,0:T(8,128)S(1)}, u32[]{:S(2)}, u32[]{:S(2)}) collective-permute-start(f32[6,128,128]{2,1,0:T(8,128)S(1)} %constant_dynamic-slice_fusion), channel_id=1, source_target_pairs={{0,6},{2,4},{4,2},{6,0},{1,7},{3,5},{5,3},{7,1},{8,14},{10,12},{12... | collective-permute-start | bytes 1179656 | tf_op jit(solution)/shard_map/ppermute | solution.py:391
  12.1 29.4 %collective-permute-start.6 = (f32[6,128,128]{2,1,0:T(8,128)S(1)}, f32[6,128,128]{2,1,0:T(8,128)S(1)}, u32[]{:S(2)}, u32[]{:S(2)}) collective-permute-start(f32[6,128,128]{2,1,0:T(8,128)S(1)} %collective-permute-done.5), channel_id=1, source_target_pairs={{0,2},{2,0},{1,3},{3,1},{4,6},{6,4},{5,7},{7,5},{8,10},{10,8},{9,1... | collective-permute-start | bytes 1179656 | tf_op jit(solution)/shard_map/ppermute | solution.py:345
  17.5 33.1 %collective-permute-start.2 = (f32[32,2048]{1,0:T(8,128)}, f32[32,2048]{1,0:T(8,128)S(1)}, u32[]{:S(2)}, u32[]{:S(2)}) collective-permute-start(f32[32,2048]{1,0:T(8,128)} %refs_5_.1), channel_id=1, source_target_pairs={{0,4},{4,0},{1,5},{5,1},{2,6},{6,2},{3,7},{7,3},{8,12},{12,8},{9,1... | collective-permute-start | bytes 786440 | tf_op jit(solution)/shard_map/ppermute | solution.py:345
  21.0 29.6 %collective-permute-start.1 = (f32[32,2048]{1,0:T(8,128)}, f32[32,2048]{1,0:T(8,128)S(1)}, u32[]{:S(2)}, u32[]{:S(2)}) collective-permute-start(f32[32,2048]{1,0:T(8,128)} %refs_5_.1), channel_id=1, source_target_pairs={{0,504},{8,16},{16,8},{24,32},{32,24},{40,48},{48,40},{56,64},{64,... | collective-permute-start | bytes 786440 | tf_op jit(solution)/shard_map/ppermute | solution.py:365
  36.7 14.0 %collective-permute-start = (f32[32,2048]{1,0:T(8,128)}, f32[32,2048]{1,0:T(8,128)S(1)}, u32[]{:S(2)}, u32[]{:S(2)}) collective-permute-start(f32[32,2048]{1,0:T(8,128)} %refs_5_.1), channel_id=1, source_target_pairs={{0,8},{8,0},{16,24},{24,16},{32,40},{40,32},{48,56},{56,48},{64,72... | collective-permute-start | bytes 786440 | tf_op jit(solution)/shard_map/ppermute | solution.py:364
  38.6 13.1 %collective-permute-start.3 = (f32[32,2048]{1,0:T(8,128)}, f32[32,2048]{1,0:T(8,128)S(1)}, u32[]{:S(2)}, u32[]{:S(2)}) collective-permute-start(f32[32,2048]{1,0:T(8,128)} %refs_5_.1), channel_id=1, source_target_pairs={{0,508},{4,8},{8,4},{12,16},{16,12},{20,24},{24,20},{28,32},{32,28... | collective-permute-start | bytes 786440 | tf_op jit(solution)/shard_map/ppermute | solution.py:370
  41.5 10.2 %copy-start = (f32[32,2048]{1,0:T(8,128)S(1)}, f32[32,2048]{1,0:T(8,128)}, u32[]{:S(2)}) copy-start(f32[32,2048]{1,0:T(8,128)} %refs_5_.1) | copy-start | bytes 786436
  41.5 10.2 %copy-start.1 = (s32[24]{0:T(128)S(1)}, s32[24]{0:T(128)}, u32[]{:S(2)}) copy-start(s32[24]{0:T(128)} %refs_1_.1) | copy-start | bytes 292
  41.5 10.2 %copy-start.2 = (s32[24]{0:T(128)S(1)}, s32[24]{0:T(128)}, u32[]{:S(2)}) copy-start(s32[24]{0:T(128)} %refs_2_.1) | copy-start | bytes 292
  41.5 27.5 %collective-permute-start.7 = (f32[12,128,128]{2,1,0:T(8,128)S(1)}, f32[12,128,128]{2,1,0:T(8,128)S(1)}, u32[]{:S(2)}, u32[]{:S(2)}) collective-permute-start(f32[12,128,128]{2,1,0:T(8,128)S(1)} %constant_dynamic-update-slice_fusion.pair), channel_id=1, source_target_pairs={{0,1},{1,0},{2,3},{3,2},{4,5},{5,4},{6,7},{7,6},{8,9},{9,8},{10,11... | collective-permute-start | bytes 2359304 | tf_op jit(solution)/shard_map/ppermute | solution.py:345
  52.8 7.5 %collective-permute-start.4 = (f32[17,16,128]{2,1,0:T(8,128)S(1)}, f32[17,16,128]{2,1,0:T(8,128)S(1)}, u32[]{:S(2)}, u32[]{:S(2)}) collective-permute-start(f32[17,16,128]{2,1,0:T(8,128)S(1)} %get-tuple-element.15), channel_id=1, source_target_pairs={{0,4},{4,0},{1,5},{5,1},{2,6},{6,2},{3,7},{7,3},{8,12},{12,8},{9,1... | collective-permute-start | bytes 417800 | tf_op jit(solution)/shard_map/ppermute | solution.py:345
  60.3 12.2 %collective-permute-start.9 = (f32[32,16,128]{2,1,0:T(8,128)S(1)}, f32[32,16,128]{2,1,0:T(8,128)S(1)}, u32[]{:S(2)}, u32[]{:S(2)}) collective-permute-start(f32[32,16,128]{2,1,0:T(8,128)S(1)} %pad_maximum_fusion.1.refs_2_.refs_4_), channel_id=1, source_target_pairs={{0,504},{8,16},{16,8},{24,32},{32,24},{40,48},{48,40},{56,64},{64,... | collective-permute-start | bytes 786440 | tf_op jit(solution)/shard_map/ppermute | solution.py:365
  67.1 8.9 %collective-permute-start.8 = (f32[32,16,128]{2,1,0:T(8,128)S(1)}, f32[32,16,128]{2,1,0:T(8,128)S(1)}, u32[]{:S(2)}, u32[]{:S(2)}) collective-permute-start(f32[32,16,128]{2,1,0:T(8,128)S(1)} %pad_maximum_fusion.1.refs_2_.refs_4_), channel_id=1, source_target_pairs={{0,8},{8,0},{16,24},{24,16},{32,40},{40,32},{48,56},{56,48},{64,72... | collective-permute-start | bytes 786440 | tf_op jit(solution)/shard_map/ppermute | solution.py:364
  77.0 11.4 %collective-permute-start.11 = (f32[32,16,128]{2,1,0:T(8,128)S(1)}, f32[32,16,128]{2,1,0:T(8,128)S(1)}, u32[]{:S(2)}, u32[]{:S(2)}) collective-permute-start(f32[32,16,128]{2,1,0:T(8,128)S(1)} %shard_map.71.refs_2_.refs_4_), channel_id=1, source_target_pairs={{0,504},{8,16},{16,8},{24,32},{32,24},{40,48},{48,40},{56,64},{64,... | collective-permute-start | bytes 786440 | tf_op jit(solution)/shard_map/ppermute | solution.py:365
  81.7 8.0 %collective-permute-start.10 = (f32[32,16,128]{2,1,0:T(8,128)S(1)}, f32[32,16,128]{2,1,0:T(8,128)S(1)}, u32[]{:S(2)}, u32[]{:S(2)}) collective-permute-start(f32[32,16,128]{2,1,0:T(8,128)S(1)} %shard_map.71.refs_2_.refs_4_), channel_id=1, source_target_pairs={{0,8},{8,0},{16,24},{24,16},{32,40},{40,32},{48,56},{56,48},{64,72... | collective-permute-start | bytes 786440 | tf_op jit(solution)/shard_map/ppermute | solution.py:364
  90.7 10.4 %collective-permute-start.13 = (f32[32,16,128]{2,1,0:T(8,128)S(1)}, f32[32,16,128]{2,1,0:T(8,128)S(1)}, u32[]{:S(2)}, u32[]{:S(2)}) collective-permute-start(f32[32,16,128]{2,1,0:T(8,128)S(1)} %shard_map.74.refs_2_), channel_id=1, source_target_pairs={{0,504},{8,16},{16,8},{24,32},{32,24},{40,48},{48,40},{56,64},{64,... | collective-permute-start | bytes 786440 | tf_op jit(solution)/shard_map/ppermute | solution.py:365
  95.3 7.4 %collective-permute-start.12 = (f32[32,16,128]{2,1,0:T(8,128)S(1)}, f32[32,16,128]{2,1,0:T(8,128)S(1)}, u32[]{:S(2)}, u32[]{:S(2)}) collective-permute-start(f32[32,16,128]{2,1,0:T(8,128)S(1)} %shard_map.74.refs_2_), channel_id=1, source_target_pairs={{0,8},{8,0},{16,24},{24,16},{32,40},{40,32},{48,56},{56,48},{64,72... | collective-permute-start | bytes 786440 | tf_op jit(solution)/shard_map/ppermute | solution.py:364
  117.9 8.7 %collective-permute-start.14 = (f32[128,512]{1,0:T(8,128)S(1)}, f32[128,512]{1,0:T(8,128)S(1)}, u32[]{:S(2)}, u32[]{:S(2)}) collective-permute-start(f32[128,512]{1,0:T(8,128)S(1)} %get-tuple-element.21.refs_0_), channel_id=1, source_target_pairs={{0,2},{2,0},{1,3},{3,1},{4,6},{6,4},{5,7},{7,5},{8,10},{10,8},{9,1... | collective-permute-start | bytes 786440 | tf_op jit(solution)/shard_map/ppermute | solution.py:345
  126.6 43.5 %collective-permute-start.15 = (f32[256,512]{1,0:T(8,128)S(1)}, f32[256,512]{1,0:T(8,128)S(1)}, u32[]{:S(2)}, u32[]{:S(2)}) collective-permute-start(f32[256,512]{1,0:T(8,128)S(1)} %pad_maximum_fusion), channel_id=1, source_target_pairs={{0,1},{1,0},{2,3},{3,2},{4,5},{5,4},{6,7},{7,6},{8,9},{9,8},{10,11... | collective-permute-start | bytes 1572872 | tf_op jit(solution)/shard_map/ppermute | solution.py:345

commit v7 on v6

--- a/solution.py
+++ b/solution.py
@@ -59,18 +59,18 @@
         row, column, place = slot_of(slot)
         owner = column >> 4
         step = lax.rem((owner >> 1) - q + 1 + count_q, count_q)
-        near = (step == 2) == ((q & 1) == 0)
-        piece = jnp.where(step == 1, 0, jnp.where(near, 2, 1))
-        local = ((owner & 1) ^ xh) * RB_DEV + (column & (RB_DEV - 1))
-        fill = jnp.where(piece == 0, fills[0], jnp.where(piece == 1, fills[1], fills[2]))
-        lists[piece * TILE_CAP + fill] = row + HALF * local + HALF * HALF * place
-        return tuple(fills[k] + (piece == k).astype(jnp.int32) for k in range(3))
+        far = (step != 1).astype(jnp.int32)
+        even = jnp.where((step == 2) == ((q & 1) == 0), far, 0)
+        local = even * HALF + ((owner & 1) ^ xh) * RB_DEV + (column & (RB_DEV - 1))
+        fill = jnp.where(far == 1, fills[1], fills[0])
+        lists[far * TILE_CAP + fill] = row + HALF * local + 2 * HALF * HALF * place
+        return fills[0] + 1 - far, fills[1] + far
 
     zero = jnp.int32(0)
-    fills = lax.fori_loop(0, live, body, (zero, zero, zero))
-    for k in range(3):
-        lists[3 * TILE_CAP + k] = fills[k]
-    lists[3 * TILE_CAP + 3] = xh * RB_DEV
+    fills = lax.fori_loop(0, live, body, (zero, zero))
+    for k in range(2):
+        lists[2 * TILE_CAP + k] = fills[k]
+    lists[2 * TILE_CAP + 2] = xh * RB_DEV
 
 
 def split_into(value, out_ref, slot):
@@ -101,7 +101,7 @@
         lax.fori_loop(k * chunk, (k + 1) * chunk, body, 0, unroll=2)
 
 
-def other_kernel(count_q, ids, notes, pair, far, split_ref, lists):
+def partner_kernel(count_q, ids, notes, lists):
     quarter = TILE_CAP // 4
 
     def slot_of(slot):
@@ -112,12 +112,16 @@
         return row, notes[1, slot].astype(jnp.int32), order * quarter + slot - part * quarter
 
     sort_slots(ids, count_q, notes[2, 0].astype(jnp.int32), slot_of, lists)
-    for base, piece in ((0, pair), (2 * quarter, far)):
-        def body(slot, carry, base=base, piece=piece):
-            split_into(piece[slot], split_ref, base + slot)
+
+
+def other_kernel(pair, far, split_ref):
+    quarter = TILE_CAP // 4
+    for k, (piece, start) in enumerate(((pair, 0), (pair, quarter + 1), (far, 0), (far, quarter + 1))):
+        def body(slot, carry, k=k, piece=piece, start=start):
+            split_into(piece[start + slot], split_ref, k * quarter + slot)
             return carry
 
-        lax.fori_loop(0, 2 * quarter, body, 0, unroll=2)
+        lax.fori_loop(0, quarter, body, 0, unroll=2)
 
 
 def dot_t(left, right, precision=None):
@@ -130,46 +134,48 @@
     )
 
 
-def part_kernel(piece, final, *refs):
-    own_list, other_list, source_ref, *middle, own_ref, other_ref, out_ref, window, total = refs
-
-    def fill(block, carry):
-        high, low = split_bf16(source_ref[block])
-        window[block, 0:COLS] = high
-        window[block, COLS : 2 * COLS] = low
-        return carry
-
-    lax.fori_loop(0, HALF, fill, 0, unroll=8)
-    if piece == 0:
+def part_kernel(halos, final, *refs):
+    own_list, other_list, *refs = refs
+    sources, refs = (refs[:2], refs[2:]) if halos else (refs[:1], refs[1:])
+    *middle, own_ref, other_ref, out_ref, window, total = refs
+    for base, source_ref in enumerate(sources):
+        def fill(block, carry, base=base, source_ref=source_ref):
+            high, low = split_bf16(source_ref[block])
+            window[base * HALF + block, 0:COLS] = high
+            window[base * HALF + block, COLS : 2 * COLS] = low
+            return carry
+
+        lax.fori_loop(0, HALF, fill, 0, unroll=8)
+    if halos:
+        total[...] = middle[0][...]
+    else:
         total[...] = jnp.zeros_like(total)
-    else:
-        total[...] = middle[0][...]
-    base = piece * TILE_CAP
+    base = TILE_CAP if halos else 0
     for lists, tiles in ((own_list, own_ref), (other_list, other_ref)):
-        live = lists[3 * TILE_CAP + piece]
+        live = lists[2 * TILE_CAP + int(halos)]
 
         def body(group, carry, lists=lists, tiles=tiles, live=live):
             terms, rows = [], []
             for inner in range(UNROLL):
                 slot = group * UNROLL + inner
                 entry = jnp.where(slot < live, lists[base + slot], 0)
-                both = window[(entry // HALF) % HALF]
-                place = entry // (HALF * HALF)
+                both = window[(entry >> 5) & (2 * HALF - 1)]
+                place = entry >> 11
                 wide = dot_b(both, tiles[place, 0])
                 narrow = dot_b(both[:COLS], tiles[place, 1])
                 term = wide[:COLS] + (wide[COLS:] + narrow)
                 terms.append(jnp.where(slot < live, term, jnp.zeros_like(term)))
-                rows.append(entry % HALF)
+                rows.append(entry & (HALF - 1))
             for inner in range(UNROLL):
                 total[rows[inner]] = total[rows[inner]] + terms[inner]
             return carry
 
         lax.fori_loop(0, (live + UNROLL - 1) // UNROLL, body, 0)
-    if piece < 2:
+    if not halos:
         out_ref[...] = total[...]
         return
     prev_ref = middle[1]
-    swap = own_list[3 * TILE_CAP + 3] if final else 0
+    swap = own_list[2 * TILE_CAP + 2] if final else 0
 
     def finish(block, carry):
         source = block ^ swap if final else block
@@ -186,7 +192,7 @@
 
 
 def first_kernel(count_b, *refs):
-    ids, rows, cols, count, notes_ref, *refs = refs
+    ids, rows, cols, count, *refs = refs
     *pieces, tiles, mine_ref, given_ref, start_ref, window, total = refs
     q, xh = ids[0], ids[1]
 
@@ -229,18 +235,18 @@
         for half, ref in enumerate((pieces[0], pieces[3])):
             value = ref[:, block * BS : (block + 1) * BS]
             start_ref[half * RB_DEV + block] = jnp.where(upper, value[COLS:], value[:COLS])
-    given_ref[RB_DEV] = notes_ref[...]
-
-
-def graph_part(lists, piece, source, middle, own_tiles, other_tiles, final):
-    operands = [*lists, source, *middle, own_tiles, other_tiles]
+
+
+def graph_part(lists, sources, middle, own_tiles, other_tiles, final):
+    halos = len(sources) == 2
+    operands = [*lists, *sources, *middle, own_tiles, other_tiles]
     return call(
-        functools.partial(part_kernel, piece, final),
+        functools.partial(part_kernel, halos, final),
         jax.ShapeDtypeStruct((HALF, COLS, BS), jnp.float32),
         operands,
         [SMEM] * 2 + [VMEM] * (len(operands) - 2),
         scratch=[
-            pltpu.VMEM((HALF, 2 * COLS, BS), jnp.bfloat16),
+            pltpu.VMEM((len(sources) * HALF, 2 * COLS, BS), jnp.bfloat16),
             pltpu.VMEM((HALF, COLS, BS), jnp.float32),
         ],
         flops=2 * TILE_CAP * 2 * COLS * BS * BS,
@@ -329,6 +335,8 @@
     own = place_ref[0]
     count = K // 4
     inverse = work[pl.ds(pl.multiple_of(own * count, count), count), K:] * scale
+    inverse_high, inverse_low = split_bf16(inverse)
+    both = jnp.concatenate([inverse_high, inverse_low], axis=0)
     width = 4 * BS
     mine, second, pair = slices
     for other, value in (
@@ -338,7 +346,10 @@
         (3, pair[K:]),
     ):
         start = pl.multiple_of((own ^ other) * width, width)
-        ortho_ref[:, pl.ds(start, width)] = dot_n(inverse, value)
+        high, low = split_bf16(value)
+        wide = dot_b(both, high)
+        product = wide[:count] + (wide[count:] + dot_b(inverse_high, low))
+        ortho_ref[:, pl.ds(start, width)] = product
 
 
 def exchange(value, axis):
@@ -371,7 +382,7 @@
     across = exchange(start_panel, "xh")
     one, two = halo(start_panel)
     ids = jnp.stack([q, xh, c])
-    order = jax.ShapeDtypeStruct((3 * TILE_CAP + 4,), jnp.int32)
+    order = jax.ShapeDtypeStruct((2 * TILE_CAP + 3,), jnp.int32)
     split = jax.ShapeDtypeStruct((TILE_CAP, 2, BS, BS), jnp.bfloat16)
     own_tiles, own_list = pl.pallas_call(
         functools.partial(own_kernel, count_q),
@@ -388,10 +399,6 @@
         name="own",
     )(ids, in_hbm(tile_rows), in_hbm(tile_cols), tile_counts, in_hbm(tile_values))
     piece = lax.dynamic_slice_in_dim(tile_values, c * quarter, quarter, 0)
-    first = lax.ppermute(piece, ("xh", "xl"), [(i, 3 - i) for i in range(4)])
-    second = exchange(first, "xl")
-    pair = jnp.concatenate([first, second], axis=0)
-    far = exchange(pair, "core")
     notes = jnp.concatenate(
         [
             tile_rows.astype(jnp.float32)[None],
@@ -400,20 +407,25 @@
         ],
         axis=0,
     )
-    notes = jnp.pad(notes, ((0, COLS - 3), (0, BS - TILE_CAP)))
+    notes = jnp.pad(notes, ((0, BS - 3), (0, BS - TILE_CAP)))
+    piece = jnp.concatenate([piece, notes[None]], axis=0)
+    first = lax.ppermute(piece, ("xh", "xl"), [(i, 3 - i) for i in range(4)])
+    second = exchange(first, "xl")
+    pair = jnp.concatenate([first, second], axis=0)
+    far = exchange(pair, "core")
     half = jax.ShapeDtypeStruct((RB_DEV, COLS, BS), jnp.float32)
     mine, given, previous = call(
         functools.partial(first_kernel, count),
         (
             half,
-            jax.ShapeDtypeStruct((RB_DEV + 1, COLS, BS), jnp.float32),
+            half,
             jax.ShapeDtypeStruct((HALF, COLS, BS), jnp.float32),
         ),
         [
             ids, tile_rows, tile_cols, tile_counts,
-            notes, start_panel, one, two, across, diagonal, own_tiles,
+            start_panel, one, two, across, diagonal, own_tiles,
         ],
-        [SMEM] * 4 + [VMEM] * 7,
+        [SMEM] * 4 + [VMEM] * 6,
         scratch=[
             pltpu.VMEM((5 * RB_DEV, 4 * COLS, BS), jnp.bfloat16),
             pltpu.VMEM((RB_DEV, 2 * COLS, BS), jnp.float32),
@@ -422,25 +434,22 @@
         moved=4 << 20,
     )
     got = exchange(given, "xh")
-    current = jnp.concatenate([mine, got[:RB_DEV]], axis=0)
-    other_tiles, other_list = pl.pallas_call(
-        functools.partial(other_kernel, count_q),
-        out_shape=(split, order),
-        in_specs=[SMEM] * 2 + [VMEM] * 2,
-        out_specs=(VMEM, SMEM),
-        compiler_params=pltpu.CompilerParams(vmem_limit_bytes=24 << 20),
-        cost_estimate=pl.CostEstimate(flops=0, bytes_accessed=6 << 20, transcendentals=0),
+    current = jnp.concatenate([mine, got], axis=0)
+    other_list = pl.pallas_call(
+        functools.partial(partner_kernel, count_q),
+        out_shape=order,
+        in_specs=[SMEM] * 2,
+        out_specs=SMEM,
         interpret=INTERPRET,
-        name="other",
-    )(ids, got[RB_DEV, :3, :TILE_CAP], pair, far)
+        name="partner",
+    )(ids, first[quarter, :3, :TILE_CAP])
+    other_tiles = call(other_kernel, split, [pair, far], [VMEM] * 2, moved=6 << 20)
     lists = (own_list, other_list)
     for step in range(1, DEGREE):
-        two, one = halo(current)
-        final = step == DEGREE - 1
-        tiles = (own_tiles, other_tiles, final)
-        part = graph_part(lists, 0, current, (), *tiles)
-        part = graph_part(lists, 1, one, (part,), *tiles)
-        upcoming = graph_part(lists, 2, two, (part, previous), *tiles)
+        even_half, odd_half = halo(current)
+        tiles = (own_tiles, other_tiles, step == DEGREE - 1)
+        part = graph_part(lists, (current,), (), *tiles)
+        upcoming = graph_part(lists, (odd_half, even_half), (part, previous), *tiles)
         previous, current = current, upcoming
 
     parts = to_all(current.reshape(8, 4, COLS, BS), GROUP)

time: 179 us -> 198 us (1.11)
  waiting for transfers between devices: 25.1 us -> 43.8 us
  starting transfers between devices: 71.4 us -> 67.2 us
  local copies, waits for them, and re-layouts: 1.22 us -> 4.16 us
    ppermute x6, waiting for transfers between devices: 8.96 us -> 18.1 us  [exchange(): return lax.ppermute(value, axis, [(0, 1), (1, 0)])]
    ppermute x1, waiting for transfers between devices: 1.02 us -> 7.05 us  [filtered_basis(): diagonal = lax.ppermute(start_panel, ('q', 'xh'), near)]
    ppermute x4, starting transfers between devices: 31.7 us -> 26 us  [halo(): two = lax.ppermute(value, 'q', odd)]
    ppermute x4, waiting for transfers between devices: 6.66 us -> 11.3 us  [halo(): two = lax.ppermute(value, 'q', odd)]
    ppermute x4, waiting for transfers between devices: 3.27 us -> 0.75 us  [halo(): one = lax.ppermute(value, 'q', even)]
    pallas_call x12 -> x10, Pallas kernels: 19.2 us -> 19.5 us  [call(): pl.pallas_call(kernel, out_shape=out_shape, in_specs=specs, out_specs=out...]
  transfers between devices with their start and end apart: 16 -> 16, of which waited for: 9 -> 9; matrix products, arithmetic and copies ran while one was open for 1% -> 1% of each run, Pallas kernels for 7% -> 6%
where the time goes in v7:
time: 198 us; the launch traced here: 197 us
  starting transfers between devices  67.2 us (34%)
  blocking collectives  54.8 us (28%)
  waiting for transfers between devices  43.8 us (22%)
  Pallas kernels  24.3 us (12%)
  local copies, waits for them, and re-layouts  4.16 us (2%)
    all_to_all x4, blocking collectives, to_all(): return lax.all_to_all(value, axis, 0, 0, tiled=True)  54.8 us
    ppermute x4, starting transfers between devices, halo(): two = lax.ppermute(value, 'q', odd)  26 us
    ppermute x6, starting transfers between devices, exchange(): return lax.ppermute(value, axis, [(0, 1), (1, 0)])  25.2 us
    pallas_call x10, Pallas kernels, call(): pl.pallas_call(kernel, out_shape=out_shape, in_specs=specs, out_specs=out...  19.5 us
    ppermute x6, waiting for transfers between devices, exchange(): return lax.ppermute(value, axis, [(0, 1), (1, 0)])  18.1 us
    ppermute x4, waiting for transfers between devices, halo(): two = lax.ppermute(value, 'q', odd)  11.3 us
    ppermute x4, starting transfers between devices, halo(): one = lax.ppermute(value, 'q', even)  7.68 us
    ppermute x1, waiting for transfers between devices, filtered_basis(): diagonal = lax.ppermute(start_panel, ('q', 'xh'), near)  7.05 us
  transfers between devices with their start and end apart: 16, of which 9 were waited for; matrix products, arithmetic and copies ran while one was open for 1% of the time, Pallas kernels for 6%

profile of v7, /device:TPU:1, one launch (start us, length us, event | category | flops | bytes accessed | tf_op | source)
XLA Modules:
  0.0 197.0 jit_solution(16728003416570682313)
XLA Ops:
  3.2 5.3 %collective-permute-start = (f32[7,128,128]{2,1,0:T(8,128)S(1)}, f32[7,128,128]{2,1,0:T(8,128)S(1)}, u32[]{:S(2)}, u32[]{:S(2)}) collective-permute-start(f32[7,128,128]{2,1,0:T(8,128)S(1)} %pad_maximum_fusion.1), channel_id=1, source_target_pairs={{0,6},{2,4},{4,2},{6,0},{1,7},{3,5},{5,3},{7,1},{8,14},{10,12},{12... | collective-permute-start | bytes 1376264 | tf_op jit(solution)/shard_map/ppermute | solution.py:412
  8.6 6.6 %collective-permute-done = f32[7,128,128]{2,1,0:T(8,128)S(1)} collective-permute-done((f32[7,128,128]{2,1,0:T(8,128)S(1)}, f32[7,128,128]{2,1,0:T(8,128)S(1)}, u32[]{:S(2)}, u32[]{:S(2)}) %collective-permute-start) | collective-permute-done | bytes 458784 | tf_op jit(solution)/shard_map/ppermute | solution.py:412
  15.1 5.4 %collective-permute-start.8 = (f32[7,128,128]{2,1,0:T(8,128)S(1)}, f32[7,128,128]{2,1,0:T(8,128)S(1)}, u32[]{:S(2)}, u32[]{:S(2)}) collective-permute-start(f32[7,128,128]{2,1,0:T(8,128)S(1)} %collective-permute-done), channel_id=1, source_target_pairs={{0,2},{2,0},{1,3},{3,1},{4,6},{6,4},{5,7},{7,5},{8,10},{10,8},{9,1... | collective-permute-start | bytes 1376264 | tf_op jit(solution)/shard_map/ppermute | solution.py:356
  20.6 7.0 %collective-permute-done.8 = f32[7,128,128]{2,1,0:T(8,128)S(1)} collective-permute-done((f32[7,128,128]{2,1,0:T(8,128)S(1)}, f32[7,128,128]{2,1,0:T(8,128)S(1)}, u32[]{:S(2)}, u32[]{:S(2)}) %collective-permute-start.8) | collective-permute-done | bytes 458784 | tf_op jit(solution)/shard_map/ppermute | solution.py:356
  27.6 6.4 %collective-permute-start.9 = (f32[14,128,128]{2,1,0:T(8,128)S(1)}, f32[14,128,128]{2,1,0:T(8,128)}, u32[]{:S(2)}, u32[]{:S(2)}) collective-permute-start(f32[14,128,128]{2,1,0:T(8,128)S(1)} %constant_dynamic-update-slice_fusion.2.pair), channel_id=1, source_target_pairs={{0,1},{1,0},{2,3},{3,2},{4,5},{5,4},{6,7},{7,6},{8,9},{9,8},{10,11... | collective-permute-start | bytes 2752520 | tf_op jit(solution)/shard_map/ppermute | solution.py:356
  34.1 4.8 %collective-permute-start.3 = (f32[32,2048]{1,0:T(8,128)S(1)}, f32[32,2048]{1,0:T(8,128)S(1)}, u32[]{:S(2)}, u32[]{:S(2)}) collective-permute-start(f32[32,2048]{1,0:T(8,128)S(1)} %copy-done), channel_id=1, source_target_pairs={{0,4},{4,0},{1,5},{5,1},{2,6},{6,2},{3,7},{7,3},{8,12},{12,8},{9,1... | collective-permute-start | bytes 786440 | tf_op jit(solution)/shard_map/ppermute | solution.py:356
  38.9 14.2 %collective-permute-start.2 = (f32[32,2048]{1,0:T(8,128)S(1)}, f32[32,2048]{1,0:T(8,128)S(1)}, u32[]{:S(2)}, u32[]{:S(2)}) collective-permute-start(f32[32,2048]{1,0:T(8,128)S(1)} %copy-done), channel_id=1, source_target_pairs={{0,504},{8,16},{16,8},{24,32},{32,24},{40,48},{48,40},{56,64},{64,... | collective-permute-start | bytes 786440 | tf_op jit(solution)/shard_map/ppermute | solution.py:376
  53.2 1.9 collective-permute-start.1
  55.1 2.9 %collective-permute-start.4 = (f32[32,2048]{1,0:T(8,128)S(1)}, f32[32,2048]{1,0:T(8,128)}, u32[]{:S(2)}, u32[]{:S(2)}) collective-permute-start(f32[32,2048]{1,0:T(8,128)S(1)} %copy-done), channel_id=1, source_target_pairs={{0,508},{4,8},{8,4},{12,16},{16,12},{20,24},{24,20},{28,32},{32,28... | collective-permute-start | bytes 786440 | tf_op jit(solution)/shard_map/ppermute | solution.py:381
  58.1 3.5 %own.1 = (bf16[24,2,128,128]{3,2,1,0:T(8,128)(2,1)S(1)}, s32[51]{0:T(128)S(1)}) custom-call(s32[3]{0:T(128)S(1)} %pad_add_fusion.ids.refs_0_, s32[24]{0:T(128)} %refs_1_.1, s32[24]{0:T(128)} %refs_2_.1, s32[1]{0:T(128)S(6)} %copy.11.count.refs_3_, f32[24,128,128]{2,1,0:T(8,128)} %tiles.1), custom_call_target="tpu_custom_call" | custom-call | bytes 6291456 | tf_op jit(solution)/shard_map/own/pallas_call | solution.py:387
  63.1 7.1 %collective-permute-done.4.refs_8_ = f32[32,2048]{1,0:T(8,128)} collective-permute-done((f32[32,2048]{1,0:T(8,128)S(1)}, f32[32,2048]{1,0:T(8,128)}, u32[]{:S(2)}, u32[]{:S(2)}) %collective-permute-start.4) | collective-permute-done | bytes 262176 | tf_op jit(solution)/shard_map/ppermute | solution.py:381
  71.1 1.5 shard_map.68
  72.6 2.6 %collective-permute-start.5 = (f32[16,16,128]{2,1,0:T(8,128)S(1)}, f32[16,16,128]{2,1,0:T(8,128)S(1)}, u32[]{:S(2)}, u32[]{:S(2)}) collective-permute-start(f32[16,16,128]{2,1,0:T(8,128)S(1)} %get-tuple-element.14), channel_id=1, source_target_pairs={{0,4},{4,0},{1,5},{5,1},{2,6},{6,2},{3,7},{7,3},{8,12},{12,8},{9,1... | collective-permute-start | bytes 393224 | tf_op jit(solution)/shard_map/ppermute | solution.py:356
  75.2 4.6 %collective-permute-done.5 = f32[16,16,128]{2,1,0:T(8,128)S(1)} collective-permute-done((f32[16,16,128]{2,1,0:T(8,128)S(1)}, f32[16,16,128]{2,1,0:T(8,128)S(1)}, u32[]{:S(2)}, u32[]{:S(2)}) %collective-permute-start.5) | collective-permute-done | bytes 131104 | tf_op jit(solution)/shard_map/ppermute | solution.py:356
  79.9 1.9 collective-permute-start.7
  81.8 1.9 collective-permute-start.6
  86.4 2.4 %shard_map.69.refs_4_.refs_7_ = bf16[24,2,128,128]{3,2,1,0:T(8,128)(2,1)S(1)} custom-call(f32[14,128,128]{2,1,0:T(8,128)S(1)} %constant_dynamic-update-slice_fusion.2.pair, f32[14,128,128]{2,1,0:T(8,128)} %collective-permute-done.9.far), custom_call_target="tpu_custom_call" | custom-call | bytes 6291456 | tf_op jit(solution)/shard_map/pallas_call | solution.py:43
  89.9 2.4 %collective-permute-done.6.refs_2_ = f32[32,16,128]{2,1,0:T(8,128)S(1)} collective-permute-done((f32[32,16,128]{2,1,0:T(8,128)S(1)}, f32[32,16,128]{2,1,0:T(8,128)S(1)}, u32[]{:S(2)}, u32[]{:S(2)}) %collective-permute-start.6) | collective-permute-done | bytes 262176 | tf_op jit(solution)/shard_map/ppermute | solution.py:376
  93.5 1.9 collective-permute-start.11
  95.4 4.8 %collective-permute-start.10 = (f32[32,16,128]{2,1,0:T(8,128)S(1)}, f32[32,16,128]{2,1,0:T(8,128)S(1)}, u32[]{:S(2)}, u32[]{:S(2)}) collective-permute-start(f32[32,16,128]{2,1,0:T(8,128)S(1)} %shard_map.71.refs_2_.refs_5_), channel_id=1, source_target_pairs={{0,504},{8,16},{16,8},{24,32},{32,24},{40,48},{48,40},{56,64},{64,... | collective-permute-start | bytes 786440 | tf_op jit(solution)/shard_map/ppermute | solution.py:376
  101.3 4.6 %collective-permute-done.10.refs_2_ = f32[32,16,128]{2,1,0:T(8,128)S(1)} collective-permute-done((f32[32,16,128]{2,1,0:T(8,128)S(1)}, f32[32,16,128]{2,1,0:T(8,128)S(1)}, u32[]{:S(2)}, u32[]{:S(2)}) %collective-permute-start.10) | collective-permute-done | bytes 262176 | tf_op jit(solution)/shard_map/ppermute | solution.py:376
  107.1 1.9 collective-permute-start.13
  109.0 5.0 %collective-permute-start.12 = (f32[32,16,128]{2,1,0:T(8,128)S(1)}, f32[32,16,128]{2,1,0:T(8,128)S(1)}, u32[]{:S(2)}, u32[]{:S(2)}) collective-permute-start(f32[32,16,128]{2,1,0:T(8,128)S(1)} %shard_map.73.refs_2_), channel_id=1, source_target_pairs={{0,504},{8,16},{16,8},{24,32},{32,24},{40,48},{48,40},{56,64},{64,... | collective-permute-start | bytes 786440 | tf_op jit(solution)/shard_map/ppermute | solution.py:376
  115.1 4.4 %collective-permute-done.12.refs_2_ = f32[32,16,128]{2,1,0:T(8,128)S(1)} collective-permute-done((f32[32,16,128]{2,1,0:T(8,128)S(1)}, f32[32,16,128]{2,1,0:T(8,128)S(1)}, u32[]{:S(2)}, u32[]{:S(2)}) %collective-permute-start.12) | collective-permute-done | bytes 262176 | tf_op jit(solution)/shard_map/ppermute | solution.py:376
  120.8 14.9 %all_to_all.24.parts_ref = f32[8,4,16,128]{3,2,1,0:T(8,128)S(1)} all-to-all(f32[8,4,16,128]{3,2,1,0:T(8,128)S(1)} %bitcast.15), channel_id=1, replica_groups=mesh['q'=64,'xh'=2,'xl'=2,'core'=2] {'xh','xl','core'}, dimensions={0} | all-to-all | bytes 524288 | tf_op jit(solution)/shard_map/all_to_all | solution.py:360
  136.1 2.2 %collective-permute-start.14 = (f32[128,512]{1,0:T(8,128)S(1)}, f32[128,512]{1,0:T(8,128)S(1)}, u32[]{:S(2)}, u32[]{:S(2)}) collective-permute-start(f32[128,512]{1,0:T(8,128)S(1)} %get-tuple-element.17.refs_0_), channel_id=1, source_target_pairs={{0,2},{2,0},{1,3},{3,1},{4,6},{6,4},{5,7},{7,5},{8,10},{10,8},{9,1... | collective-permute-start | bytes 786440 | tf_op jit(solution)/shard_map/ppermute | solution.py:356
  138.3 6.5 %collective-permute-done.14.refs_1_ = f32[128,512]{1,0:T(8,128)S(1)} collective-permute-done((f32[128,512]{1,0:T(8,128)S(1)}, f32[128,512]{1,0:T(8,128)S(1)}, u32[]{:S(2)}, u32[]{:S(2)}) %collective-permute-start.14) | collective-permute-done | bytes 262176 | tf_op jit(solution)/shard_map/ppermute | solution.py:356
  144.8 3.8 %collective-permute-start.15 = (f32[256,512]{1,0:T(8,128)S(1)}, f32[256,512]{1,0:T(8,128)S(1)}, u32[]{:S(2)}, u32[]{:S(2)}) collective-permute-start(f32[256,512]{1,0:T(8,128)S(1)} %pad_maximum_fusion), channel_id=1, source_target_pairs={{0,1},{1,0},{2,3},{3,2},{4,5},{5,4},{6,7},{7,6},{8,9},{9,8},{10,11... | collective-permute-start | bytes 1572872 | tf_op jit(solution)/shard_map/ppermute | solution.py:356
  148.6 16.5 %all_to_all.25 = f32[64,2,128]{2,1,0:T(2,128)S(1)} all-to-all(f32[64,2,128]{2,1,0:T(2,128)S(1)} %bitcast.17), channel_id=1, replica_groups=mesh['q'=64,'xh'=2,'xl'=2,'core'=2] {'q'}, dimensions={0} | all-to-all | bytes 131072 | tf_op jit(solution)/shard_map/all_to_all | solution.py:360
  165.2 8.4 %all_to_all.26 = f32[8,2,128]{2,1,0:T(2,128)S(1)} all-to-all(f32[8,2,128]{2,1,0:T(2,128)S(1)} %broadcast_in_dim.38), channel_id=1, replica_groups=mesh['q'=64,'xh'=2,'xl'=2,'core'=2] {'xh','xl','core'}, dimensions={0} | all-to-all | bytes 16384 | tf_op jit(solution)/shard_map/all_to_all | solution.py:360
  173.7 15.0 %all_to_all.27 = f32[64,2,128]{2,1,0:T(2,128)S(1)} all-to-all(f32[64,2,128]{2,1,0:T(2,128)S(1)} %broadcast_in_dim.39), channel_id=1, replica_groups=mesh['q'=64,'xh'=2,'xl'=2,'core'=2] {'q'}, dimensions={0} | all-to-all | bytes 131072 | tf_op jit(solution)/shard_map/all_to_all | solution.py:360
  188.7 8.3 %shard_map.77 = (f32[128,128]{1,0:T(8,128)}, f32[32,2048]{1,0:T(8,128)}) custom-call(s32[1]{0:T(128)} %bitcast.place_ref, f32[128,128]{1,0:T(8,128)S(1)} %bitcast.16, f32[128,512]{1,0:T(8,128)S(1)} %get-tuple-element.17.refs_0_, f32[128,512]{1,0:T(8,128)S(1)} %collective-permute-done.14.refs_1_, f32[256,512]{1,0:T(8,128)S(1)} %collective-permute-done.15.refs_2_), custom_call_target="tpu_custom_call" | custom-call | flops 100663296 | bytes 1048576 | tf_op jit(solution)/shard_map/pallas_call | solution.py:43
  (49 shorter events, 14.5 us)
Async XLA Ops:
  3.1 31.0 %copy-start = (f32[32,2048]{1,0:T(8,128)S(1)}, f32[32,2048]{1,0:T(8,128)}, u32[]{:S(2)}) copy-start(f32[32,2048]{1,0:T(8,128)} %refs_4_.1) | copy-start | bytes 786436
  3.2 66.9 %copy-start.5 = (s32[24]{0:T(128)S(1)}, s32[24]{0:T(128)}, u32[]{:S(2)}) copy-start(s32[24]{0:T(128)} %refs_1_.1) | copy-start | bytes 292
  3.2 66.9 %copy-start.6 = (s32[24]{0:T(128)S(1)}, s32[24]{0:T(128)}, u32[]{:S(2)}) copy-start(s32[24]{0:T(128)} %refs_2_.1) | copy-start | bytes 292
  3.2 11.9 %collective-permute-start = (f32[7,128,128]{2,1,0:T(8,128)S(1)}, f32[7,128,128]{2,1,0:T(8,128)S(1)}, u32[]{:S(2)}, u32[]{:S(2)}) collective-permute-start(f32[7,128,128]{2,1,0:T(8,128)S(1)} %pad_maximum_fusion.1), channel_id=1, source_target_pairs={{0,6},{2,4},{4,2},{6,0},{1,7},{3,5},{5,3},{7,1},{8,14},{10,12},{12... | collective-permute-start | bytes 1376264 | tf_op jit(solution)/shard_map/ppermute | solution.py:412
  15.1 12.5 %copy-start.7 = (f32[7,128,128]{2,1,0:T(8,128)}, f32[7,128,128]{2,1,0:T(8,128)S(1)}, u32[]{:S(2)}) copy-start(f32[7,128,128]{2,1,0:T(8,128)S(1)} %collective-permute-done) | copy-start | bytes 1376260
  15.1 12.5 %collective-permute-start.8 = (f32[7,128,128]{2,1,0:T(8,128)S(1)}, f32[7,128,128]{2,1,0:T(8,128)S(1)}, u32[]{:S(2)}, u32[]{:S(2)}) collective-permute-start(f32[7,128,128]{2,1,0:T(8,128)S(1)} %collective-permute-done), channel_id=1, source_target_pairs={{0,2},{2,0},{1,3},{3,1},{4,6},{6,4},{5,7},{7,5},{8,10},{10,8},{9,1... | collective-permute-start | bytes 1376264 | tf_op jit(solution)/shard_map/ppermute | solution.py:356
  27.6 58.7 %collective-permute-start.9 = (f32[14,128,128]{2,1,0:T(8,128)S(1)}, f32[14,128,128]{2,1,0:T(8,128)}, u32[]{:S(2)}, u32[]{:S(2)}) collective-permute-start(f32[14,128,128]{2,1,0:T(8,128)S(1)} %constant_dynamic-update-slice_fusion.2.pair), channel_id=1, source_target_pairs={{0,1},{1,0},{2,3},{3,2},{4,5},{5,4},{6,7},{7,6},{8,9},{9,8},{10,11... | collective-permute-start | bytes 2752520 | tf_op jit(solution)/shard_map/ppermute | solution.py:356
  34.1 27.5 %collective-permute-start.3 = (f32[32,2048]{1,0:T(8,128)S(1)}, f32[32,2048]{1,0:T(8,128)S(1)}, u32[]{:S(2)}, u32[]{:S(2)}) collective-permute-start(f32[32,2048]{1,0:T(8,128)S(1)} %copy-done), channel_id=1, source_target_pairs={{0,4},{4,0},{1,5},{5,1},{2,6},{6,2},{3,7},{7,3},{8,12},{12,8},{9,1... | collective-permute-start | bytes 786440 | tf_op jit(solution)/shard_map/ppermute | solution.py:356
  38.9 22.7 %collective-permute-start.2 = (f32[32,2048]{1,0:T(8,128)S(1)}, f32[32,2048]{1,0:T(8,128)S(1)}, u32[]{:S(2)}, u32[]{:S(2)}) collective-permute-start(f32[32,2048]{1,0:T(8,128)S(1)} %copy-done), channel_id=1, source_target_pairs={{0,504},{8,16},{16,8},{24,32},{32,24},{40,48},{48,40},{56,64},{64,... | collective-permute-start | bytes 786440 | tf_op jit(solution)/shard_map/ppermute | solution.py:376
  53.2 9.2 %collective-permute-start.1 = (f32[32,2048]{1,0:T(8,128)S(1)}, f32[32,2048]{1,0:T(8,128)S(1)}, u32[]{:S(2)}, u32[]{:S(2)}) collective-permute-start(f32[32,2048]{1,0:T(8,128)S(1)} %copy-done), channel_id=1, source_target_pairs={{0,8},{8,0},{16,24},{24,16},{32,40},{40,32},{48,56},{56,48},{64,72... | collective-permute-start | bytes 786440 | tf_op jit(solution)/shard_map/ppermute | solution.py:375
  55.1 15.0 %collective-permute-start.4 = (f32[32,2048]{1,0:T(8,128)S(1)}, f32[32,2048]{1,0:T(8,128)}, u32[]{:S(2)}, u32[]{:S(2)}) collective-permute-start(f32[32,2048]{1,0:T(8,128)S(1)} %copy-done), channel_id=1, source_target_pairs={{0,508},{4,8},{8,4},{12,16},{16,12},{20,24},{24,20},{28,32},{32,28... | collective-permute-start | bytes 786440 | tf_op jit(solution)/shard_map/ppermute | solution.py:381
  58.1 14.5 %copy-start.4 = (s32[3]{0:T(128)}, s32[3]{0:T(128)S(1)}, u32[]{:S(2)}) copy-start(s32[3]{0:T(128)S(1)} %pad_add_fusion.ids.refs_0_) | copy-start | bytes 40
  62.4 0.7 copy-start.1
  70.1 1.0 copy-start.2
  72.6 7.2 %collective-permute-start.5 = (f32[16,16,128]{2,1,0:T(8,128)S(1)}, f32[16,16,128]{2,1,0:T(8,128)S(1)}, u32[]{:S(2)}, u32[]{:S(2)}) collective-permute-start(f32[16,16,128]{2,1,0:T(8,128)S(1)} %get-tuple-element.14), channel_id=1, source_target_pairs={{0,4},{4,0},{1,5},{5,1},{2,6},{6,2},{3,7},{7,3},{8,12},{12,8},{9,1... | collective-permute-start | bytes 393224 | tf_op jit(solution)/shard_map/ppermute | solution.py:356
  79.9 10.0 %collective-permute-start.7 = (f32[32,16,128]{2,1,0:T(8,128)S(1)}, f32[32,16,128]{2,1,0:T(8,128)S(1)}, u32[]{:S(2)}, u32[]{:S(2)}) collective-permute-start(f32[32,16,128]{2,1,0:T(8,128)S(1)} %constant_dynamic-update-slice_fusion.refs_2_.refs_5_), channel_id=1, source_target_pairs={{0,8},{8,0},{16,24},{24,16},{32,40},{40,32},{48,56},{56,48},{64,72... | collective-permute-start | bytes 786440 | tf_op jit(solution)/shard_map/ppermute | solution.py:375
  81.8 10.4 %collective-permute-start.6 = (f32[32,16,128]{2,1,0:T(8,128)S(1)}, f32[32,16,128]{2,1,0:T(8,128)S(1)}, u32[]{:S(2)}, u32[]{:S(2)}) collective-permute-start(f32[32,16,128]{2,1,0:T(8,128)S(1)} %constant_dynamic-update-slice_fusion.refs_2_.refs_5_), channel_id=1, source_target_pairs={{0,504},{8,16},{16,8},{24,32},{32,24},{40,48},{48,40},{56,64},{64,... | collective-permute-start | bytes 786440 | tf_op jit(solution)/shard_map/ppermute | solution.py:376
  86.4 2.5 %copy-start.3 = (s32[51]{0:T(128)S(1)}, s32[51]{0:T(128)}, u32[]{:S(2)}) copy-start(s32[51]{0:T(128)} %partner.1.refs_1_) | copy-start | bytes 616
  93.5 7.8 %collective-permute-start.11 = (f32[32,16,128]{2,1,0:T(8,128)S(1)}, f32[32,16,128]{2,1,0:T(8,128)S(1)}, u32[]{:S(2)}, u32[]{:S(2)}) collective-permute-start(f32[32,16,128]{2,1,0:T(8,128)S(1)} %shard_map.71.refs_2_.refs_5_), channel_id=1, source_target_pairs={{0,8},{8,0},{16,24},{24,16},{32,40},{40,32},{48,56},{56,48},{64,72... | collective-permute-start | bytes 786440 | tf_op jit(solution)/shard_map/ppermute | solution.py:375
  95.4 10.4 %collective-permute-start.10 = (f32[32,16,128]{2,1,0:T(8,128)S(1)}, f32[32,16,128]{2,1,0:T(8,128)S(1)}, u32[]{:S(2)}, u32[]{:S(2)}) collective-permute-start(f32[32,16,128]{2,1,0:T(8,128)S(1)} %shard_map.71.refs_2_.refs_5_), channel_id=1, source_target_pairs={{0,504},{8,16},{16,8},{24,32},{32,24},{40,48},{48,40},{56,64},{64,... | collective-permute-start | bytes 786440 | tf_op jit(solution)/shard_map/ppermute | solution.py:376
  107.1 8.0 %collective-permute-start.13 = (f32[32,16,128]{2,1,0:T(8,128)S(1)}, f32[32,16,128]{2,1,0:T(8,128)S(1)}, u32[]{:S(2)}, u32[]{:S(2)}) collective-permute-start(f32[32,16,128]{2,1,0:T(8,128)S(1)} %shard_map.73.refs_2_), channel_id=1, source_target_pairs={{0,8},{8,0},{16,24},{24,16},{32,40},{40,32},{48,56},{56,48},{64,72... | collective-permute-start | bytes 786440 | tf_op jit(solution)/shard_map/ppermute | solution.py:375
  109.0 10.4 %collective-permute-start.12 = (f32[32,16,128]{2,1,0:T(8,128)S(1)}, f32[32,16,128]{2,1,0:T(8,128)S(1)}, u32[]{:S(2)}, u32[]{:S(2)}) collective-permute-start(f32[32,16,128]{2,1,0:T(8,128)S(1)} %shard_map.73.refs_2_), channel_id=1, source_target_pairs={{0,504},{8,16},{16,8},{24,32},{32,24},{40,48},{48,40},{56,64},{64,... | collective-permute-start | bytes 786440 | tf_op jit(solution)/shard_map/ppermute | solution.py:376
  136.1 8.7 %collective-permute-start.14 = (f32[128,512]{1,0:T(8,128)S(1)}, f32[128,512]{1,0:T(8,128)S(1)}, u32[]{:S(2)}, u32[]{:S(2)}) collective-permute-start(f32[128,512]{1,0:T(8,128)S(1)} %get-tuple-element.17.refs_0_), channel_id=1, source_target_pairs={{0,2},{2,0},{1,3},{3,1},{4,6},{6,4},{5,7},{7,5},{8,10},{10,8},{9,1... | collective-permute-start | bytes 786440 | tf_op jit(solution)/shard_map/ppermute | solution.py:356
  144.8 43.9 %collective-permute-start.15 = (f32[256,512]{1,0:T(8,128)S(1)}, f32[256,512]{1,0:T(8,128)S(1)}, u32[]{:S(2)}, u32[]{:S(2)}) collective-permute-start(f32[256,512]{1,0:T(8,128)S(1)} %pad_maximum_fusion), channel_id=1, source_target_pairs={{0,1},{1,0},{2,3},{3,2},{4,5},{5,4},{6,7},{7,6},{8,9},{9,8},{10,11... | collective-permute-start | bytes 1572872 | tf_op jit(solution)/shard_map/ppermute | solution.py:356

commit v8 on v7

--- a/solution.py
+++ b/solution.py
@@ -101,8 +101,23 @@
         lax.fori_loop(k * chunk, (k + 1) * chunk, body, 0, unroll=2)
 
 
-def partner_kernel(count_q, ids, notes, lists):
+def cut_kernel(ids, count, rows, cols, tiles, piece_ref, sem):
     quarter = TILE_CAP // 4
+    source = tiles.at[pl.ds(ids[2] * quarter, quarter)]
+    copy = pltpu.make_async_copy(source, piece_ref.at[pl.ds(0, quarter)], sem)
+    copy.start()
+    piece_ref[quarter] = jnp.zeros((BS, BS), jnp.float32)
+    piece_ref[quarter, 0:1, 0:TILE_CAP] = rows[...].astype(jnp.float32)
+    piece_ref[quarter, 1:2, 0:TILE_CAP] = cols[...].astype(jnp.float32)
+    piece_ref[quarter, 2:3, 0:TILE_CAP] = jnp.full((1, TILE_CAP), count[0].astype(jnp.float32))
+    copy.wait()
+
+
+def partner_kernel(count_q, ids, first, lists, notes, sem):
+    quarter = TILE_CAP // 4
+    copy = pltpu.make_async_copy(first.at[quarter, pl.ds(0, 8)], notes, sem)
+    copy.start()
+    copy.wait()
 
     def slot_of(slot):
         row = (notes[0, slot].astype(jnp.int32) & (RB_DEV - 1)) + RB_DEV
@@ -398,17 +413,16 @@
         interpret=INTERPRET,
         name="own",
     )(ids, in_hbm(tile_rows), in_hbm(tile_cols), tile_counts, in_hbm(tile_values))
-    piece = lax.dynamic_slice_in_dim(tile_values, c * quarter, quarter, 0)
-    notes = jnp.concatenate(
-        [
-            tile_rows.astype(jnp.float32)[None],
-            tile_cols.astype(jnp.float32)[None],
-            jnp.broadcast_to(tile_counts.astype(jnp.float32)[None], (1, TILE_CAP)),
-        ],
-        axis=0,
-    )
-    notes = jnp.pad(notes, ((0, BS - 3), (0, BS - TILE_CAP)))
-    piece = jnp.concatenate([piece, notes[None]], axis=0)
+    piece = pl.pallas_call(
+        cut_kernel,
+        out_shape=jax.ShapeDtypeStruct((quarter + 1, BS, BS), jnp.float32),
+        in_specs=[SMEM] * 2 + [VMEM] * 2 + [pl.BlockSpec(memory_space=pltpu.MemorySpace.HBM)],
+        out_specs=VMEM,
+        scratch_shapes=[pltpu.SemaphoreType.DMA],
+        compiler_params=pltpu.CompilerParams(vmem_limit_bytes=24 << 20),
+        interpret=INTERPRET,
+        name="cut",
+    )(ids, tile_counts, in_hbm(tile_rows[None]), in_hbm(tile_cols[None]), in_hbm(tile_values))
     first = lax.ppermute(piece, ("xh", "xl"), [(i, 3 - i) for i in range(4)])
     second = exchange(first, "xl")
     pair = jnp.concatenate([first, second], axis=0)
@@ -438,11 +452,13 @@
     other_list = pl.pallas_call(
         functools.partial(partner_kernel, count_q),
         out_shape=order,
-        in_specs=[SMEM] * 2,
+        in_specs=[SMEM, VMEM],
         out_specs=SMEM,
+        scratch_shapes=[pltpu.SMEM((8, BS), jnp.float32), pltpu.SemaphoreType.DMA],
+        compiler_params=pltpu.CompilerParams(vmem_limit_bytes=24 << 20),
         interpret=INTERPRET,
         name="partner",
-    )(ids, first[quarter, :3, :TILE_CAP])
+    )(ids, first)
     other_tiles = call(other_kernel, split, [pair, far], [VMEM] * 2, moved=6 << 20)
     lists = (own_list, other_list)
     for step in range(1, DEGREE):

time: 198 us -> 196 us (0.990)
  waiting for transfers between devices: 43.8 us -> 50.3 us
  local copies, waits for them, and re-layouts: 4.16 us -> 0.13 us
  starting transfers between devices: 67.2 us -> 63.2 us
    ppermute x4, starting transfers between devices: 26 us -> 22.2 us  [halo(): two = lax.ppermute(value, 'q', odd)]
    ppermute x4, waiting for transfers between devices: 11.3 us -> 14.8 us  [halo(): two = lax.ppermute(value, 'q', odd)]
    ppermute x4, waiting for transfers between devices: 0.75 us -> 3.17 us  [halo(): one = lax.ppermute(value, 'q', even)]
  transfers between devices with their start and end apart: 16 -> 16, of which waited for: 9 -> 11; matrix products, arithmetic and copies ran while one was open for 1% -> 0% of each run, Pallas kernels for 6% -> 6%
where the time goes in v8:
time: 196 us; the launch traced here: 195 us
  starting transfers between devices  63.2 us (32%)
  blocking collectives  54.8 us (28%)
  waiting for transfers between devices  50.3 us (26%)
  Pallas kernels  25.1 us (13%)
    all_to_all x4, blocking collectives, to_all(): return lax.all_to_all(value, axis, 0, 0, tiled=True)  54.8 us
    ppermute x6, starting transfers between devices, exchange(): return lax.ppermute(value, axis, [(0, 1), (1, 0)])  25.2 us
    ppermute x4, starting transfers between devices, halo(): two = lax.ppermute(value, 'q', odd)  22.2 us
    ppermute x6, waiting for transfers between devices, exchange(): return lax.ppermute(value, axis, [(0, 1), (1, 0)])  18.1 us
    pallas_call x10, Pallas kernels, call(): pl.pallas_call(kernel, out_shape=out_shape, in_specs=specs, out_specs=out...  18 us
    ppermute x4, waiting for transfers between devices, halo(): two = lax.ppermute(value, 'q', odd)  14.8 us
    ppermute x4, starting transfers between devices, halo(): one = lax.ppermute(value, 'q', even)  7.68 us
    ppermute x1, waiting for transfers between devices, filtered_basis(): diagonal = lax.ppermute(start_panel, ('q', 'xh'), near)  7.65 us
  transfers between devices with their start and end apart: 16, of which 11 were waited for; matrix products, arithmetic and copies ran while one was open for 0% of the time, Pallas kernels for 6%

profile of v8, /device:TPU:1, one launch (start us, length us, event | category | flops | bytes accessed | tf_op | source)
XLA Modules:
  0.0 195.3 jit_solution(16476729877417422452)
XLA Ops:
  1.4 1.7 cut.1
  3.1 5.2 %collective-permute-start = (f32[7,128,128]{2,1,0:T(8,128)S(1)}, f32[7,128,128]{2,1,0:T(8,128)S(1)}, u32[]{:S(2)}, u32[]{:S(2)}) collective-permute-start(f32[7,128,128]{2,1,0:T(8,128)S(1)} %cut.1), channel_id=1, source_target_pairs={{0,6},{2,4},{4,2},{6,0},{1,7},{3,5},{5,3},{7,1},{8,14},{10,12},{12... | collective-permute-start | bytes 1376264 | tf_op jit(solution)/shard_map/ppermute | solution.py:426
  8.3 6.6 %collective-permute-done.first = f32[7,128,128]{2,1,0:T(8,128)S(1)} collective-permute-done((f32[7,128,128]{2,1,0:T(8,128)S(1)}, f32[7,128,128]{2,1,0:T(8,128)S(1)}, u32[]{:S(2)}, u32[]{:S(2)}) %collective-permute-start) | collective-permute-done | bytes 458784 | tf_op jit(solution)/shard_map/ppermute | solution.py:426
  14.9 5.4 %collective-permute-start.8 = (f32[7,128,128]{2,1,0:T(8,128)S(1)}, f32[7,128,128]{2,1,0:T(8,128)S(1)}, u32[]{:S(2)}, u32[]{:S(2)}) collective-permute-start(f32[7,128,128]{2,1,0:T(8,128)S(1)} %collective-permute-done.first), channel_id=1, source_target_pairs={{0,2},{2,0},{1,3},{3,1},{4,6},{6,4},{5,7},{7,5},{8,10},{10,8},{9,1... | collective-permute-start | bytes 1376264 | tf_op jit(solution)/shard_map/ppermute | solution.py:371
  20.4 7.0 %collective-permute-done.8 = f32[7,128,128]{2,1,0:T(8,128)S(1)} collective-permute-done((f32[7,128,128]{2,1,0:T(8,128)S(1)}, f32[7,128,128]{2,1,0:T(8,128)S(1)}, u32[]{:S(2)}, u32[]{:S(2)}) %collective-permute-start.8) | collective-permute-done | bytes 458784 | tf_op jit(solution)/shard_map/ppermute | solution.py:371
  27.4 6.4 %collective-permute-start.9 = (f32[14,128,128]{2,1,0:T(8,128)S(1)}, f32[14,128,128]{2,1,0:T(8,128)S(1)}, u32[]{:S(2)}, u32[]{:S(2)}) collective-permute-start(f32[14,128,128]{2,1,0:T(8,128)S(1)} %constant_dynamic-update-slice_fusion.2.pair), channel_id=1, source_target_pairs={{0,1},{1,0},{2,3},{3,2},{4,5},{5,4},{6,7},{7,6},{8,9},{9,8},{10,11... | collective-permute-start | bytes 2752520 | tf_op jit(solution)/shard_map/ppermute | solution.py:371
  33.9 4.8 %collective-permute-start.3 = (f32[32,2048]{1,0:T(8,128)S(1)}, f32[32,2048]{1,0:T(8,128)S(1)}, u32[]{:S(2)}, u32[]{:S(2)}) collective-permute-start(f32[32,2048]{1,0:T(8,128)S(1)} %copy-done), channel_id=1, source_target_pairs={{0,4},{4,0},{1,5},{5,1},{2,6},{6,2},{3,7},{7,3},{8,12},{12,8},{9,1... | collective-permute-start | bytes 786440 | tf_op jit(solution)/shard_map/ppermute | solution.py:371
  38.7 14.2 %collective-permute-start.2 = (f32[32,2048]{1,0:T(8,128)S(1)}, f32[32,2048]{1,0:T(8,128)S(1)}, u32[]{:S(2)}, u32[]{:S(2)}) collective-permute-start(f32[32,2048]{1,0:T(8,128)S(1)} %copy-done), channel_id=1, source_target_pairs={{0,504},{8,16},{16,8},{24,32},{32,24},{40,48},{48,40},{56,64},{64,... | collective-permute-start | bytes 786440 | tf_op jit(solution)/shard_map/ppermute | solution.py:391
  52.9 1.9 collective-permute-start.1
  54.9 2.9 %collective-permute-start.4 = (f32[32,2048]{1,0:T(8,128)S(1)}, f32[32,2048]{1,0:T(8,128)S(1)}, u32[]{:S(2)}, u32[]{:S(2)}) collective-permute-start(f32[32,2048]{1,0:T(8,128)S(1)} %copy-done), channel_id=1, source_target_pairs={{0,508},{4,8},{8,4},{12,16},{16,12},{20,24},{24,20},{28,32},{32,28... | collective-permute-start | bytes 786440 | tf_op jit(solution)/shard_map/ppermute | solution.py:396
  57.8 3.5 %own.1 = (bf16[24,2,128,128]{3,2,1,0:T(8,128)(2,1)S(1)}, s32[51]{0:T(128)S(1)}) custom-call(s32[3]{0:T(128)S(1)} %pad_add_fusion.ids.refs_0_, s32[24]{0:T(128)} %refs_1_.1, s32[24]{0:T(128)} %refs_2_.1, s32[1]{0:T(128)S(6)} %copy.11.count.refs_3_, f32[24,128,128]{2,1,0:T(8,128)} %tiles.3), custom_call_target="tpu_custom_call" | custom-call | bytes 6291456 | tf_op jit(solution)/shard_map/own/pallas_call | solution.py:402
  62.1 7.7 %collective-permute-done.4.refs_8_ = f32[32,2048]{1,0:T(8,128)S(1)} collective-permute-done((f32[32,2048]{1,0:T(8,128)S(1)}, f32[32,2048]{1,0:T(8,128)S(1)}, u32[]{:S(2)}, u32[]{:S(2)}) %collective-permute-start.4) | collective-permute-done | bytes 262176 | tf_op jit(solution)/shard_map/ppermute | solution.py:396
  70.9 2.6 %collective-permute-start.5 = (f32[16,16,128]{2,1,0:T(8,128)S(1)}, f32[16,16,128]{2,1,0:T(8,128)S(1)}, u32[]{:S(2)}, u32[]{:S(2)}) collective-permute-start(f32[16,16,128]{2,1,0:T(8,128)S(1)} %get-tuple-element.14), channel_id=1, source_target_pairs={{0,4},{4,0},{1,5},{5,1},{2,6},{6,2},{3,7},{7,3},{8,12},{12,8},{9,1... | collective-permute-start | bytes 393224 | tf_op jit(solution)/shard_map/ppermute | solution.py:371
  73.5 4.6 %collective-permute-done.5 = f32[16,16,128]{2,1,0:T(8,128)S(1)} collective-permute-done((f32[16,16,128]{2,1,0:T(8,128)S(1)}, f32[16,16,128]{2,1,0:T(8,128)S(1)}, u32[]{:S(2)}, u32[]{:S(2)}) %collective-permute-start.5) | collective-permute-done | bytes 131104 | tf_op jit(solution)/shard_map/ppermute | solution.py:371
  78.2 1.9 collective-permute-start.7
  80.1 1.9 collective-permute-start.6
  82.0 1.9 partner.1.refs_1_
  86.2 4.3 %collective-permute-done.6.refs_2_ = f32[32,16,128]{2,1,0:T(8,128)S(1)} collective-permute-done((f32[32,16,128]{2,1,0:T(8,128)S(1)}, f32[32,16,128]{2,1,0:T(8,128)S(1)}, u32[]{:S(2)}, u32[]{:S(2)}) %collective-permute-start.6) | collective-permute-done | bytes 262176 | tf_op jit(solution)/shard_map/ppermute | solution.py:391
  91.8 1.9 collective-permute-start.11
  93.7 2.9 %collective-permute-start.10 = (f32[32,16,128]{2,1,0:T(8,128)S(1)}, f32[32,16,128]{2,1,0:T(8,128)S(1)}, u32[]{:S(2)}, u32[]{:S(2)}) collective-permute-start(f32[32,16,128]{2,1,0:T(8,128)S(1)} %shard_map.71.refs_2_.refs_5_), channel_id=1, source_target_pairs={{0,504},{8,16},{16,8},{24,32},{32,24},{40,48},{48,40},{56,64},{64,... | collective-permute-start | bytes 786440 | tf_op jit(solution)/shard_map/ppermute | solution.py:391
  98.9 5.2 %collective-permute-done.10.refs_2_ = f32[32,16,128]{2,1,0:T(8,128)S(1)} collective-permute-done((f32[32,16,128]{2,1,0:T(8,128)S(1)}, f32[32,16,128]{2,1,0:T(8,128)S(1)}, u32[]{:S(2)}, u32[]{:S(2)}) %collective-permute-start.10) | collective-permute-done | bytes 262176 | tf_op jit(solution)/shard_map/ppermute | solution.py:391
  105.4 1.9 collective-permute-start.13
  107.4 3.1 %collective-permute-start.12 = (f32[32,16,128]{2,1,0:T(8,128)S(1)}, f32[32,16,128]{2,1,0:T(8,128)S(1)}, u32[]{:S(2)}, u32[]{:S(2)}) collective-permute-start(f32[32,16,128]{2,1,0:T(8,128)S(1)} %shard_map.73.refs_2_), channel_id=1, source_target_pairs={{0,504},{8,16},{16,8},{24,32},{32,24},{40,48},{48,40},{56,64},{64,... | collective-permute-start | bytes 786440 | tf_op jit(solution)/shard_map/ppermute | solution.py:391
  112.5 5.2 %collective-permute-done.12.refs_2_ = f32[32,16,128]{2,1,0:T(8,128)S(1)} collective-permute-done((f32[32,16,128]{2,1,0:T(8,128)S(1)}, f32[32,16,128]{2,1,0:T(8,128)S(1)}, u32[]{:S(2)}, u32[]{:S(2)}) %collective-permute-start.12) | collective-permute-done | bytes 262176 | tf_op jit(solution)/shard_map/ppermute | solution.py:391
  119.1 14.9 %all_to_all.24.parts_ref = f32[8,4,16,128]{3,2,1,0:T(8,128)S(1)} all-to-all(f32[8,4,16,128]{3,2,1,0:T(8,128)S(1)} %bitcast.8), channel_id=1, replica_groups=mesh['q'=64,'xh'=2,'xl'=2,'core'=2] {'xh','xl','core'}, dimensions={0} | all-to-all | bytes 524288 | tf_op jit(solution)/shard_map/all_to_all | solution.py:375
  134.4 2.2 %collective-permute-start.14 = (f32[128,512]{1,0:T(8,128)S(1)}, f32[128,512]{1,0:T(8,128)S(1)}, u32[]{:S(2)}, u32[]{:S(2)}) collective-permute-start(f32[128,512]{1,0:T(8,128)S(1)} %get-tuple-element.17.refs_0_), channel_id=1, source_target_pairs={{0,2},{2,0},{1,3},{3,1},{4,6},{6,4},{5,7},{7,5},{8,10},{10,8},{9,1... | collective-permute-start | bytes 786440 | tf_op jit(solution)/shard_map/ppermute | solution.py:371
  136.6 6.5 %collective-permute-done.14.refs_1_ = f32[128,512]{1,0:T(8,128)S(1)} collective-permute-done((f32[128,512]{1,0:T(8,128)S(1)}, f32[128,512]{1,0:T(8,128)S(1)}, u32[]{:S(2)}, u32[]{:S(2)}) %collective-permute-start.14) | collective-permute-done | bytes 262176 | tf_op jit(solution)/shard_map/ppermute | solution.py:371
  143.2 3.8 %collective-permute-start.15 = (f32[256,512]{1,0:T(8,128)S(1)}, f32[256,512]{1,0:T(8,128)S(1)}, u32[]{:S(2)}, u32[]{:S(2)}) collective-permute-start(f32[256,512]{1,0:T(8,128)S(1)} %pad_maximum_fusion), channel_id=1, source_target_pairs={{0,1},{1,0},{2,3},{3,2},{4,5},{5,4},{6,7},{7,6},{8,9},{9,8},{10,11... | collective-permute-start | bytes 1572872 | tf_op jit(solution)/shard_map/ppermute | solution.py:371
  147.0 16.5 %all_to_all.25 = f32[64,2,128]{2,1,0:T(2,128)S(1)} all-to-all(f32[64,2,128]{2,1,0:T(2,128)S(1)} %bitcast.10), channel_id=1, replica_groups=mesh['q'=64,'xh'=2,'xl'=2,'core'=2] {'q'}, dimensions={0} | all-to-all | bytes 131072 | tf_op jit(solution)/shard_map/all_to_all | solution.py:375
  163.6 8.4 %all_to_all.26 = f32[8,2,128]{2,1,0:T(2,128)S(1)} all-to-all(f32[8,2,128]{2,1,0:T(2,128)S(1)} %broadcast_in_dim.24), channel_id=1, replica_groups=mesh['q'=64,'xh'=2,'xl'=2,'core'=2] {'xh','xl','core'}, dimensions={0} | all-to-all | bytes 16384 | tf_op jit(solution)/shard_map/all_to_all | solution.py:375
  172.0 15.0 %all_to_all.27 = f32[64,2,128]{2,1,0:T(2,128)S(1)} all-to-all(f32[64,2,128]{2,1,0:T(2,128)S(1)} %broadcast_in_dim.25), channel_id=1, replica_groups=mesh['q'=64,'xh'=2,'xl'=2,'core'=2] {'q'}, dimensions={0} | all-to-all | bytes 131072 | tf_op jit(solution)/shard_map/all_to_all | solution.py:375
  187.0 8.3 %shard_map.77 = (f32[128,128]{1,0:T(8,128)}, f32[32,2048]{1,0:T(8,128)}) custom-call(s32[1]{0:T(128)} %bitcast.place_ref, f32[128,128]{1,0:T(8,128)S(1)} %bitcast.9, f32[128,512]{1,0:T(8,128)S(1)} %get-tuple-element.17.refs_0_, f32[128,512]{1,0:T(8,128)S(1)} %collective-permute-done.14.refs_1_, f32[256,512]{1,0:T(8,128)S(1)} %collective-permute-done.15.refs_2_), custom_call_target="tpu_custom_call" | custom-call | flops 100663296 | bytes 1048576 | tf_op jit(solution)/shard_map/pallas_call | solution.py:43
  (33 shorter events, 13.1 us)
Async XLA Ops:
  1.4 32.5 %copy-start = (f32[32,2048]{1,0:T(8,128)S(1)}, f32[32,2048]{1,0:T(8,128)}, u32[]{:S(2)}) copy-start(f32[32,2048]{1,0:T(8,128)} %refs_4_.1) | copy-start | bytes 786436
  3.1 66.7 %copy-start.1 = (s32[24]{0:T(128)S(1)}, s32[24]{0:T(128)}, u32[]{:S(2)}) copy-start(s32[24]{0:T(128)} %refs_1_.1) | copy-start | bytes 292
  3.1 66.7 %copy-start.2 = (s32[24]{0:T(128)S(1)}, s32[24]{0:T(128)}, u32[]{:S(2)}) copy-start(s32[24]{0:T(128)} %refs_2_.1) | copy-start | bytes 292
  3.1 11.8 %collective-permute-start = (f32[7,128,128]{2,1,0:T(8,128)S(1)}, f32[7,128,128]{2,1,0:T(8,128)S(1)}, u32[]{:S(2)}, u32[]{:S(2)}) collective-permute-start(f32[7,128,128]{2,1,0:T(8,128)S(1)} %cut.1), channel_id=1, source_target_pairs={{0,6},{2,4},{4,2},{6,0},{1,7},{3,5},{5,3},{7,1},{8,14},{10,12},{12... | collective-permute-start | bytes 1376264 | tf_op jit(solution)/shard_map/ppermute | solution.py:426
  14.9 12.5 %collective-permute-start.8 = (f32[7,128,128]{2,1,0:T(8,128)S(1)}, f32[7,128,128]{2,1,0:T(8,128)S(1)}, u32[]{:S(2)}, u32[]{:S(2)}) collective-permute-start(f32[7,128,128]{2,1,0:T(8,128)S(1)} %collective-permute-done.first), channel_id=1, source_target_pairs={{0,2},{2,0},{1,3},{3,1},{4,6},{6,4},{5,7},{7,5},{8,10},{10,8},{9,1... | collective-permute-start | bytes 1376264 | tf_op jit(solution)/shard_map/ppermute | solution.py:371
  27.4 56.5 %collective-permute-start.9 = (f32[14,128,128]{2,1,0:T(8,128)S(1)}, f32[14,128,128]{2,1,0:T(8,128)S(1)}, u32[]{:S(2)}, u32[]{:S(2)}) collective-permute-start(f32[14,128,128]{2,1,0:T(8,128)S(1)} %constant_dynamic-update-slice_fusion.2.pair), channel_id=1, source_target_pairs={{0,1},{1,0},{2,3},{3,2},{4,5},{5,4},{6,7},{7,6},{8,9},{9,8},{10,11... | collective-permute-start | bytes 2752520 | tf_op jit(solution)/shard_map/ppermute | solution.py:371
  33.9 27.4 %collective-permute-start.3 = (f32[32,2048]{1,0:T(8,128)S(1)}, f32[32,2048]{1,0:T(8,128)S(1)}, u32[]{:S(2)}, u32[]{:S(2)}) collective-permute-start(f32[32,2048]{1,0:T(8,128)S(1)} %copy-done), channel_id=1, source_target_pairs={{0,4},{4,0},{1,5},{5,1},{2,6},{6,2},{3,7},{7,3},{8,12},{12,8},{9,1... | collective-permute-start | bytes 786440 | tf_op jit(solution)/shard_map/ppermute | solution.py:371
  38.7 22.6 %collective-permute-start.2 = (f32[32,2048]{1,0:T(8,128)S(1)}, f32[32,2048]{1,0:T(8,128)S(1)}, u32[]{:S(2)}, u32[]{:S(2)}) collective-permute-start(f32[32,2048]{1,0:T(8,128)S(1)} %copy-done), channel_id=1, source_target_pairs={{0,504},{8,16},{16,8},{24,32},{32,24},{40,48},{48,40},{56,64},{64,... | collective-permute-start | bytes 786440 | tf_op jit(solution)/shard_map/ppermute | solution.py:391
  52.9 9.2 %collective-permute-start.1 = (f32[32,2048]{1,0:T(8,128)S(1)}, f32[32,2048]{1,0:T(8,128)S(1)}, u32[]{:S(2)}, u32[]{:S(2)}) collective-permute-start(f32[32,2048]{1,0:T(8,128)S(1)} %copy-done), channel_id=1, source_target_pairs={{0,8},{8,0},{16,24},{24,16},{32,40},{40,32},{48,56},{56,48},{64,72... | collective-permute-start | bytes 786440 | tf_op jit(solution)/shard_map/ppermute | solution.py:390
  54.9 14.9 %collective-permute-start.4 = (f32[32,2048]{1,0:T(8,128)S(1)}, f32[32,2048]{1,0:T(8,128)S(1)}, u32[]{:S(2)}, u32[]{:S(2)}) collective-permute-start(f32[32,2048]{1,0:T(8,128)S(1)} %copy-done), channel_id=1, source_target_pairs={{0,508},{4,8},{8,4},{12,16},{16,12},{20,24},{24,20},{28,32},{32,28... | collective-permute-start | bytes 786440 | tf_op jit(solution)/shard_map/ppermute | solution.py:396
  70.9 7.2 %collective-permute-start.5 = (f32[16,16,128]{2,1,0:T(8,128)S(1)}, f32[16,16,128]{2,1,0:T(8,128)S(1)}, u32[]{:S(2)}, u32[]{:S(2)}) collective-permute-start(f32[16,16,128]{2,1,0:T(8,128)S(1)} %get-tuple-element.14), channel_id=1, source_target_pairs={{0,4},{4,0},{1,5},{5,1},{2,6},{6,2},{3,7},{7,3},{8,12},{12,8},{9,1... | collective-permute-start | bytes 393224 | tf_op jit(solution)/shard_map/ppermute | solution.py:371
  78.2 8.1 %collective-permute-start.7 = (f32[32,16,128]{2,1,0:T(8,128)S(1)}, f32[32,16,128]{2,1,0:T(8,128)S(1)}, u32[]{:S(2)}, u32[]{:S(2)}) collective-permute-start(f32[32,16,128]{2,1,0:T(8,128)S(1)} %constant_dynamic-update-slice_fusion.refs_2_.refs_5_), channel_id=1, source_target_pairs={{0,8},{8,0},{16,24},{24,16},{32,40},{40,32},{48,56},{56,48},{64,72... | collective-permute-start | bytes 786440 | tf_op jit(solution)/shard_map/ppermute | solution.py:390
  80.1 10.4 %collective-permute-start.6 = (f32[32,16,128]{2,1,0:T(8,128)S(1)}, f32[32,16,128]{2,1,0:T(8,128)S(1)}, u32[]{:S(2)}, u32[]{:S(2)}) collective-permute-start(f32[32,16,128]{2,1,0:T(8,128)S(1)} %constant_dynamic-update-slice_fusion.refs_2_.refs_5_), channel_id=1, source_target_pairs={{0,504},{8,16},{16,8},{24,32},{32,24},{40,48},{48,40},{56,64},{64,... | collective-permute-start | bytes 786440 | tf_op jit(solution)/shard_map/ppermute | solution.py:391
  91.8 7.1 %collective-permute-start.11 = (f32[32,16,128]{2,1,0:T(8,128)S(1)}, f32[32,16,128]{2,1,0:T(8,128)S(1)}, u32[]{:S(2)}, u32[]{:S(2)}) collective-permute-start(f32[32,16,128]{2,1,0:T(8,128)S(1)} %shard_map.71.refs_2_.refs_5_), channel_id=1, source_target_pairs={{0,8},{8,0},{16,24},{24,16},{32,40},{40,32},{48,56},{56,48},{64,72... | collective-permute-start | bytes 786440 | tf_op jit(solution)/shard_map/ppermute | solution.py:390
  93.7 10.4 %collective-permute-start.10 = (f32[32,16,128]{2,1,0:T(8,128)S(1)}, f32[32,16,128]{2,1,0:T(8,128)S(1)}, u32[]{:S(2)}, u32[]{:S(2)}) collective-permute-start(f32[32,16,128]{2,1,0:T(8,128)S(1)} %shard_map.71.refs_2_.refs_5_), channel_id=1, source_target_pairs={{0,504},{8,16},{16,8},{24,32},{32,24},{40,48},{48,40},{56,64},{64,... | collective-permute-start | bytes 786440 | tf_op jit(solution)/shard_map/ppermute | solution.py:391
  105.4 7.1 %collective-permute-start.13 = (f32[32,16,128]{2,1,0:T(8,128)S(1)}, f32[32,16,128]{2,1,0:T(8,128)S(1)}, u32[]{:S(2)}, u32[]{:S(2)}) collective-permute-start(f32[32,16,128]{2,1,0:T(8,128)S(1)} %shard_map.73.refs_2_), channel_id=1, source_target_pairs={{0,8},{8,0},{16,24},{24,16},{32,40},{40,32},{48,56},{56,48},{64,72... | collective-permute-start | bytes 786440 | tf_op jit(solution)/shard_map/ppermute | solution.py:390
  107.4 10.4 %collective-permute-start.12 = (f32[32,16,128]{2,1,0:T(8,128)S(1)}, f32[32,16,128]{2,1,0:T(8,128)S(1)}, u32[]{:S(2)}, u32[]{:S(2)}) collective-permute-start(f32[32,16,128]{2,1,0:T(8,128)S(1)} %shard_map.73.refs_2_), channel_id=1, source_target_pairs={{0,504},{8,16},{16,8},{24,32},{32,24},{40,48},{48,40},{56,64},{64,... | collective-permute-start | bytes 786440 | tf_op jit(solution)/shard_map/ppermute | solution.py:391
  134.4 8.7 %collective-permute-start.14 = (f32[128,512]{1,0:T(8,128)S(1)}, f32[128,512]{1,0:T(8,128)S(1)}, u32[]{:S(2)}, u32[]{:S(2)}) collective-permute-start(f32[128,512]{1,0:T(8,128)S(1)} %get-tuple-element.17.refs_0_), channel_id=1, source_target_pairs={{0,2},{2,0},{1,3},{3,1},{4,6},{6,4},{5,7},{7,5},{8,10},{10,8},{9,1... | collective-permute-start | bytes 786440 | tf_op jit(solution)/shard_map/ppermute | solution.py:371
  143.2 43.9 %collective-permute-start.15 = (f32[256,512]{1,0:T(8,128)S(1)}, f32[256,512]{1,0:T(8,128)S(1)}, u32[]{:S(2)}, u32[]{:S(2)}) collective-permute-start(f32[256,512]{1,0:T(8,128)S(1)} %pad_maximum_fusion), channel_id=1, source_target_pairs={{0,1},{1,0},{2,3},{3,2},{4,5},{5,4},{6,7},{7,6},{8,9},{9,8},{10,11... | collective-permute-start | bytes 1572872 | tf_op jit(solution)/shard_map/ppermute | solution.py:371
